TPU v7x, 256 devices: a whole 4x4x8 slice. The times are simulated.
256 devices in a mesh: tm: 128 (over y, x, z), tok: 2 (over core).
Axes of the slice: x: 4, y: 4, z: 8, core: 2. Of those that a mesh axis runs over, the one named last changes fastest.
Arguments:
- patches: bfloat16 [128, 12, 12, 12, 512], P('tm', 'tok'), may hold values from -6 to 6
- patch_weight: bfloat16 [512, 512], replicated, may hold values from -0.25 to 0.25
- conv_taps: bfloat16 [27, 512], replicated, may hold values from -2 to 2
- gain_space: bfloat16 [512], replicated, may hold values from 0.099609375 to 1.8984375
- qkv_space: bfloat16 [512, 1536], replicated, may hold values from -0.25 to 0.25
- out_space: bfloat16 [512, 512], replicated, may hold values from -0.25 to 0.25
- gain_time: bfloat16 [512], replicated, may hold values from 0.099609375 to 1.8984375
- qkv_time: bfloat16 [512, 1536], replicated, may hold values from -0.25 to 0.25
- out_time: bfloat16 [512, 512], replicated, may hold values from -0.25 to 0.25
Outputs:
- block_out: bfloat16 [128, 12, 12, 12, 512], P('tm', 'tok')
All inputs are finite; a program needn't handle non-finite values.
Results may differ from a plain program's by a relative error of at most 0.018.
Values may be sent and summed in bfloat16 or wider, within the bound.
A program may use at most 128 MiB of HBM per device.

v0:
```python
import jax
import jax.numpy as jnp
from jax import lax
from jax.sharding import PartitionSpec as P
from jax.experimental import pallas as pl
from jax.experimental.pallas import tpu as pltpu
import functools

D = 512
H = 8
WIN = 4


def extended(block, sides, width):
    for axis, dim in sides:
        count = lax.axis_size(axis)
        forward = [(i, i + 1) for i in range(count - 1)]
        backward = [(target, source) for source, target in forward]
        low = lax.ppermute(
            lax.slice_in_dim(block, block.shape[dim] - width, None, axis=dim), axis, forward
        )
        high = lax.ppermute(lax.slice_in_dim(block, 0, width, axis=dim), axis, backward)
        block = jnp.concatenate([low, block, high], axis=dim)
    return block


def from_behind(value, axis, steps):
    count = lax.axis_size(axis)
    leading, last = (max(0, -steps), min(count, count - steps))
    return lax.ppermute(value, axis, [(source, source + steps) for source in range(leading, last)])


def rms_scale(values, gain):
    mean_sq = jnp.mean(values * values, axis=-1, keepdims=True)
    return values * lax.rsqrt(mean_sq + 1e-06) * gain.astype(jnp.float32)


def split_heads(block, count, head_size):
    return block.reshape(block.shape[0], count, head_size).transpose(1, 0, 2)


def attend(query, keys, values):
    rows, cols = query.shape
    head_size = D // H
    count = cols // head_size
    scale = head_size ** (-0.5)

    def one_head(parts):
        q_one, k_one, v_one = parts
        scores = jnp.dot(q_one, k_one.T, preferred_element_type=jnp.float32) * scale
        expo = jnp.exp(scores)
        mixed = jnp.dot(expo.astype(jnp.bfloat16), v_one, preferred_element_type=jnp.float32)
        return (mixed / jnp.sum(expo, axis=-1, keepdims=True)).astype(jnp.bfloat16)

    parts = (
        split_heads(query, count, head_size),
        split_heads(keys, count, head_size),
        split_heads(values, count, head_size),
    )
    result = lax.map(one_head, parts)
    return result.transpose(1, 0, 2).reshape(rows, cols)


def pair_attention_kernel(q_ref, k_ref, v_ref, o_ref):
    head_size = D // H
    scale = head_size ** (-0.5)
    q = q_ref[...]
    k = k_ref[...]
    v = v_ref[...]
    lane = lax.broadcasted_iota(jnp.int32, (1, q.shape[1]), 1)
    first = lane < head_size
    outs = []
    for mask in (first, jnp.logical_not(first)):
        q_one = jnp.where(mask, q, jnp.zeros_like(q))
        scores = lax.dot_general(
            q_one, k, (((1,), (1,)), ((), ())), preferred_element_type=jnp.float32
        ) * scale
        expo = jnp.exp(scores)
        total = jnp.sum(expo, axis=-1, keepdims=True)
        mixed = jnp.dot(expo.astype(jnp.bfloat16), v, preferred_element_type=jnp.float32)
        outs.append(mixed / total)
    o_ref[...] = jnp.where(first, outs[0], outs[1]).astype(o_ref.dtype)


def spatial_attention(query, keys, values, block_rows=288):
    rows, width = query.shape
    count = keys.shape[0]
    lanes = 2 * (D // H)
    grid = (width // lanes, rows // block_rows)
    return pl.pallas_call(
        pair_attention_kernel,
        out_shape=jax.ShapeDtypeStruct((rows, width), jnp.bfloat16),
        grid=grid,
        in_specs=[
            pl.BlockSpec((block_rows, lanes), lambda h, r: (r, h)),
            pl.BlockSpec((count, lanes), lambda h, r: (0, h)),
            pl.BlockSpec((count, lanes), lambda h, r: (0, h)),
        ],
        out_specs=pl.BlockSpec((block_rows, lanes), lambda h, r: (r, h)),
    )(query, keys, values)


def block_kernel(
    chunks, proj_ref, other_ref, stream_ref, wo_ref, gain_ref, wt_ref,
    out_ref, stream2_ref, own, query2, hist, mixed, total, sum_ref, send_sem, recv_sem,
):
    me = lax.axis_index("tm")
    count = lax.axis_size("tm")
    core = lax.axis_index("tok")
    has_left = me > 0
    has_right = me < count - 1
    rows_all, width = own.shape
    rows = rows_all // chunks
    head_size = width // H
    scale = head_size ** (-0.5)
    lanes = 2 * head_size
    mesh_ids = pl.DeviceIdType.MESH

    @pl.when(jnp.logical_not(has_left))
    def _():
        hist[...] = jnp.zeros_like(hist)

    barrier = pltpu.get_barrier_semaphore()

    @pl.when(has_left)
    def _():
        pl.semaphore_signal(barrier, inc=1, device_id=(me - 1, core), device_id_type=mesh_ids)

    @pl.when(has_right)
    def _():
        pl.semaphore_signal(barrier, inc=1, device_id=(me + 1, core), device_id_type=mesh_ids)

    @pl.when(jnp.logical_and(has_left, has_right))
    def _():
        pl.semaphore_wait(barrier, 2)

    @pl.when(jnp.logical_xor(has_left, has_right))
    def _():
        pl.semaphore_wait(barrier, 1)

    def span_of(piece):
        return pl.ds(pl.multiple_of(piece * rows, 8), rows)

    def copy_of(hop, piece):
        span = span_of(piece)
        source = own.at[span] if hop == 0 else hist.at[hop - 1, span]
        return pltpu.make_async_remote_copy(
            src_ref=source,
            dst_ref=hist.at[hop, span],
            send_sem=send_sem.at[hop, piece],
            recv_sem=recv_sem.at[hop, piece],
            device_id=(me + 1, core),
            device_id_type=mesh_ids,
        )

    lane = lax.broadcasted_iota(jnp.int32, (1, lanes), 1)
    first_half = lane < head_size
    heads = lax.broadcasted_iota(jnp.int32, (width, width), 0) // head_size
    same_head = heads == lax.broadcasted_iota(jnp.int32, (width, width), 1) // head_size
    sum_ref[...] = same_head.astype(jnp.bfloat16)

    def space_step(piece, carry):
        span = span_of(piece)
        pieces = []
        for pair in range(width // lanes):
            cols = slice(pair * lanes, (pair + 1) * lanes)
            q = proj_ref[span, cols]
            key_cols = slice(width + pair * lanes, width + (pair + 1) * lanes)
            value_cols = slice(2 * width + pair * lanes, 2 * width + (pair + 1) * lanes)
            sources = (
                (proj_ref[:, key_cols], proj_ref[:, value_cols]),
                (other_ref[:, cols], other_ref[:, key_cols]),
            )
            outs = []
            for mask in (first_half, jnp.logical_not(first_half)):
                q_one = jnp.where(mask, q, jnp.zeros_like(q))
                rowsum = None
                mixed_one = None
                for k, v in sources:
                    scores = lax.dot_general(
                        q_one, k, (((1,), (1,)), ((), ())), preferred_element_type=jnp.float32
                    ) * scale
                    expo = jnp.exp(scores)
                    part_sum = jnp.sum(expo, axis=-1, keepdims=True)
                    part = jnp.dot(
                        expo.astype(jnp.bfloat16), v, preferred_element_type=jnp.float32
                    )
                    rowsum = part_sum if rowsum is None else rowsum + part_sum
                    mixed_one = part if mixed_one is None else mixed_one + part
                outs.append(mixed_one / rowsum)
            pieces.append(jnp.where(first_half, outs[0], outs[1]).astype(jnp.bfloat16))
        spatial = jnp.concatenate(pieces, axis=1)
        stream2 = (
            stream_ref[span, :].astype(jnp.float32)
            + jnp.dot(spatial, wo_ref[...], preferred_element_type=jnp.float32)
        ).astype(jnp.bfloat16)
        stream2_ref[span, :] = stream2
        values = stream2.astype(jnp.float32)
        mean_sq = jnp.mean(values * values, axis=-1, keepdims=True)
        normed2 = (values * lax.rsqrt(mean_sq + 1e-06) * gain_ref[...]).astype(jnp.bfloat16)
        own[span, :] = normed2
        query2[span, :] = jnp.dot(
            normed2, wt_ref[:, :width], preferred_element_type=jnp.float32
        ).astype(jnp.bfloat16)

        @pl.when(jnp.logical_and(has_right, piece >= 1))
        def _():
            copy_of(0, piece - 1).start()

        return carry

    lax.fori_loop(0, chunks, space_step, 0)

    def add_term(block, span, valid, first):
        kv = jnp.dot(block, wt_ref[:, width:], preferred_element_type=jnp.float32).astype(jnp.bfloat16)
        keys2 = kv[:, :width].astype(jnp.float32)
        values2 = kv[:, width:].astype(jnp.float32)
        prod = query2[span, :].astype(jnp.float32) * keys2
        high = prod.astype(jnp.bfloat16)
        low = (prod - high.astype(jnp.float32)).astype(jnp.bfloat16)
        summer = sum_ref[...]
        scores = (
            jnp.dot(high, summer, preferred_element_type=jnp.float32)
            + jnp.dot(low, summer, preferred_element_type=jnp.float32)
        ) * scale
        expo = jnp.where(valid, jnp.exp(scores), 0.0)
        part = expo.astype(jnp.bfloat16).astype(jnp.float32) * values2
        if first:
            mixed[span, :] = part
            total[span, :] = expo
        else:
            mixed[span, :] += part
            total[span, :] += expo

    def own_step(piece, carry):
        span = span_of(piece)
        add_term(own[span, :], span, True, True)
        return carry

    lax.fori_loop(0, chunks, own_step, 0)

    @pl.when(has_right)
    def _():
        copy_of(0, chunks - 1).start()

    for hop in range(WIN):
        def hop_step(piece, carry, hop=hop):
            span = span_of(piece)

            @pl.when(has_left)
            def _():
                copy_of(hop, piece).wait_recv()

            if hop + 1 < WIN:
                @pl.when(has_right)
                def _():
                    copy_of(hop + 1, piece).start()

            add_term(hist[hop, span, :], span, me - (hop + 1) >= 0, False)
            return carry

        lax.fori_loop(0, chunks, hop_step, 0)

    @pl.when(has_right)
    def _():
        for hop in range(WIN):
            for piece in range(chunks):
                copy_of(hop, piece).wait_send()

    out_ref[...] = (mixed[...] / total[...]).astype(out_ref.dtype)


def block_tail(proj, other, stream, out_space, gain_time, qkv_time, chunks=6):
    rows, width = stream.shape
    gain = gain_time.astype(jnp.float32).reshape(1, width)
    vmem = pl.BlockSpec(memory_space=pltpu.VMEM)
    plane = jax.ShapeDtypeStruct((rows, width), jnp.bfloat16)
    return pl.pallas_call(
        functools.partial(block_kernel, chunks),
        out_shape=(plane, plane),
        in_specs=[vmem] * 6,
        out_specs=(vmem, vmem),
        scratch_shapes=[
            pltpu.VMEM((rows, width), jnp.bfloat16),
            pltpu.VMEM((rows, width), jnp.bfloat16),
            pltpu.VMEM((WIN, rows, width), jnp.bfloat16),
            pltpu.VMEM((rows, width), jnp.float32),
            pltpu.VMEM((rows, width), jnp.float32),
            pltpu.VMEM((width, width), jnp.bfloat16),
            pltpu.SemaphoreType.DMA((WIN, chunks)),
            pltpu.SemaphoreType.DMA((WIN, chunks)),
        ],
        compiler_params=pltpu.CompilerParams(
            collective_id=0, has_side_effects=True, vmem_limit_bytes=56 * 1024 * 1024
        ),
    )(proj, other, stream, out_space, gain, qkv_time)


def local(
    patches,
    patch_weight,
    conv_taps,
    gain_space,
    qkv_space,
    out_space,
    gain_time,
    qkv_time,
    out_time,
):
    frames, zdev, grid, _, patch = patches.shape
    width = patch_weight.shape[1]
    tokens = zdev * grid * grid
    embed = jnp.dot(
        patches.reshape(-1, patch), patch_weight, preferred_element_type=jnp.float32
    ).astype(jnp.bfloat16)
    embed = embed.reshape(frames, zdev, grid, grid, width)
    padded = extended(embed, (("tok", 1),), 1)
    padded = jnp.pad(padded, ((0, 0), (0, 0), (1, 1), (1, 1), (0, 0)))
    conv = jnp.zeros((frames, zdev, grid, grid, width), jnp.float32)
    for dz in range(3):
        for dy in range(3):
            for dx in range(3):
                tap = conv_taps[9 * dz + 3 * dy + dx].astype(jnp.float32)
                conv = conv + tap * padded[
                    :, dz : dz + zdev, dy : dy + grid, dx : dx + grid
                ].astype(jnp.float32)
    stream = (embed.astype(jnp.float32) + conv).astype(jnp.bfloat16).reshape(frames, tokens, width)
    normed = rms_scale(stream.astype(jnp.float32), gain_space).astype(jnp.bfloat16)
    proj = jnp.dot(normed.reshape(-1, width), qkv_space, preferred_element_type=jnp.float32).astype(
        jnp.bfloat16
    )
    proj = proj.reshape(frames, tokens, 3 * width)
    own_kv = proj[0, :, width:]
    count = lax.axis_size("tok")
    other_kv = lax.ppermute(own_kv, "tok", [(i, (i + 1) % count) for i in range(count)])
    temporal, stream2 = block_tail(
        proj[0], other_kv, stream.reshape(-1, width), out_space, gain_time, qkv_time
    )
    time_proj = jnp.dot(
        temporal.reshape(-1, width), out_time, preferred_element_type=jnp.float32
    ).reshape(frames, tokens, width)
    output = (stream2.astype(jnp.float32) + time_proj).astype(jnp.bfloat16)
    return output.reshape(frames, zdev, grid, grid, width)


def solution(mesh):
    placed = (P("tm", "tok", None, None, None), P(), P(), P(), P(), P(), P(), P(), P())
    return jax.shard_map(
        local,
        mesh=mesh,
        in_specs=placed,
        out_specs=P("tm", "tok", None, None, None),
        check_vma=False,
    )
```

profile of v0, /device:TPU:24, one launch (start us, length us, event | category | flops | bytes accessed | tf_op | source)
XLA Modules:
  0.0 134.0 jit_solution(14982529904837079628)
XLA Ops:
  0.0 0.0 copy-start
  0.0 1.5 %reshape.335 = bf16[864,512]{1,0:T(8,128)(2,1)S(1)} reshape(bf16[1,6,12,12,512]{4,3,2,1,0:T(8,128)(2,1)} %param.9) | data formatting | bytes 1769472 | tf_op jit(solution)/shard_map/reshape | solution.py:314
  1.5 0.0 copy-start.4
  1.5 0.0 copy-start.5
  1.5 2.6 %convolution_convert_fusion.1 = bf16[864,512]{1,0:T(8,128)(2,1)} fusion(bf16[864,512]{1,0:T(8,128)(2,1)S(1)} %reshape.335, bf16[512,512]{1,0:T(8,128)(2,1)} %param.10), kind=kOutput, calls=%fused_computation.34 | convolution fusion | flops 453427200 | bytes 2293760 | tf_op jit(solution)/shard_map/dot_general | solution.py:313
  4.1 1.3 reshape.336
  5.4 1.8 %collective-permute-start = (bf16[1,1,12,12,512]{4,3,2,1,0:T(8,128)(2,1)S(1)}, bf16[1,1,12,12,512]{4,3,2,1,0:T(8,128)(2,1)S(1)}, u32[]{:S(2)}, u32[]{:S(2)}) collective-permute-start(bf16[1,1,12,12,512]{4,3,2,1,0:T(8,128)(2,1)S(1)} %get-tuple-element.11), channel_id=1, source_target_pairs={{0,1},{2,3},{4,5},{6,7},{8,9},{10,11},{12,13},{14,15},{16,17},{18,... | collective-permute-start | bytes 442376 | tf_op jit(solution)/shard_map/ppermute | solution.py:19
  7.2 1.3 collective-permute-start.1
  8.5 0.0 copy-done.4
  8.5 0.0 copy-done.5
  8.6 0.0 collective-permute-done
  8.6 1.9 %collective-permute-done.1 = bf16[1,1,12,12,512]{4,3,2,1,0:T(8,128)(2,1)S(1)} collective-permute-done((bf16[1,1,12,12,512]{4,3,2,1,0:T(8,128)(2,1)S(1)}, bf16[1,1,12,12,512]{4,3,2,1,0:T(8,128)(2,1)S(1)}, u32[]{:S(2)}, u32[]{:S(2)}) %collective-permute-start.1) | collective-permute-done | bytes 147488 | tf_op jit(solution)/shard_map/ppermute | solution.py:22
  10.5 0.9 select_maximum_fusion
  11.4 9.9 %multiply_reduce_fusion = (f32[6,12,12]{2,1,0:T(8,128)S(1)}, bf16[1,6,12,12,512]{4,3,2,1,0:T(8,128)(2,1)}) fusion(bf16[1,8,14,14,512]{4,3,2,1,0:T(8,128)(2,1)S(1)} %select_maximum_fusion, f32[512]{0:T(512)S(1)} %bitcast.62, f32[512]{0:T(512)S(1)} %bitcast.63, f32[512]{0:T(512)S(1)} %bitcast.38, f32[512]{0:T(512)S(1)} %bitcast.39, ...), kind=kLoop, calls=%fused_computation.24 | loop fusion | flops 38485152 | bytes 23356800 | tf_op jit(solution)/shard_map/reduce_sum | solution.py:34
  21.3 1.4 %reshape.337.stream_ref = bf16[864,512]{1,0:T(8,128)(2,1)S(1)} reshape(bf16[1,6,12,12,512]{4,3,2,1,0:T(8,128)(2,1)} %get-tuple-element.10) | data formatting | bytes 1769472 | tf_op jit(solution)/shard_map/reshape | solution.py:327
  22.7 0.0 copy-start.2
  22.7 0.1 rsqrt.12
  22.8 0.0 copy-done
  22.8 1.6 %convolution_convert_fusion.proj_ref = bf16[864,1536]{1,0:T(8,128)(2,1)S(1)} fusion(bf16[512,1536]{1,0:T(8,128)(2,1)S(1)} %copy-done, bf16[864,512]{1,0:T(8,128)(2,1)S(1)} %reshape.337.stream_ref, f32[512]{0:T(512)S(1)} %convert_element_type.486, f32[864]{0:T(1024)S(1)} %rsqrt.12), kind=kOutput, calls=%fused_computation.7 | convolution fusion | flops 1362051072 | bytes 5117312 | tf_op jit(solution)/shard_map/dot_general | solution.py:329
  24.4 0.0 copy-done.2
  24.5 0.0 copy-start.1
  24.5 0.0 copy-start.6
  24.5 0.3 slice_bitcast_fusion
  24.7 0.2 collective-permute-start.2
  25.0 0.2 copy-done.6
  25.2 0.7 reshape.369
  25.9 2.6 %collective-permute-done.2.other_ref = bf16[864,1024]{1,0:T(8,128)(2,1)S(1)} collective-permute-done((bf16[864,1024]{1,0:T(8,128)(2,1)S(1)}, bf16[864,1024]{1,0:T(8,128)(2,1)S(1)}, u32[]{:S(2)}, u32[]{:S(2)}) %collective-permute-start.2) | collective-permute-done | bytes 1769504 | tf_op jit(solution)/shard_map/ppermute | solution.py:335
  28.5 0.0 copy-start.3
  28.5 0.0 copy-done.1
  28.5 1.2 copy-done.3
  29.7 0.0 copy-start.7
  29.7 101.0 %shard_map.91 = (bf16[864,512]{1,0:T(8,128)(2,1)}, bf16[864,512]{1,0:T(8,128)(2,1)}) custom-call(bf16[864,1536]{1,0:T(8,128)(2,1)} %copy-done.1, bf16[864,1024]{1,0:T(8,128)(2,1)} %copy-done.3, bf16[864,512]{1,0:T(8,128)(2,1)} %copy-done.2, bf16[512,512]{1,0:T(8,128)(2,1)} %wo_ref.1, f32[1,512]{1,0:T(1,128)} %bitcast.64, bf16[512,1536]{1,0:T(8,128)(2,1)} %wt_ref.1), custom_call_target="tpu_custom_call" | custom-call | tf_op jit(solution)/shard_map/pallas_call | solution.py:278
  130.7 0.0 copy-done.7
  130.7 2.1 %add_convert_fusion = bf16[864,512]{1,0:T(8,128)(2,1)S(1)} fusion(bf16[864,512]{1,0:T(8,128)(2,1)} %get-tuple-element.7, bf16[864,512]{1,0:T(8,128)(2,1)} %get-tuple-element.8, bf16[512,512]{1,0:T(8,128)(2,1)S(1)} %copy-done.7), kind=kOutput, calls=%fused_computation.32 | convolution fusion | flops 454311936 | bytes 3178496 | tf_op jit(solution)/shard_map/dot_general | solution.py:339
  132.8 1.2 reshape.341
  (5 shorter events, 0.1 us)
Async XLA Ops:
  0.0 22.8 %copy-start = (bf16[512,1536]{1,0:T(8,128)(2,1)S(1)}, bf16[512,1536]{1,0:T(8,128)(2,1)}, u32[]{:S(2)}) copy-start(bf16[512,1536]{1,0:T(8,128)(2,1)} %param.13) | copy-start | bytes 4718596
  1.5 7.0 %copy-start.4 = (bf16[27,512]{1,0:T(8,128)(2,1)S(1)}, bf16[27,512]{1,0:T(8,128)(2,1)}, u32[]{:S(2)}) copy-start(bf16[27,512]{1,0:T(8,128)(2,1)} %param.11) | copy-start | bytes 82948
  1.5 7.0 %copy-start.5 = (bf16[512]{0:T(512)(128)(2,1)S(1)}, bf16[512]{0:T(512)(128)(2,1)}, u32[]{:S(2)}) copy-start(bf16[512]{0:T(512)(128)(2,1)} %param.12) | copy-start | bytes 3076
  5.4 3.2 %collective-permute-start = (bf16[1,1,12,12,512]{4,3,2,1,0:T(8,128)(2,1)S(1)}, bf16[1,1,12,12,512]{4,3,2,1,0:T(8,128)(2,1)S(1)}, u32[]{:S(2)}, u32[]{:S(2)}) collective-permute-start(bf16[1,1,12,12,512]{4,3,2,1,0:T(8,128)(2,1)S(1)} %get-tuple-element.11), channel_id=1, source_target_pairs={{0,1},{2,3},{4,5},{6,7},{8,9},{10,11},{12,13},{14,15},{16,17},{18,... | collective-permute-start | bytes 442376 | tf_op jit(solution)/shard_map/ppermute | solution.py:19
  7.2 3.3 %collective-permute-start.1 = (bf16[1,1,12,12,512]{4,3,2,1,0:T(8,128)(2,1)S(1)}, bf16[1,1,12,12,512]{4,3,2,1,0:T(8,128)(2,1)S(1)}, u32[]{:S(2)}, u32[]{:S(2)}) collective-permute-start(bf16[1,1,12,12,512]{4,3,2,1,0:T(8,128)(2,1)S(1)} %get-tuple-element.12), channel_id=1, source_target_pairs={{1,0},{3,2},{5,4},{7,6},{9,8},{11,10},{13,12},{15,14},{17,16},{19,... | collective-permute-start | bytes 442376 | tf_op jit(solution)/shard_map/ppermute | solution.py:22
  22.7 1.7 %copy-start.2 = (bf16[864,512]{1,0:T(8,128)(2,1)}, bf16[864,512]{1,0:T(8,128)(2,1)S(1)}, u32[]{:S(2)}) copy-start(bf16[864,512]{1,0:T(8,128)(2,1)S(1)} %reshape.337.stream_ref) | copy-start | bytes 2654212
  24.5 4.1 %copy-start.1 = (bf16[864,1536]{1,0:T(8,128)(2,1)}, bf16[864,1536]{1,0:T(8,128)(2,1)S(1)}, u32[]{:S(2)}) copy-start(bf16[864,1536]{1,0:T(8,128)(2,1)S(1)} %convolution_convert_fusion.proj_ref) | copy-start | bytes 7962628
  24.5 0.7 copy-start.6
  24.7 3.8 %collective-permute-start.2 = (bf16[864,1024]{1,0:T(8,128)(2,1)S(1)}, bf16[864,1024]{1,0:T(8,128)(2,1)S(1)}, u32[]{:S(2)}, u32[]{:S(2)}) collective-permute-start(bf16[864,1024]{1,0:T(8,128)(2,1)S(1)} %slice_bitcast_fusion), channel_id=1, source_target_pairs={{0,1},{1,0},{2,3},{3,2},{4,5},{5,4},{6,7},{7,6},{8,9},{9,8},{10,11... | collective-permute-start | bytes 5308424 | tf_op jit(solution)/shard_map/ppermute | solution.py:335
  28.5 1.2 copy-start.3
  29.7 101.0 %copy-start.7 = (bf16[512,512]{1,0:T(8,128)(2,1)S(1)}, bf16[512,512]{1,0:T(8,128)(2,1)}, u32[]{:S(2)}) copy-start(bf16[512,512]{1,0:T(8,128)(2,1)} %param.17) | copy-start | bytes 1572868
where the time goes:
time: 134 us
  Pallas kernels  101 us (75%)
  other arithmetic  11.6 us (9%)
  local copies, waits for them, and re-layouts  7.1 us (5%)
  matrix products  6.23 us (5%)
  waiting for transfers between devices  4.55 us (3%)
  starting transfers between devices  3.27 us (2%)
    pallas_call x1, Pallas kernels, block_tail(): pl.pallas_call(functools.partial(block_kernel, chunks), out_shape=(plane,...  101 us
    reduce_sum x1, other arithmetic, rms_scale(): mean_sq = jnp.mean(values * values, axis=-1, keepdims=True)  9.94 us
  transfers between devices with their start and end apart: 3, of which 2 were waited for; matrix products, arithmetic and copies ran while one was open for 1% of the time, Pallas kernels for 0%

commit v1 on v0

--- a/solution.py
+++ b/solution.py
@@ -101,7 +101,7 @@
 
 
 def block_kernel(
-    chunks, proj_ref, other_ref, stream_ref, wo_ref, gain_ref, wt_ref,
+    chunks, proj_ref, other_ref, stream_ref, wo_ref, gain_ref, wt_ref, wout_ref,
     out_ref, stream2_ref, own, query2, hist, mixed, total, sum_ref, send_sem, recv_sem,
 ):
     me = lax.axis_index("tm")
@@ -257,6 +257,12 @@
                     copy_of(hop + 1, piece).start()
 
             add_term(hist[hop, span, :], span, me - (hop + 1) >= 0, False)
+            if hop + 1 == WIN:
+                temporal = (mixed[span, :] / total[span, :]).astype(jnp.bfloat16)
+                out_ref[span, :] = (
+                    stream2_ref[span, :].astype(jnp.float32)
+                    + jnp.dot(temporal, wout_ref[...], preferred_element_type=jnp.float32)
+                ).astype(out_ref.dtype)
             return carry
 
         lax.fori_loop(0, chunks, hop_step, 0)
@@ -267,20 +273,19 @@
             for piece in range(chunks):
                 copy_of(hop, piece).wait_send()
 
-    out_ref[...] = (mixed[...] / total[...]).astype(out_ref.dtype)
-
-
-def block_tail(proj, other, stream, out_space, gain_time, qkv_time, chunks=6):
+
+def block_tail(proj, other, stream, out_space, gain_time, qkv_time, out_time, chunks=9):
     rows, width = stream.shape
     gain = gain_time.astype(jnp.float32).reshape(1, width)
     vmem = pl.BlockSpec(memory_space=pltpu.VMEM)
     plane = jax.ShapeDtypeStruct((rows, width), jnp.bfloat16)
     return pl.pallas_call(
         functools.partial(block_kernel, chunks),
-        out_shape=(plane, plane),
-        in_specs=[vmem] * 6,
-        out_specs=(vmem, vmem),
+        out_shape=plane,
+        in_specs=[vmem] * 7,
+        out_specs=vmem,
         scratch_shapes=[
+            pltpu.VMEM((rows, width), jnp.bfloat16),
             pltpu.VMEM((rows, width), jnp.bfloat16),
             pltpu.VMEM((rows, width), jnp.bfloat16),
             pltpu.VMEM((WIN, rows, width), jnp.bfloat16),
@@ -293,7 +298,7 @@
         compiler_params=pltpu.CompilerParams(
             collective_id=0, has_side_effects=True, vmem_limit_bytes=56 * 1024 * 1024
         ),
-    )(proj, other, stream, out_space, gain, qkv_time)
+    )(proj, other, stream, out_space, gain, qkv_time, out_time)
 
 
 def local(
@@ -333,13 +338,9 @@
     own_kv = proj[0, :, width:]
     count = lax.axis_size("tok")
     other_kv = lax.ppermute(own_kv, "tok", [(i, (i + 1) % count) for i in range(count)])
-    temporal, stream2 = block_tail(
-        proj[0], other_kv, stream.reshape(-1, width), out_space, gain_time, qkv_time
+    output = block_tail(
+        proj[0], other_kv, stream.reshape(-1, width), out_space, gain_time, qkv_time, out_time
     )
-    time_proj = jnp.dot(
-        temporal.reshape(-1, width), out_time, preferred_element_type=jnp.float32
-    ).reshape(frames, tokens, width)
-    output = (stream2.astype(jnp.float32) + time_proj).astype(jnp.bfloat16)
     return output.reshape(frames, zdev, grid, grid, width)
 
 

time: 134 us -> 139 us (1.037)
  Pallas kernels: 101 us -> 107 us
  matrix products: 6.23 us -> 4.18 us
    pallas_call x1, Pallas kernels: 101 us -> 107 us  [block_tail(): pl.pallas_call(functools.partial(block_kernel, chunks), out_shape=plane,...]
    dot_general x1 -> x0, matrix products: 2.06 us -> none  [local(): jnp.dot(temporal.reshape(-1, width), out_time, preferred_element_type=jnp...]
where the time goes in v1:
time: 139 us
  Pallas kernels  107 us (77%)
  other arithmetic  11.6 us (8%)
  local copies, waits for them, and re-layouts  8.06 us (6%)
  waiting for transfers between devices  4.59 us (3%)
  matrix products  4.18 us (3%)
  starting transfers between devices  3.26 us (2%)
    pallas_call x1, Pallas kernels, block_tail(): pl.pallas_call(functools.partial(block_kernel, chunks), out_shape=plane,...  107 us
    reduce_sum x1, other arithmetic, rms_scale(): mean_sq = jnp.mean(values * values, axis=-1, keepdims=True)  9.94 us
  transfers between devices with their start and end apart: 3, of which 2 were waited for; matrix products, arithmetic and copies ran while one was open for 1% of the time, Pallas kernels for 0%

profile of v1, /device:TPU:24, one launch (start us, length us, event | category | flops | bytes accessed | tf_op | source)
XLA Modules:
  0.0 139.2 jit_solution(11947342821113008569)
XLA Ops:
  0.0 0.0 copy-start
  0.0 1.5 %reshape.331 = bf16[864,512]{1,0:T(8,128)(2,1)S(1)} reshape(bf16[1,6,12,12,512]{4,3,2,1,0:T(8,128)(2,1)} %param.9) | data formatting | bytes 1769472 | tf_op jit(solution)/shard_map/reshape | solution.py:319
  1.5 0.0 copy-start.4
  1.5 0.0 copy-start.5
  1.5 2.6 %convolution_convert_fusion.1 = bf16[864,512]{1,0:T(8,128)(2,1)} fusion(bf16[864,512]{1,0:T(8,128)(2,1)S(1)} %reshape.331, bf16[512,512]{1,0:T(8,128)(2,1)} %param.10), kind=kOutput, calls=%fused_computation.33 | convolution fusion | flops 453427200 | bytes 2293760 | tf_op jit(solution)/shard_map/dot_general | solution.py:318
  4.1 1.3 reshape.332
  5.4 1.8 %collective-permute-start = (bf16[1,1,12,12,512]{4,3,2,1,0:T(8,128)(2,1)S(1)}, bf16[1,1,12,12,512]{4,3,2,1,0:T(8,128)(2,1)S(1)}, u32[]{:S(2)}, u32[]{:S(2)}) collective-permute-start(bf16[1,1,12,12,512]{4,3,2,1,0:T(8,128)(2,1)S(1)} %get-tuple-element.7), channel_id=1, source_target_pairs={{0,1},{2,3},{4,5},{6,7},{8,9},{10,11},{12,13},{14,15},{16,17},{18,... | collective-permute-start | bytes 442376 | tf_op jit(solution)/shard_map/ppermute | solution.py:19
  7.2 1.3 collective-permute-start.1
  8.5 0.0 copy-done.4
  8.5 0.0 copy-done.5
  8.6 0.0 collective-permute-done
  8.6 1.9 %collective-permute-done.1 = bf16[1,1,12,12,512]{4,3,2,1,0:T(8,128)(2,1)S(1)} collective-permute-done((bf16[1,1,12,12,512]{4,3,2,1,0:T(8,128)(2,1)S(1)}, bf16[1,1,12,12,512]{4,3,2,1,0:T(8,128)(2,1)S(1)}, u32[]{:S(2)}, u32[]{:S(2)}) %collective-permute-start.1) | collective-permute-done | bytes 147488 | tf_op jit(solution)/shard_map/ppermute | solution.py:22
  10.5 0.9 select_maximum_fusion
  11.4 9.9 %multiply_reduce_fusion = (f32[6,12,12]{2,1,0:T(8,128)S(1)}, bf16[1,6,12,12,512]{4,3,2,1,0:T(8,128)(2,1)}) fusion(bf16[1,8,14,14,512]{4,3,2,1,0:T(8,128)(2,1)S(1)} %select_maximum_fusion, f32[512]{0:T(512)S(1)} %bitcast.60, f32[512]{0:T(512)S(1)} %bitcast.61, f32[512]{0:T(512)S(1)} %bitcast.36, f32[512]{0:T(512)S(1)} %bitcast.37, ...), kind=kLoop, calls=%fused_computation.24 | loop fusion | flops 38485152 | bytes 23356800 | tf_op jit(solution)/shard_map/reduce_sum | solution.py:34
  21.3 1.4 reshape.333.stream_ref
  22.7 0.0 copy-start.2
  22.7 0.1 rsqrt.12
  22.8 0.0 copy-done
  22.8 1.6 %convolution_convert_fusion.proj_ref = bf16[864,1536]{1,0:T(8,128)(2,1)S(1)} fusion(bf16[512,1536]{1,0:T(8,128)(2,1)S(1)} %copy-done, bf16[864,512]{1,0:T(8,128)(2,1)S(1)} %reshape.333.stream_ref, f32[512]{0:T(512)S(1)} %convert_element_type.479, f32[864]{0:T(1024)S(1)} %rsqrt.12), kind=kOutput, calls=%fused_computation.7 | convolution fusion | flops 1362051072 | bytes 5117312 | tf_op jit(solution)/shard_map/dot_general | solution.py:334
  24.5 0.0 copy-done.2
  24.5 0.0 copy-start.1
  24.5 0.0 copy-start.6
  24.5 0.3 slice_bitcast_fusion
  24.7 0.2 collective-permute-start.2
  25.0 0.2 copy-done.6
  25.2 0.7 reshape.365
  25.9 2.7 %collective-permute-done.2.other_ref = bf16[864,1024]{1,0:T(8,128)(2,1)S(1)} collective-permute-done((bf16[864,1024]{1,0:T(8,128)(2,1)S(1)}, bf16[864,1024]{1,0:T(8,128)(2,1)S(1)}, u32[]{:S(2)}, u32[]{:S(2)}) %collective-permute-start.2) | collective-permute-done | bytes 1769504 | tf_op jit(solution)/shard_map/ppermute | solution.py:340
  28.5 0.0 copy-start.3
  28.5 0.0 copy-done.1
  28.5 1.2 copy-done.3
  29.7 107.3 %shard_map.91 = bf16[864,512]{1,0:T(8,128)(2,1)} custom-call(bf16[864,1536]{1,0:T(8,128)(2,1)} %copy-done.1, bf16[864,1024]{1,0:T(8,128)(2,1)} %copy-done.3, bf16[864,512]{1,0:T(8,128)(2,1)} %copy-done.2, bf16[512,512]{1,0:T(8,128)(2,1)} %wo_ref.1, f32[1,512]{1,0:T(1,128)} %bitcast.62, bf16[512,1536]{1,0:T(8,128)(2,1)} %wt_ref.1, bf16[512,512]{1,0:T(8,128)(2,1)} %wout_ref.1), custom_call_target="tpu_custom_call" | custom-call | tf_op jit(solution)/shard_map/pallas_call | solution.py:282
  137.0 2.2 %reshape.337 = bf16[1,6,12,12,512]{4,3,2,1,0:T(8,128)(2,1)} reshape(bf16[864,512]{1,0:T(8,128)(2,1)} %shard_map.91) | data formatting | bytes 1769472 | tf_op jit(solution)/shard_map/reshape | solution.py:344
  (5 shorter events, 0.1 us)
Async XLA Ops:
  0.0 22.8 %copy-start = (bf16[512,1536]{1,0:T(8,128)(2,1)S(1)}, bf16[512,1536]{1,0:T(8,128)(2,1)}, u32[]{:S(2)}) copy-start(bf16[512,1536]{1,0:T(8,128)(2,1)} %param.13) | copy-start | bytes 4718596
  1.5 7.0 %copy-start.4 = (bf16[27,512]{1,0:T(8,128)(2,1)S(1)}, bf16[27,512]{1,0:T(8,128)(2,1)}, u32[]{:S(2)}) copy-start(bf16[27,512]{1,0:T(8,128)(2,1)} %param.11) | copy-start | bytes 82948
  1.5 7.0 %copy-start.5 = (bf16[512]{0:T(512)(128)(2,1)S(1)}, bf16[512]{0:T(512)(128)(2,1)}, u32[]{:S(2)}) copy-start(bf16[512]{0:T(512)(128)(2,1)} %param.12) | copy-start | bytes 3076
  5.4 3.2 %collective-permute-start = (bf16[1,1,12,12,512]{4,3,2,1,0:T(8,128)(2,1)S(1)}, bf16[1,1,12,12,512]{4,3,2,1,0:T(8,128)(2,1)S(1)}, u32[]{:S(2)}, u32[]{:S(2)}) collective-permute-start(bf16[1,1,12,12,512]{4,3,2,1,0:T(8,128)(2,1)S(1)} %get-tuple-element.7), channel_id=1, source_target_pairs={{0,1},{2,3},{4,5},{6,7},{8,9},{10,11},{12,13},{14,15},{16,17},{18,... | collective-permute-start | bytes 442376 | tf_op jit(solution)/shard_map/ppermute | solution.py:19
  7.2 3.3 %collective-permute-start.1 = (bf16[1,1,12,12,512]{4,3,2,1,0:T(8,128)(2,1)S(1)}, bf16[1,1,12,12,512]{4,3,2,1,0:T(8,128)(2,1)S(1)}, u32[]{:S(2)}, u32[]{:S(2)}) collective-permute-start(bf16[1,1,12,12,512]{4,3,2,1,0:T(8,128)(2,1)S(1)} %get-tuple-element.8), channel_id=1, source_target_pairs={{1,0},{3,2},{5,4},{7,6},{9,8},{11,10},{13,12},{15,14},{17,16},{19,... | collective-permute-start | bytes 442376 | tf_op jit(solution)/shard_map/ppermute | solution.py:22
  22.7 1.8 %copy-start.2 = (bf16[864,512]{1,0:T(8,128)(2,1)}, bf16[864,512]{1,0:T(8,128)(2,1)S(1)}, u32[]{:S(2)}) copy-start(bf16[864,512]{1,0:T(8,128)(2,1)S(1)} %reshape.333.stream_ref) | copy-start | bytes 2654212
  24.5 4.1 %copy-start.1 = (bf16[864,1536]{1,0:T(8,128)(2,1)}, bf16[864,1536]{1,0:T(8,128)(2,1)S(1)}, u32[]{:S(2)}) copy-start(bf16[864,1536]{1,0:T(8,128)(2,1)S(1)} %convolution_convert_fusion.proj_ref) | copy-start | bytes 7962628
  24.5 0.7 copy-start.6
  24.7 3.8 %collective-permute-start.2 = (bf16[864,1024]{1,0:T(8,128)(2,1)S(1)}, bf16[864,1024]{1,0:T(8,128)(2,1)S(1)}, u32[]{:S(2)}, u32[]{:S(2)}) collective-permute-start(bf16[864,1024]{1,0:T(8,128)(2,1)S(1)} %slice_bitcast_fusion), channel_id=1, source_target_pairs={{0,1},{1,0},{2,3},{3,2},{4,5},{5,4},{6,7},{7,6},{8,9},{9,8},{10,11... | collective-permute-start | bytes 5308424 | tf_op jit(solution)/shard_map/ppermute | solution.py:340
  28.5 1.2 copy-start.3

commit v2 on v0

--- a/solution.py
+++ b/solution.py
@@ -61,48 +61,9 @@
     return result.transpose(1, 0, 2).reshape(rows, cols)
 
 
-def pair_attention_kernel(q_ref, k_ref, v_ref, o_ref):
-    head_size = D // H
-    scale = head_size ** (-0.5)
-    q = q_ref[...]
-    k = k_ref[...]
-    v = v_ref[...]
-    lane = lax.broadcasted_iota(jnp.int32, (1, q.shape[1]), 1)
-    first = lane < head_size
-    outs = []
-    for mask in (first, jnp.logical_not(first)):
-        q_one = jnp.where(mask, q, jnp.zeros_like(q))
-        scores = lax.dot_general(
-            q_one, k, (((1,), (1,)), ((), ())), preferred_element_type=jnp.float32
-        ) * scale
-        expo = jnp.exp(scores)
-        total = jnp.sum(expo, axis=-1, keepdims=True)
-        mixed = jnp.dot(expo.astype(jnp.bfloat16), v, preferred_element_type=jnp.float32)
-        outs.append(mixed / total)
-    o_ref[...] = jnp.where(first, outs[0], outs[1]).astype(o_ref.dtype)
-
-
-def spatial_attention(query, keys, values, block_rows=288):
-    rows, width = query.shape
-    count = keys.shape[0]
-    lanes = 2 * (D // H)
-    grid = (width // lanes, rows // block_rows)
-    return pl.pallas_call(
-        pair_attention_kernel,
-        out_shape=jax.ShapeDtypeStruct((rows, width), jnp.bfloat16),
-        grid=grid,
-        in_specs=[
-            pl.BlockSpec((block_rows, lanes), lambda h, r: (r, h)),
-            pl.BlockSpec((count, lanes), lambda h, r: (0, h)),
-            pl.BlockSpec((count, lanes), lambda h, r: (0, h)),
-        ],
-        out_specs=pl.BlockSpec((block_rows, lanes), lambda h, r: (r, h)),
-    )(query, keys, values)
-
-
 def block_kernel(
-    chunks, proj_ref, other_ref, stream_ref, wo_ref, gain_ref, wt_ref,
-    out_ref, stream2_ref, own, query2, hist, mixed, total, sum_ref, send_sem, recv_sem,
+    chunks, group, proj_ref, other_ref, stream_ref, wo_ref, gain_ref, wt_ref,
+    out_ref, stream2_ref, own, query2, hist, mixed, total, sum_ref, send_first, recv_first, send_sem, recv_sem,
 ):
     me = lax.axis_index("tm")
     count = lax.axis_size("tm")
@@ -142,13 +103,19 @@
         return pl.ds(pl.multiple_of(piece * rows, 8), rows)
 
     def copy_of(hop, piece):
-        span = span_of(piece)
-        source = own.at[span] if hop == 0 else hist.at[hop - 1, span]
+        if hop == 0:
+            span = span_of(piece)
+            source = own.at[span]
+            sems = (send_first.at[piece], recv_first.at[piece])
+        else:
+            span = pl.ds(pl.multiple_of(piece * rows * group, 8), rows * group)
+            source = hist.at[hop - 1, span]
+            sems = (send_sem.at[hop - 1, piece], recv_sem.at[hop - 1, piece])
         return pltpu.make_async_remote_copy(
             src_ref=source,
             dst_ref=hist.at[hop, span],
-            send_sem=send_sem.at[hop, piece],
-            recv_sem=recv_sem.at[hop, piece],
+            send_sem=sems[0],
+            recv_sem=sems[1],
             device_id=(me + 1, core),
             device_id_type=mesh_ids,
         )
@@ -243,10 +210,24 @@
     def _():
         copy_of(0, chunks - 1).start()
 
-    for hop in range(WIN):
+    def first_step(piece, carry):
+        span = span_of(piece)
+
+        @pl.when(has_left)
+        def _():
+            copy_of(0, piece).wait_recv()
+
+        @pl.when(jnp.logical_and(has_right, piece % group == group - 1))
+        def _():
+            copy_of(1, piece // group).start()
+
+        add_term(hist[0, span, :], span, me - 1 >= 0, False)
+        return carry
+
+    lax.fori_loop(0, chunks, first_step, 0)
+
+    for hop in range(1, WIN):
         def hop_step(piece, carry, hop=hop):
-            span = span_of(piece)
-
             @pl.when(has_left)
             def _():
                 copy_of(hop, piece).wait_recv()
@@ -256,27 +237,31 @@
                 def _():
                     copy_of(hop + 1, piece).start()
 
-            add_term(hist[hop, span, :], span, me - (hop + 1) >= 0, False)
+            for part in range(group):
+                span = span_of(piece * group + part)
+                add_term(hist[hop, span, :], span, me - (hop + 1) >= 0, False)
             return carry
 
-        lax.fori_loop(0, chunks, hop_step, 0)
+        lax.fori_loop(0, chunks // group, hop_step, 0)
 
     @pl.when(has_right)
     def _():
-        for hop in range(WIN):
-            for piece in range(chunks):
+        for piece in range(chunks):
+            copy_of(0, piece).wait_send()
+        for hop in range(1, WIN):
+            for piece in range(chunks // group):
                 copy_of(hop, piece).wait_send()
 
     out_ref[...] = (mixed[...] / total[...]).astype(out_ref.dtype)
 
 
-def block_tail(proj, other, stream, out_space, gain_time, qkv_time, chunks=6):
+def block_tail(proj, other, stream, out_space, gain_time, qkv_time, chunks=6, group=3):
     rows, width = stream.shape
     gain = gain_time.astype(jnp.float32).reshape(1, width)
     vmem = pl.BlockSpec(memory_space=pltpu.VMEM)
     plane = jax.ShapeDtypeStruct((rows, width), jnp.bfloat16)
     return pl.pallas_call(
-        functools.partial(block_kernel, chunks),
+        functools.partial(block_kernel, chunks, group),
         out_shape=(plane, plane),
         in_specs=[vmem] * 6,
         out_specs=(vmem, vmem),
@@ -287,8 +272,10 @@
             pltpu.VMEM((rows, width), jnp.float32),
             pltpu.VMEM((rows, width), jnp.float32),
             pltpu.VMEM((width, width), jnp.bfloat16),
-            pltpu.SemaphoreType.DMA((WIN, chunks)),
-            pltpu.SemaphoreType.DMA((WIN, chunks)),
+            pltpu.SemaphoreType.DMA((chunks,)),
+            pltpu.SemaphoreType.DMA((chunks,)),
+            pltpu.SemaphoreType.DMA((WIN - 1, chunks // group)),
+            pltpu.SemaphoreType.DMA((WIN - 1, chunks // group)),
         ],
         compiler_params=pltpu.CompilerParams(
             collective_id=0, has_side_effects=True, vmem_limit_bytes=56 * 1024 * 1024

time: 134 us -> 135 us (level)
  no operation moved by 1% of the time
where the time goes in v2:
time: 135 us; the launch traced here: 134 us
  Pallas kernels  101 us (75%)
  other arithmetic  11.6 us (9%)
  local copies, waits for them, and re-layouts  7.1 us (5%)
  matrix products  6.23 us (5%)
  waiting for transfers between devices  4.55 us (3%)
  starting transfers between devices  3.27 us (2%)
    pallas_call x1, Pallas kernels, block_tail(): pl.pallas_call(functools.partial(block_kernel, chunks, group), out_shape=...  101 us
    reduce_sum x1, other arithmetic, rms_scale(): mean_sq = jnp.mean(values * values, axis=-1, keepdims=True)  9.94 us
  transfers between devices with their start and end apart: 3, of which 2 were waited for; matrix products, arithmetic and copies ran while one was open for 1% of the time, Pallas kernels for 0%

profile of v2, /device:TPU:24, one launch (start us, length us, event | category | flops | bytes accessed | tf_op | source)
XLA Modules:
  0.0 134.5 jit_solution(8925100281328113026)
XLA Ops:
  0.0 0.0 copy-start
  0.0 1.5 %reshape.335 = bf16[864,512]{1,0:T(8,128)(2,1)S(1)} reshape(bf16[1,6,12,12,512]{4,3,2,1,0:T(8,128)(2,1)} %param.9) | data formatting | bytes 1769472 | tf_op jit(solution)/shard_map/reshape | solution.py:301
  1.5 0.0 copy-start.4
  1.5 0.0 copy-start.5
  1.5 2.6 %convolution_convert_fusion.1 = bf16[864,512]{1,0:T(8,128)(2,1)} fusion(bf16[864,512]{1,0:T(8,128)(2,1)S(1)} %reshape.335, bf16[512,512]{1,0:T(8,128)(2,1)} %param.10), kind=kOutput, calls=%fused_computation.34 | convolution fusion | flops 453427200 | bytes 2293760 | tf_op jit(solution)/shard_map/dot_general | solution.py:300
  4.1 1.3 reshape.336
  5.4 1.8 %collective-permute-start = (bf16[1,1,12,12,512]{4,3,2,1,0:T(8,128)(2,1)S(1)}, bf16[1,1,12,12,512]{4,3,2,1,0:T(8,128)(2,1)S(1)}, u32[]{:S(2)}, u32[]{:S(2)}) collective-permute-start(bf16[1,1,12,12,512]{4,3,2,1,0:T(8,128)(2,1)S(1)} %get-tuple-element.11), channel_id=1, source_target_pairs={{0,1},{2,3},{4,5},{6,7},{8,9},{10,11},{12,13},{14,15},{16,17},{18,... | collective-permute-start | bytes 442376 | tf_op jit(solution)/shard_map/ppermute | solution.py:19
  7.2 1.3 collective-permute-start.1
  8.5 0.0 copy-done.4
  8.5 0.0 copy-done.5
  8.6 0.0 collective-permute-done
  8.6 1.9 %collective-permute-done.1 = bf16[1,1,12,12,512]{4,3,2,1,0:T(8,128)(2,1)S(1)} collective-permute-done((bf16[1,1,12,12,512]{4,3,2,1,0:T(8,128)(2,1)S(1)}, bf16[1,1,12,12,512]{4,3,2,1,0:T(8,128)(2,1)S(1)}, u32[]{:S(2)}, u32[]{:S(2)}) %collective-permute-start.1) | collective-permute-done | bytes 147488 | tf_op jit(solution)/shard_map/ppermute | solution.py:22
  10.5 0.9 select_maximum_fusion
  11.4 9.9 %multiply_reduce_fusion = (f32[6,12,12]{2,1,0:T(8,128)S(1)}, bf16[1,6,12,12,512]{4,3,2,1,0:T(8,128)(2,1)}) fusion(bf16[1,8,14,14,512]{4,3,2,1,0:T(8,128)(2,1)S(1)} %select_maximum_fusion, f32[512]{0:T(512)S(1)} %bitcast.62, f32[512]{0:T(512)S(1)} %bitcast.63, f32[512]{0:T(512)S(1)} %bitcast.38, f32[512]{0:T(512)S(1)} %bitcast.39, ...), kind=kLoop, calls=%fused_computation.24 | loop fusion | flops 38485152 | bytes 23356800 | tf_op jit(solution)/shard_map/reduce_sum | solution.py:34
  21.3 1.4 %reshape.337.stream_ref = bf16[864,512]{1,0:T(8,128)(2,1)S(1)} reshape(bf16[1,6,12,12,512]{4,3,2,1,0:T(8,128)(2,1)} %get-tuple-element.10) | data formatting | bytes 1769472 | tf_op jit(solution)/shard_map/reshape | solution.py:314
  22.7 0.0 copy-start.2
  22.7 0.1 rsqrt.12
  22.8 0.0 copy-done
  22.8 1.6 %convolution_convert_fusion.proj_ref = bf16[864,1536]{1,0:T(8,128)(2,1)S(1)} fusion(bf16[512,1536]{1,0:T(8,128)(2,1)S(1)} %copy-done, bf16[864,512]{1,0:T(8,128)(2,1)S(1)} %reshape.337.stream_ref, f32[512]{0:T(512)S(1)} %convert_element_type.486, f32[864]{0:T(1024)S(1)} %rsqrt.12), kind=kOutput, calls=%fused_computation.7 | convolution fusion | flops 1362051072 | bytes 5117312 | tf_op jit(solution)/shard_map/dot_general | solution.py:316
  24.4 0.0 copy-done.2
  24.5 0.0 copy-start.1
  24.5 0.0 copy-start.6
  24.5 0.3 slice_bitcast_fusion
  24.7 0.2 collective-permute-start.2
  25.0 0.2 copy-done.6
  25.2 0.7 reshape.369
  25.9 2.6 %collective-permute-done.2.other_ref = bf16[864,1024]{1,0:T(8,128)(2,1)S(1)} collective-permute-done((bf16[864,1024]{1,0:T(8,128)(2,1)S(1)}, bf16[864,1024]{1,0:T(8,128)(2,1)S(1)}, u32[]{:S(2)}, u32[]{:S(2)}) %collective-permute-start.2) | collective-permute-done | bytes 1769504 | tf_op jit(solution)/shard_map/ppermute | solution.py:322
  28.5 0.0 copy-start.3
  28.5 0.0 copy-done.1
  28.5 1.2 copy-done.3
  29.7 0.0 copy-start.7
  29.7 101.5 %shard_map.91 = (bf16[864,512]{1,0:T(8,128)(2,1)}, bf16[864,512]{1,0:T(8,128)(2,1)}) custom-call(bf16[864,1536]{1,0:T(8,128)(2,1)} %copy-done.1, bf16[864,1024]{1,0:T(8,128)(2,1)} %copy-done.3, bf16[864,512]{1,0:T(8,128)(2,1)} %copy-done.2, bf16[512,512]{1,0:T(8,128)(2,1)} %wo_ref.1, f32[1,512]{1,0:T(1,128)} %bitcast.64, bf16[512,1536]{1,0:T(8,128)(2,1)} %wt_ref.1), custom_call_target="tpu_custom_call" | custom-call | tf_op jit(solution)/shard_map/pallas_call | solution.py:263
  131.2 0.0 copy-done.7
  131.2 2.1 %add_convert_fusion = bf16[864,512]{1,0:T(8,128)(2,1)S(1)} fusion(bf16[864,512]{1,0:T(8,128)(2,1)} %get-tuple-element.7, bf16[864,512]{1,0:T(8,128)(2,1)} %get-tuple-element.8, bf16[512,512]{1,0:T(8,128)(2,1)S(1)} %copy-done.7), kind=kOutput, calls=%fused_computation.32 | convolution fusion | flops 454311936 | bytes 3178496 | tf_op jit(solution)/shard_map/dot_general | solution.py:326
  133.3 1.2 reshape.341
  (5 shorter events, 0.1 us)
Async XLA Ops:
  0.0 22.8 %copy-start = (bf16[512,1536]{1,0:T(8,128)(2,1)S(1)}, bf16[512,1536]{1,0:T(8,128)(2,1)}, u32[]{:S(2)}) copy-start(bf16[512,1536]{1,0:T(8,128)(2,1)} %param.13) | copy-start | bytes 4718596
  1.5 7.0 %copy-start.4 = (bf16[27,512]{1,0:T(8,128)(2,1)S(1)}, bf16[27,512]{1,0:T(8,128)(2,1)}, u32[]{:S(2)}) copy-start(bf16[27,512]{1,0:T(8,128)(2,1)} %param.11) | copy-start | bytes 82948
  1.5 7.0 %copy-start.5 = (bf16[512]{0:T(512)(128)(2,1)S(1)}, bf16[512]{0:T(512)(128)(2,1)}, u32[]{:S(2)}) copy-start(bf16[512]{0:T(512)(128)(2,1)} %param.12) | copy-start | bytes 3076
  5.4 3.2 %collective-permute-start = (bf16[1,1,12,12,512]{4,3,2,1,0:T(8,128)(2,1)S(1)}, bf16[1,1,12,12,512]{4,3,2,1,0:T(8,128)(2,1)S(1)}, u32[]{:S(2)}, u32[]{:S(2)}) collective-permute-start(bf16[1,1,12,12,512]{4,3,2,1,0:T(8,128)(2,1)S(1)} %get-tuple-element.11), channel_id=1, source_target_pairs={{0,1},{2,3},{4,5},{6,7},{8,9},{10,11},{12,13},{14,15},{16,17},{18,... | collective-permute-start | bytes 442376 | tf_op jit(solution)/shard_map/ppermute | solution.py:19
  7.2 3.3 %collective-permute-start.1 = (bf16[1,1,12,12,512]{4,3,2,1,0:T(8,128)(2,1)S(1)}, bf16[1,1,12,12,512]{4,3,2,1,0:T(8,128)(2,1)S(1)}, u32[]{:S(2)}, u32[]{:S(2)}) collective-permute-start(bf16[1,1,12,12,512]{4,3,2,1,0:T(8,128)(2,1)S(1)} %get-tuple-element.12), channel_id=1, source_target_pairs={{1,0},{3,2},{5,4},{7,6},{9,8},{11,10},{13,12},{15,14},{17,16},{19,... | collective-permute-start | bytes 442376 | tf_op jit(solution)/shard_map/ppermute | solution.py:22
  22.7 1.7 %copy-start.2 = (bf16[864,512]{1,0:T(8,128)(2,1)}, bf16[864,512]{1,0:T(8,128)(2,1)S(1)}, u32[]{:S(2)}) copy-start(bf16[864,512]{1,0:T(8,128)(2,1)S(1)} %reshape.337.stream_ref) | copy-start | bytes 2654212
  24.5 4.1 %copy-start.1 = (bf16[864,1536]{1,0:T(8,128)(2,1)}, bf16[864,1536]{1,0:T(8,128)(2,1)S(1)}, u32[]{:S(2)}) copy-start(bf16[864,1536]{1,0:T(8,128)(2,1)S(1)} %convolution_convert_fusion.proj_ref) | copy-start | bytes 7962628
  24.5 0.7 copy-start.6
  24.7 3.8 %collective-permute-start.2 = (bf16[864,1024]{1,0:T(8,128)(2,1)S(1)}, bf16[864,1024]{1,0:T(8,128)(2,1)S(1)}, u32[]{:S(2)}, u32[]{:S(2)}) collective-permute-start(bf16[864,1024]{1,0:T(8,128)(2,1)S(1)} %slice_bitcast_fusion), channel_id=1, source_target_pairs={{0,1},{1,0},{2,3},{3,2},{4,5},{5,4},{6,7},{7,6},{8,9},{9,8},{10,11... | collective-permute-start | bytes 5308424 | tf_op jit(solution)/shard_map/ppermute | solution.py:322
  28.5 1.2 copy-start.3
  29.7 101.5 %copy-start.7 = (bf16[512,512]{1,0:T(8,128)(2,1)S(1)}, bf16[512,512]{1,0:T(8,128)(2,1)}, u32[]{:S(2)}) copy-start(bf16[512,512]{1,0:T(8,128)(2,1)} %param.17) | copy-start | bytes 1572868

commit v3 on v0

--- a/solution.py
+++ b/solution.py
@@ -59,45 +59,6 @@
     )
     result = lax.map(one_head, parts)
     return result.transpose(1, 0, 2).reshape(rows, cols)
-
-
-def pair_attention_kernel(q_ref, k_ref, v_ref, o_ref):
-    head_size = D // H
-    scale = head_size ** (-0.5)
-    q = q_ref[...]
-    k = k_ref[...]
-    v = v_ref[...]
-    lane = lax.broadcasted_iota(jnp.int32, (1, q.shape[1]), 1)
-    first = lane < head_size
-    outs = []
-    for mask in (first, jnp.logical_not(first)):
-        q_one = jnp.where(mask, q, jnp.zeros_like(q))
-        scores = lax.dot_general(
-            q_one, k, (((1,), (1,)), ((), ())), preferred_element_type=jnp.float32
-        ) * scale
-        expo = jnp.exp(scores)
-        total = jnp.sum(expo, axis=-1, keepdims=True)
-        mixed = jnp.dot(expo.astype(jnp.bfloat16), v, preferred_element_type=jnp.float32)
-        outs.append(mixed / total)
-    o_ref[...] = jnp.where(first, outs[0], outs[1]).astype(o_ref.dtype)
-
-
-def spatial_attention(query, keys, values, block_rows=288):
-    rows, width = query.shape
-    count = keys.shape[0]
-    lanes = 2 * (D // H)
-    grid = (width // lanes, rows // block_rows)
-    return pl.pallas_call(
-        pair_attention_kernel,
-        out_shape=jax.ShapeDtypeStruct((rows, width), jnp.bfloat16),
-        grid=grid,
-        in_specs=[
-            pl.BlockSpec((block_rows, lanes), lambda h, r: (r, h)),
-            pl.BlockSpec((count, lanes), lambda h, r: (0, h)),
-            pl.BlockSpec((count, lanes), lambda h, r: (0, h)),
-        ],
-        out_specs=pl.BlockSpec((block_rows, lanes), lambda h, r: (r, h)),
-    )(query, keys, values)
 
 
 def block_kernel(
@@ -158,6 +119,27 @@
     heads = lax.broadcasted_iota(jnp.int32, (width, width), 0) // head_size
     same_head = heads == lax.broadcasted_iota(jnp.int32, (width, width), 1) // head_size
     sum_ref[...] = same_head.astype(jnp.bfloat16)
+
+    def add_term(block, span, valid, first):
+        kv = jnp.dot(block, wt_ref[:, width:], preferred_element_type=jnp.float32).astype(jnp.bfloat16)
+        keys2 = kv[:, :width].astype(jnp.float32)
+        values2 = kv[:, width:].astype(jnp.float32)
+        prod = query2[span, :].astype(jnp.float32) * keys2
+        high = prod.astype(jnp.bfloat16)
+        low = (prod - high.astype(jnp.float32)).astype(jnp.bfloat16)
+        summer = sum_ref[...]
+        scores = (
+            jnp.dot(high, summer, preferred_element_type=jnp.float32)
+            + jnp.dot(low, summer, preferred_element_type=jnp.float32)
+        ) * scale
+        expo = jnp.where(valid, jnp.exp(scores), 0.0)
+        part = expo.astype(jnp.bfloat16).astype(jnp.float32) * values2
+        if first:
+            mixed[span, :] = part
+            total[span, :] = expo
+        else:
+            mixed[span, :] += part
+            total[span, :] += expo
 
     def space_step(piece, carry):
         span = span_of(piece)
@@ -203,45 +185,15 @@
             normed2, wt_ref[:, :width], preferred_element_type=jnp.float32
         ).astype(jnp.bfloat16)
 
-        @pl.when(jnp.logical_and(has_right, piece >= 1))
+        add_term(own[span, :], span, True, True)
+
+        @pl.when(has_right)
         def _():
-            copy_of(0, piece - 1).start()
+            copy_of(0, piece).start()
 
         return carry
 
     lax.fori_loop(0, chunks, space_step, 0)
-
-    def add_term(block, span, valid, first):
-        kv = jnp.dot(block, wt_ref[:, width:], preferred_element_type=jnp.float32).astype(jnp.bfloat16)
-        keys2 = kv[:, :width].astype(jnp.float32)
-        values2 = kv[:, width:].astype(jnp.float32)
-        prod = query2[span, :].astype(jnp.float32) * keys2
-        high = prod.astype(jnp.bfloat16)
-        low = (prod - high.astype(jnp.float32)).astype(jnp.bfloat16)
-        summer = sum_ref[...]
-        scores = (
-            jnp.dot(high, summer, preferred_element_type=jnp.float32)
-            + jnp.dot(low, summer, preferred_element_type=jnp.float32)
-        ) * scale
-        expo = jnp.where(valid, jnp.exp(scores), 0.0)
-        part = expo.astype(jnp.bfloat16).astype(jnp.float32) * values2
-        if first:
-            mixed[span, :] = part
-            total[span, :] = expo
-        else:
-            mixed[span, :] += part
-            total[span, :] += expo
-
-    def own_step(piece, carry):
-        span = span_of(piece)
-        add_term(own[span, :], span, True, True)
-        return carry
-
-    lax.fori_loop(0, chunks, own_step, 0)
-
-    @pl.when(has_right)
-    def _():
-        copy_of(0, chunks - 1).start()
 
     for hop in range(WIN):
         def hop_step(piece, carry, hop=hop):

time: 134 us -> 133 us (level)
  no operation moved by 1% of the time
where the time goes in v3:
time: 133 us
  Pallas kernels  100 us (75%)
  other arithmetic  11.6 us (9%)
  local copies, waits for them, and re-layouts  7.1 us (5%)
  matrix products  6.23 us (5%)
  waiting for transfers between devices  4.55 us (3%)
  starting transfers between devices  3.27 us (2%)
    pallas_call x1, Pallas kernels, block_tail(): pl.pallas_call(functools.partial(block_kernel, chunks), out_shape=(plane,...  100 us
    reduce_sum x1, other arithmetic, rms_scale(): mean_sq = jnp.mean(values * values, axis=-1, keepdims=True)  9.94 us
  transfers between devices with their start and end apart: 3, of which 2 were waited for; matrix products, arithmetic and copies ran while one was open for 1% of the time, Pallas kernels for 0%

profile of v3, /device:TPU:24, one launch (start us, length us, event | category | flops | bytes accessed | tf_op | source)
XLA Modules:
  0.0 133.0 jit_solution(4359796992144025703)
XLA Ops:
  0.0 0.0 copy-start
  0.0 1.5 %reshape.335 = bf16[864,512]{1,0:T(8,128)(2,1)S(1)} reshape(bf16[1,6,12,12,512]{4,3,2,1,0:T(8,128)(2,1)} %param.9) | data formatting | bytes 1769472 | tf_op jit(solution)/shard_map/reshape | solution.py:266
  1.5 0.0 copy-start.4
  1.5 0.0 copy-start.5
  1.5 2.6 %convolution_convert_fusion.1 = bf16[864,512]{1,0:T(8,128)(2,1)} fusion(bf16[864,512]{1,0:T(8,128)(2,1)S(1)} %reshape.335, bf16[512,512]{1,0:T(8,128)(2,1)} %param.10), kind=kOutput, calls=%fused_computation.34 | convolution fusion | flops 453427200 | bytes 2293760 | tf_op jit(solution)/shard_map/dot_general | solution.py:265
  4.1 1.3 reshape.336
  5.4 1.8 %collective-permute-start = (bf16[1,1,12,12,512]{4,3,2,1,0:T(8,128)(2,1)S(1)}, bf16[1,1,12,12,512]{4,3,2,1,0:T(8,128)(2,1)S(1)}, u32[]{:S(2)}, u32[]{:S(2)}) collective-permute-start(bf16[1,1,12,12,512]{4,3,2,1,0:T(8,128)(2,1)S(1)} %get-tuple-element.11), channel_id=1, source_target_pairs={{0,1},{2,3},{4,5},{6,7},{8,9},{10,11},{12,13},{14,15},{16,17},{18,... | collective-permute-start | bytes 442376 | tf_op jit(solution)/shard_map/ppermute | solution.py:19
  7.2 1.3 collective-permute-start.1
  8.5 0.0 copy-done.4
  8.5 0.0 copy-done.5
  8.6 0.0 collective-permute-done
  8.6 1.9 %collective-permute-done.1 = bf16[1,1,12,12,512]{4,3,2,1,0:T(8,128)(2,1)S(1)} collective-permute-done((bf16[1,1,12,12,512]{4,3,2,1,0:T(8,128)(2,1)S(1)}, bf16[1,1,12,12,512]{4,3,2,1,0:T(8,128)(2,1)S(1)}, u32[]{:S(2)}, u32[]{:S(2)}) %collective-permute-start.1) | collective-permute-done | bytes 147488 | tf_op jit(solution)/shard_map/ppermute | solution.py:22
  10.5 0.9 select_maximum_fusion
  11.4 9.9 %multiply_reduce_fusion = (f32[6,12,12]{2,1,0:T(8,128)S(1)}, bf16[1,6,12,12,512]{4,3,2,1,0:T(8,128)(2,1)}) fusion(bf16[1,8,14,14,512]{4,3,2,1,0:T(8,128)(2,1)S(1)} %select_maximum_fusion, f32[512]{0:T(512)S(1)} %bitcast.62, f32[512]{0:T(512)S(1)} %bitcast.63, f32[512]{0:T(512)S(1)} %bitcast.38, f32[512]{0:T(512)S(1)} %bitcast.39, ...), kind=kLoop, calls=%fused_computation.24 | loop fusion | flops 38485152 | bytes 23356800 | tf_op jit(solution)/shard_map/reduce_sum | solution.py:34
  21.3 1.4 %reshape.337.stream_ref = bf16[864,512]{1,0:T(8,128)(2,1)S(1)} reshape(bf16[1,6,12,12,512]{4,3,2,1,0:T(8,128)(2,1)} %get-tuple-element.10) | data formatting | bytes 1769472 | tf_op jit(solution)/shard_map/reshape | solution.py:279
  22.7 0.0 copy-start.2
  22.7 0.1 rsqrt.12
  22.8 0.0 copy-done
  22.8 1.6 %convolution_convert_fusion.proj_ref = bf16[864,1536]{1,0:T(8,128)(2,1)S(1)} fusion(bf16[512,1536]{1,0:T(8,128)(2,1)S(1)} %copy-done, bf16[864,512]{1,0:T(8,128)(2,1)S(1)} %reshape.337.stream_ref, f32[512]{0:T(512)S(1)} %convert_element_type.486, f32[864]{0:T(1024)S(1)} %rsqrt.12), kind=kOutput, calls=%fused_computation.7 | convolution fusion | flops 1362051072 | bytes 5117312 | tf_op jit(solution)/shard_map/dot_general | solution.py:281
  24.4 0.0 copy-done.2
  24.5 0.0 copy-start.1
  24.5 0.0 copy-start.6
  24.5 0.3 slice_bitcast_fusion
  24.7 0.2 collective-permute-start.2
  25.0 0.2 copy-done.6
  25.2 0.7 reshape.369
  25.9 2.6 %collective-permute-done.2.other_ref = bf16[864,1024]{1,0:T(8,128)(2,1)S(1)} collective-permute-done((bf16[864,1024]{1,0:T(8,128)(2,1)S(1)}, bf16[864,1024]{1,0:T(8,128)(2,1)S(1)}, u32[]{:S(2)}, u32[]{:S(2)}) %collective-permute-start.2) | collective-permute-done | bytes 1769504 | tf_op jit(solution)/shard_map/ppermute | solution.py:287
  28.5 0.0 copy-start.3
  28.5 0.0 copy-done.1
  28.5 1.2 copy-done.3
  29.7 0.0 copy-start.7
  29.7 100.0 %shard_map.91 = (bf16[864,512]{1,0:T(8,128)(2,1)}, bf16[864,512]{1,0:T(8,128)(2,1)}) custom-call(bf16[864,1536]{1,0:T(8,128)(2,1)} %copy-done.1, bf16[864,1024]{1,0:T(8,128)(2,1)} %copy-done.3, bf16[864,512]{1,0:T(8,128)(2,1)} %copy-done.2, bf16[512,512]{1,0:T(8,128)(2,1)} %wo_ref.1, f32[1,512]{1,0:T(1,128)} %bitcast.64, bf16[512,1536]{1,0:T(8,128)(2,1)} %wt_ref.1), custom_call_target="tpu_custom_call" | custom-call | tf_op jit(solution)/shard_map/pallas_call | solution.py:230
  129.7 0.0 copy-done.7
  129.7 2.1 %add_convert_fusion = bf16[864,512]{1,0:T(8,128)(2,1)S(1)} fusion(bf16[864,512]{1,0:T(8,128)(2,1)} %get-tuple-element.7, bf16[864,512]{1,0:T(8,128)(2,1)} %get-tuple-element.8, bf16[512,512]{1,0:T(8,128)(2,1)S(1)} %copy-done.7), kind=kOutput, calls=%fused_computation.32 | convolution fusion | flops 454311936 | bytes 3178496 | tf_op jit(solution)/shard_map/dot_general | solution.py:291
  131.8 1.2 reshape.341
  (5 shorter events, 0.1 us)
Async XLA Ops:
  0.0 22.8 %copy-start = (bf16[512,1536]{1,0:T(8,128)(2,1)S(1)}, bf16[512,1536]{1,0:T(8,128)(2,1)}, u32[]{:S(2)}) copy-start(bf16[512,1536]{1,0:T(8,128)(2,1)} %param.13) | copy-start | bytes 4718596
  1.5 7.0 %copy-start.4 = (bf16[27,512]{1,0:T(8,128)(2,1)S(1)}, bf16[27,512]{1,0:T(8,128)(2,1)}, u32[]{:S(2)}) copy-start(bf16[27,512]{1,0:T(8,128)(2,1)} %param.11) | copy-start | bytes 82948
  1.5 7.0 %copy-start.5 = (bf16[512]{0:T(512)(128)(2,1)S(1)}, bf16[512]{0:T(512)(128)(2,1)}, u32[]{:S(2)}) copy-start(bf16[512]{0:T(512)(128)(2,1)} %param.12) | copy-start | bytes 3076
  5.4 3.2 %collective-permute-start = (bf16[1,1,12,12,512]{4,3,2,1,0:T(8,128)(2,1)S(1)}, bf16[1,1,12,12,512]{4,3,2,1,0:T(8,128)(2,1)S(1)}, u32[]{:S(2)}, u32[]{:S(2)}) collective-permute-start(bf16[1,1,12,12,512]{4,3,2,1,0:T(8,128)(2,1)S(1)} %get-tuple-element.11), channel_id=1, source_target_pairs={{0,1},{2,3},{4,5},{6,7},{8,9},{10,11},{12,13},{14,15},{16,17},{18,... | collective-permute-start | bytes 442376 | tf_op jit(solution)/shard_map/ppermute | solution.py:19
  7.2 3.3 %collective-permute-start.1 = (bf16[1,1,12,12,512]{4,3,2,1,0:T(8,128)(2,1)S(1)}, bf16[1,1,12,12,512]{4,3,2,1,0:T(8,128)(2,1)S(1)}, u32[]{:S(2)}, u32[]{:S(2)}) collective-permute-start(bf16[1,1,12,12,512]{4,3,2,1,0:T(8,128)(2,1)S(1)} %get-tuple-element.12), channel_id=1, source_target_pairs={{1,0},{3,2},{5,4},{7,6},{9,8},{11,10},{13,12},{15,14},{17,16},{19,... | collective-permute-start | bytes 442376 | tf_op jit(solution)/shard_map/ppermute | solution.py:22
  22.7 1.7 %copy-start.2 = (bf16[864,512]{1,0:T(8,128)(2,1)}, bf16[864,512]{1,0:T(8,128)(2,1)S(1)}, u32[]{:S(2)}) copy-start(bf16[864,512]{1,0:T(8,128)(2,1)S(1)} %reshape.337.stream_ref) | copy-start | bytes 2654212
  24.5 4.1 %copy-start.1 = (bf16[864,1536]{1,0:T(8,128)(2,1)}, bf16[864,1536]{1,0:T(8,128)(2,1)S(1)}, u32[]{:S(2)}) copy-start(bf16[864,1536]{1,0:T(8,128)(2,1)S(1)} %convolution_convert_fusion.proj_ref) | copy-start | bytes 7962628
  24.5 0.7 copy-start.6
  24.7 3.8 %collective-permute-start.2 = (bf16[864,1024]{1,0:T(8,128)(2,1)S(1)}, bf16[864,1024]{1,0:T(8,128)(2,1)S(1)}, u32[]{:S(2)}, u32[]{:S(2)}) collective-permute-start(bf16[864,1024]{1,0:T(8,128)(2,1)S(1)} %slice_bitcast_fusion), channel_id=1, source_target_pairs={{0,1},{1,0},{2,3},{3,2},{4,5},{5,4},{6,7},{7,6},{8,9},{9,8},{10,11... | collective-permute-start | bytes 5308424 | tf_op jit(solution)/shard_map/ppermute | solution.py:287
  28.5 1.2 copy-start.3
  29.7 100.0 %copy-start.7 = (bf16[512,512]{1,0:T(8,128)(2,1)S(1)}, bf16[512,512]{1,0:T(8,128)(2,1)}, u32[]{:S(2)}) copy-start(bf16[512,512]{1,0:T(8,128)(2,1)} %param.17) | copy-start | bytes 1572868

commit v4 on v3

--- a/solution.py
+++ b/solution.py
@@ -59,6 +59,43 @@
     )
     result = lax.map(one_head, parts)
     return result.transpose(1, 0, 2).reshape(rows, cols)
+
+
+def conv_kernel(e_ref, t_ref, o_ref):
+    planes, rows, lanes_x, width = o_ref.shape
+
+    def plane(z, carry):
+        parts = []
+        for dx in range(3):
+            acc = None
+            for dz in range(3):
+                for dy in range(3):
+                    tap = t_ref[pl.ds(9 * dz + 3 * dy + dx, 1), :]
+                    term = e_ref[z + dz, dy:dy + rows] * tap
+                    acc = term if acc is None else acc + term
+            parts.append(acc)
+        conv = (
+            pltpu.roll(parts[0], 1, 1) + parts[1] + pltpu.roll(parts[2], lanes_x - 1, 1)
+        )
+        o_ref[z] = (e_ref[z + 1, 1:1 + rows] + conv).astype(o_ref.dtype)
+        return carry
+
+    lax.fori_loop(0, planes, plane, 0)
+
+
+def depthwise(ext, taps):
+    depth, grid, _, width = ext.shape
+    planes = depth - 2
+    padded = jnp.pad(ext.astype(jnp.float32), ((0, 0), (1, 1), (1, 3), (0, 0)))
+    vmem = pl.BlockSpec(memory_space=pltpu.VMEM)
+    out = pl.pallas_call(
+        conv_kernel,
+        out_shape=jax.ShapeDtypeStruct((planes, grid, grid + 4, width), jnp.bfloat16),
+        in_specs=[vmem, vmem],
+        out_specs=vmem,
+        compiler_params=pltpu.CompilerParams(vmem_limit_bytes=32 * 1024 * 1024),
+    )(padded, taps.astype(jnp.float32))
+    return out[:, :, 1:1 + grid]
 
 
 def block_kernel(
@@ -267,16 +304,7 @@
     ).astype(jnp.bfloat16)
     embed = embed.reshape(frames, zdev, grid, grid, width)
     padded = extended(embed, (("tok", 1),), 1)
-    padded = jnp.pad(padded, ((0, 0), (0, 0), (1, 1), (1, 1), (0, 0)))
-    conv = jnp.zeros((frames, zdev, grid, grid, width), jnp.float32)
-    for dz in range(3):
-        for dy in range(3):
-            for dx in range(3):
-                tap = conv_taps[9 * dz + 3 * dy + dx].astype(jnp.float32)
-                conv = conv + tap * padded[
-                    :, dz : dz + zdev, dy : dy + grid, dx : dx + grid
-                ].astype(jnp.float32)
-    stream = (embed.astype(jnp.float32) + conv).astype(jnp.bfloat16).reshape(frames, tokens, width)
+    stream = depthwise(padded[0], conv_taps).reshape(frames, tokens, width)
     normed = rms_scale(stream.astype(jnp.float32), gain_space).astype(jnp.bfloat16)
     proj = jnp.dot(normed.reshape(-1, width), qkv_space, preferred_element_type=jnp.float32).astype(
         jnp.bfloat16

time: 133 us -> 130 us (0.977)
  other arithmetic: 11.6 us -> 1.92 us
  Pallas kernels: 100 us -> 105 us
  local copies, waits for them, and re-layouts: 7.1 us -> 8.44 us
    reduce_sum x1, other arithmetic: 9.94 us -> 0.48 us  [rms_scale(): mean_sq = jnp.mean(values * values, axis=-1, keepdims=True)]
    pallas_call x0 -> x1, Pallas kernels: none -> 4.84 us  [depthwise(): pl.pallas_call(conv_kernel, out_shape=jax.ShapeDtypeStruct((planes, grid,...]
  transfers between devices with their start and end apart: 3 -> 3, of which waited for: 2 -> 2; matrix products, arithmetic and copies ran while one was open for 1% -> 0% of each run, Pallas kernels for 0% -> 0%
where the time goes in v4:
time: 130 us
  Pallas kernels  105 us (81%)
  local copies, waits for them, and re-layouts  8.44 us (6%)
  matrix products  6.34 us (5%)
  waiting for transfers between devices  4.94 us (4%)
  starting transfers between devices  3.18 us (2%)
  other arithmetic  1.92 us (1%)
    pallas_call x1, Pallas kernels, block_tail(): pl.pallas_call(functools.partial(block_kernel, chunks), out_shape=(plane,...  100 us
    pallas_call x1, Pallas kernels, depthwise(): pl.pallas_call(conv_kernel, out_shape=jax.ShapeDtypeStruct((planes, grid,...  4.84 us
    ppermute x1, waiting for transfers between devices, local(): lax.ppermute(own_kv, 'tok', [(i, (i + 1) % count) for i in range(count)])  2.96 us
    dot_general x1, matrix products, local(): jnp.dot(normed.reshape(-1, width), qkv_space, preferred_element_type=jnp....  2.75 us
  transfers between devices with their start and end apart: 3, of which 2 were waited for; matrix products, arithmetic and copies ran while one was open for 0% of the time, Pallas kernels for 0%

profile of v4, /device:TPU:24, one launch (start us, length us, event | category | flops | bytes accessed | tf_op | source)
XLA Modules:
  0.0 129.9 jit_solution(8994187512662011477)
XLA Ops:
  0.0 0.0 copy-start
  0.0 0.0 copy-start.6
  0.0 1.5 %reshape.74 = bf16[864,512]{1,0:T(8,128)(2,1)S(1)} reshape(bf16[1,6,12,12,512]{4,3,2,1,0:T(8,128)(2,1)} %param.9) | data formatting | bytes 1769472 | tf_op jit(solution)/shard_map/reshape | solution.py:303
  1.5 0.0 copy-done.6
  1.5 1.5 %convolution_convert_fusion.1 = bf16[864,512]{1,0:T(8,128)(2,1)} fusion(bf16[864,512]{1,0:T(8,128)(2,1)S(1)} %reshape.74, bf16[512,512]{1,0:T(8,128)(2,1)S(1)} %copy-done.6), kind=kOutput, calls=%fused_computation.7 | convolution fusion | flops 453427200 | bytes 2293760 | tf_op jit(solution)/shard_map/dot_general | solution.py:302
  3.1 0.0 copy-start.3
  3.1 0.0 copy-start.4
  3.1 1.3 reshape.75
  4.4 1.8 %collective-permute-start = (bf16[1,1,12,12,512]{4,3,2,1,0:T(8,128)(2,1)S(1)}, bf16[1,1,12,12,512]{4,3,2,1,0:T(8,128)(2,1)S(1)}, u32[]{:S(2)}, u32[]{:S(2)}) collective-permute-start(bf16[1,1,12,12,512]{4,3,2,1,0:T(8,128)(2,1)S(1)} %get-tuple-element.9), channel_id=1, source_target_pairs={{0,1},{2,3},{4,5},{6,7},{8,9},{10,11},{12,13},{14,15},{16,17},{18,... | collective-permute-start | bytes 442376 | tf_op jit(solution)/shard_map/ppermute | solution.py:19
  6.1 1.3 collective-permute-start.1
  7.4 0.0 copy-done.3
  7.5 0.0 copy-done.4
  7.5 0.0 collective-permute-done
  7.5 2.0 %collective-permute-done.1 = bf16[1,1,12,12,512]{4,3,2,1,0:T(8,128)(2,1)S(1)} collective-permute-done((bf16[1,1,12,12,512]{4,3,2,1,0:T(8,128)(2,1)S(1)}, bf16[1,1,12,12,512]{4,3,2,1,0:T(8,128)(2,1)S(1)}, u32[]{:S(2)}, u32[]{:S(2)}) %collective-permute-start.1) | collective-permute-done | bytes 147488 | tf_op jit(solution)/shard_map/ppermute | solution.py:22
  9.5 0.2 maximum_bitcast_fusion
  9.7 0.6 pad_convert_fusion.e_ref
  10.3 4.8 %shard_map.91 = bf16[6,12,16,512]{3,2,1,0:T(8,128)(2,1)S(1)} custom-call(f32[8,14,16,512]{3,2,1,0:T(8,128)S(1)} %pad_convert_fusion.e_ref, f32[27,512]{1,0:T(8,128)S(1)} %convert_element_type.44.t_ref), custom_call_target="tpu_custom_call" | custom-call | tf_op jit(solution)/shard_map/pallas_call | solution.py:91
  15.2 0.5 slice.18
  15.7 0.5 multiply_reduce_fusion
  16.1 1.1 reshape.76.stream_ref
  17.3 0.1 rsqrt.12
  17.4 0.0 copy-done
  17.4 2.8 %convolution_convert_fusion.proj_ref = bf16[864,1536]{1,0:T(8,128)(2,1)S(1)} fusion(bf16[512,1536]{1,0:T(8,128)(2,1)S(1)} %copy-done, bf16[864,512]{1,0:T(8,128)(2,1)} %reshape.76.stream_ref, f32[512]{0:T(512)S(1)} %convert_element_type.47, f32[864]{0:T(1024)S(1)} %rsqrt.12), kind=kOutput, calls=%fused_computation | convolution fusion | flops 1362051072 | bytes 5117312 | tf_op jit(solution)/shard_map/dot_general | solution.py:309
  20.1 0.0 copy-start.1
  20.1 0.0 copy-start.5
  20.2 0.3 slice_bitcast_fusion
  20.4 1.2 copy-done.1
  21.7 0.1 collective-permute-start.2
  21.8 0.0 copy-done.5
  21.8 0.6 reshape.81
  22.4 3.0 %collective-permute-done.2.other_ref = bf16[864,1024]{1,0:T(8,128)(2,1)S(1)} collective-permute-done((bf16[864,1024]{1,0:T(8,128)(2,1)S(1)}, bf16[864,1024]{1,0:T(8,128)(2,1)S(1)}, u32[]{:S(2)}, u32[]{:S(2)}) %collective-permute-start.2) | collective-permute-done | bytes 1769504 | tf_op jit(solution)/shard_map/ppermute | solution.py:315
  25.3 0.0 copy-start.2
  25.3 1.2 copy-done.2
  26.6 0.0 copy-start.7
  26.6 100.0 %shard_map.92 = (bf16[864,512]{1,0:T(8,128)(2,1)}, bf16[864,512]{1,0:T(8,128)(2,1)}) custom-call(bf16[864,1536]{1,0:T(8,128)(2,1)} %copy-done.1, bf16[864,1024]{1,0:T(8,128)(2,1)} %copy-done.2, bf16[864,512]{1,0:T(8,128)(2,1)} %reshape.76.stream_ref, bf16[512,512]{1,0:T(8,128)(2,1)} %wo_ref.1, f32[1,512]{1,0:T(1,128)} %bitcast.12, bf16[512,1536]{1,0:T(8,128)(2,1)} %wt_ref.1), custom_call_target="tpu_custom_call" | custom-call | tf_op jit(solution)/shard_map/pallas_call | solution.py:267
  126.6 0.0 copy-done.7
  126.6 2.1 %add_convert_fusion = bf16[864,512]{1,0:T(8,128)(2,1)S(1)} fusion(bf16[864,512]{1,0:T(8,128)(2,1)} %get-tuple-element.7, bf16[864,512]{1,0:T(8,128)(2,1)} %get-tuple-element.8, bf16[512,512]{1,0:T(8,128)(2,1)S(1)} %copy-done.7), kind=kOutput, calls=%fused_computation.4 | convolution fusion | flops 454311936 | bytes 3178496 | tf_op jit(solution)/shard_map/dot_general | solution.py:319
  128.6 1.2 reshape.80
  (4 shorter events, 0.1 us)
Async XLA Ops:
  0.0 17.4 %copy-start = (bf16[512,1536]{1,0:T(8,128)(2,1)S(1)}, bf16[512,1536]{1,0:T(8,128)(2,1)}, u32[]{:S(2)}) copy-start(bf16[512,1536]{1,0:T(8,128)(2,1)} %param.13) | copy-start | bytes 4718596
  0.0 1.5 %copy-start.6 = (bf16[512,512]{1,0:T(8,128)(2,1)S(1)}, bf16[512,512]{1,0:T(8,128)(2,1)}, u32[]{:S(2)}) copy-start(bf16[512,512]{1,0:T(8,128)(2,1)} %param.10) | copy-start | bytes 1572868
  3.1 4.4 %copy-start.3 = (bf16[27,512]{1,0:T(8,128)(2,1)S(1)}, bf16[27,512]{1,0:T(8,128)(2,1)}, u32[]{:S(2)}) copy-start(bf16[27,512]{1,0:T(8,128)(2,1)} %param.11) | copy-start | bytes 82948
  3.1 4.4 %copy-start.4 = (bf16[512]{0:T(512)(128)(2,1)S(1)}, bf16[512]{0:T(512)(128)(2,1)}, u32[]{:S(2)}) copy-start(bf16[512]{0:T(512)(128)(2,1)} %param.12) | copy-start | bytes 3076
  4.4 3.1 %collective-permute-start = (bf16[1,1,12,12,512]{4,3,2,1,0:T(8,128)(2,1)S(1)}, bf16[1,1,12,12,512]{4,3,2,1,0:T(8,128)(2,1)S(1)}, u32[]{:S(2)}, u32[]{:S(2)}) collective-permute-start(bf16[1,1,12,12,512]{4,3,2,1,0:T(8,128)(2,1)S(1)} %get-tuple-element.9), channel_id=1, source_target_pairs={{0,1},{2,3},{4,5},{6,7},{8,9},{10,11},{12,13},{14,15},{16,17},{18,... | collective-permute-start | bytes 442376 | tf_op jit(solution)/shard_map/ppermute | solution.py:19
  6.1 3.3 %collective-permute-start.1 = (bf16[1,1,12,12,512]{4,3,2,1,0:T(8,128)(2,1)S(1)}, bf16[1,1,12,12,512]{4,3,2,1,0:T(8,128)(2,1)S(1)}, u32[]{:S(2)}, u32[]{:S(2)}) collective-permute-start(bf16[1,1,12,12,512]{4,3,2,1,0:T(8,128)(2,1)S(1)} %get-tuple-element.10), channel_id=1, source_target_pairs={{1,0},{3,2},{5,4},{7,6},{9,8},{11,10},{13,12},{15,14},{17,16},{19,... | collective-permute-start | bytes 442376 | tf_op jit(solution)/shard_map/ppermute | solution.py:22
  20.1 1.5 %copy-start.1 = (bf16[864,1536]{1,0:T(8,128)(2,1)}, bf16[864,1536]{1,0:T(8,128)(2,1)S(1)}, u32[]{:S(2)}) copy-start(bf16[864,1536]{1,0:T(8,128)(2,1)S(1)} %convolution_convert_fusion.proj_ref) | copy-start | bytes 7962628
  20.1 1.7 %copy-start.5 = (bf16[512]{0:T(512)(128)(2,1)S(1)}, bf16[512]{0:T(512)(128)(2,1)}, u32[]{:S(2)}) copy-start(bf16[512]{0:T(512)(128)(2,1)} %param.15) | copy-start | bytes 3076
  21.7 3.7 %collective-permute-start.2 = (bf16[864,1024]{1,0:T(8,128)(2,1)S(1)}, bf16[864,1024]{1,0:T(8,128)(2,1)S(1)}, u32[]{:S(2)}, u32[]{:S(2)}) collective-permute-start(bf16[864,1024]{1,0:T(8,128)(2,1)S(1)} %slice_bitcast_fusion), channel_id=1, source_target_pairs={{0,1},{1,0},{2,3},{3,2},{4,5},{5,4},{6,7},{7,6},{8,9},{9,8},{10,11... | collective-permute-start | bytes 5308424 | tf_op jit(solution)/shard_map/ppermute | solution.py:315
  25.3 1.2 copy-start.2
  26.6 100.0 %copy-start.7 = (bf16[512,512]{1,0:T(8,128)(2,1)S(1)}, bf16[512,512]{1,0:T(8,128)(2,1)}, u32[]{:S(2)}) copy-start(bf16[512,512]{1,0:T(8,128)(2,1)} %param.17) | copy-start | bytes 1572868

commit v5 on v4

--- a/solution.py
+++ b/solution.py
@@ -99,7 +99,7 @@
 
 
 def block_kernel(
-    chunks, proj_ref, other_ref, stream_ref, wo_ref, gain_ref, wt_ref,
+    chunks, q_ref, kv_ref, other_ref, stream_ref, wo_ref, gain_ref, wt_ref,
     out_ref, stream2_ref, own, query2, hist, mixed, total, sum_ref, send_sem, recv_sem,
 ):
     me = lax.axis_index("tm")
@@ -183,11 +183,10 @@
         pieces = []
         for pair in range(width // lanes):
             cols = slice(pair * lanes, (pair + 1) * lanes)
-            q = proj_ref[span, cols]
+            q = q_ref[span, cols]
             key_cols = slice(width + pair * lanes, width + (pair + 1) * lanes)
-            value_cols = slice(2 * width + pair * lanes, 2 * width + (pair + 1) * lanes)
             sources = (
-                (proj_ref[:, key_cols], proj_ref[:, value_cols]),
+                (kv_ref[:, cols], kv_ref[:, key_cols]),
                 (other_ref[:, cols], other_ref[:, key_cols]),
             )
             outs = []
@@ -259,7 +258,7 @@
     out_ref[...] = (mixed[...] / total[...]).astype(out_ref.dtype)
 
 
-def block_tail(proj, other, stream, out_space, gain_time, qkv_time, chunks=6):
+def block_tail(query, keys_values, other, stream, out_space, gain_time, qkv_time, chunks=6):
     rows, width = stream.shape
     gain = gain_time.astype(jnp.float32).reshape(1, width)
     vmem = pl.BlockSpec(memory_space=pltpu.VMEM)
@@ -267,7 +266,7 @@
     return pl.pallas_call(
         functools.partial(block_kernel, chunks),
         out_shape=(plane, plane),
-        in_specs=[vmem] * 6,
+        in_specs=[vmem] * 7,
         out_specs=(vmem, vmem),
         scratch_shapes=[
             pltpu.VMEM((rows, width), jnp.bfloat16),
@@ -282,7 +281,7 @@
         compiler_params=pltpu.CompilerParams(
             collective_id=0, has_side_effects=True, vmem_limit_bytes=56 * 1024 * 1024
         ),
-    )(proj, other, stream, out_space, gain, qkv_time)
+    )(query, keys_values, other, stream, out_space, gain, qkv_time)
 
 
 def local(
@@ -299,22 +298,23 @@
     frames, zdev, grid, _, patch = patches.shape
     width = patch_weight.shape[1]
     tokens = zdev * grid * grid
-    embed = jnp.dot(
-        patches.reshape(-1, patch), patch_weight, preferred_element_type=jnp.float32
-    ).astype(jnp.bfloat16)
-    embed = embed.reshape(frames, zdev, grid, grid, width)
+    embed = jnp.dot(patches, patch_weight, preferred_element_type=jnp.float32).astype(
+        jnp.bfloat16
+    )
     padded = extended(embed, (("tok", 1),), 1)
     stream = depthwise(padded[0], conv_taps).reshape(frames, tokens, width)
     normed = rms_scale(stream.astype(jnp.float32), gain_space).astype(jnp.bfloat16)
-    proj = jnp.dot(normed.reshape(-1, width), qkv_space, preferred_element_type=jnp.float32).astype(
+    flat = normed.reshape(-1, width)
+    own_kv = jnp.dot(flat, qkv_space[:, width:], preferred_element_type=jnp.float32).astype(
         jnp.bfloat16
     )
-    proj = proj.reshape(frames, tokens, 3 * width)
-    own_kv = proj[0, :, width:]
     count = lax.axis_size("tok")
     other_kv = lax.ppermute(own_kv, "tok", [(i, (i + 1) % count) for i in range(count)])
+    query = jnp.dot(flat, qkv_space[:, :width], preferred_element_type=jnp.float32).astype(
+        jnp.bfloat16
+    )
     temporal, stream2 = block_tail(
-        proj[0], other_kv, stream.reshape(-1, width), out_space, gain_time, qkv_time
+        query, own_kv, other_kv, stream.reshape(-1, width), out_space, gain_time, qkv_time
     )
     time_proj = jnp.dot(
         temporal.reshape(-1, width), out_time, preferred_element_type=jnp.float32

time: 130 us -> 127 us (0.977)
  local copies, waits for them, and re-layouts: 8.44 us -> 4.53 us
  waiting for transfers between devices: 4.94 us -> 2.07 us
  matrix products: 6.34 us -> 9.09 us
    ppermute x1, waiting for transfers between devices: 2.96 us -> 0.09 us  [local(): lax.ppermute(own_kv, 'tok', [(i, (i + 1) % count) for i in range(count)])]
    reshape x2 -> x0, local copies, waits for them, and re-layouts: 2.77 us -> none  [the longest x1 1.5 us: local(): patches.reshape(-1, patch)]
    dot_general x2 -> x3, matrix products: 4.29 us -> 7.04 us  [the longest x1 2.66 us: local(): jnp.dot(flat, qkv_space[:, :width], preferred_element_type=jnp.float32)]
  transfers between devices with their start and end apart: 3 -> 3, of which waited for: 2 -> 2; matrix products, arithmetic and copies ran while one was open for 0% -> 3% of each run, Pallas kernels for 0% -> 0%
where the time goes in v5:
time: 127 us
  Pallas kernels  105 us (83%)
  matrix products  9.09 us (7%)
  local copies, waits for them, and re-layouts  4.53 us (4%)
  starting transfers between devices  3.27 us (3%)
  other arithmetic  2.12 us (2%)
  waiting for transfers between devices  2.07 us (2%)
    pallas_call x1, Pallas kernels, block_tail(): pl.pallas_call(functools.partial(block_kernel, chunks), out_shape=(plane,...  100 us
    pallas_call x1, Pallas kernels, depthwise(): pl.pallas_call(conv_kernel, out_shape=jax.ShapeDtypeStruct((planes, grid,...  4.84 us
    dot_general x1, matrix products, local(): jnp.dot(flat, qkv_space[:, :width], preferred_element_type=jnp.float32)  2.66 us
    dot_general x1, matrix products, local(): jnp.dot(flat, qkv_space[:, width:], preferred_element_type=jnp.float32)  2.57 us
  transfers between devices with their start and end apart: 3, of which 2 were waited for; matrix products, arithmetic and copies ran while one was open for 3% of the time, Pallas kernels for 0%

profile of v5, /device:TPU:24, one launch (start us, length us, event | category | flops | bytes accessed | tf_op | source)
XLA Modules:
  0.0 126.5 jit_solution(1975895306428150619)
XLA Ops:
  0.0 0.0 copy-start
  0.0 0.0 copy-start.5
  0.0 0.0 copy-start.4
  0.0 1.3 copy-done
  1.3 1.8 %fusion = bf16[1,6,12,12,512]{4,3,2,1,0:T(8,128)(2,1)S(1)} fusion(bf16[1,6,12,12,512]{4,3,2,1,0:T(8,128)(2,1)S(1)} %copy-done, bf16[512,512]{1,0:T(8,128)(2,1)} %param.10), kind=kOutput, calls=%fused_computation.8 | convolution fusion | flops 453427200 | bytes 2293760 | tf_op jit(solution)/shard_map/dot_general | solution.py:301
  3.1 1.8 %collective-permute-start = (bf16[1,1,12,12,512]{4,3,2,1,0:T(8,128)(2,1)S(1)}, bf16[1,1,12,12,512]{4,3,2,1,0:T(8,128)(2,1)S(1)}, u32[]{:S(2)}, u32[]{:S(2)}) collective-permute-start(bf16[1,1,12,12,512]{4,3,2,1,0:T(8,128)(2,1)S(1)} %get-tuple-element.9), channel_id=1, source_target_pairs={{0,1},{2,3},{4,5},{6,7},{8,9},{10,11},{12,13},{14,15},{16,17},{18,... | collective-permute-start | bytes 442376 | tf_op jit(solution)/shard_map/ppermute | solution.py:19
  4.9 1.3 %collective-permute-start.1 = (bf16[1,1,12,12,512]{4,3,2,1,0:T(8,128)(2,1)S(1)}, bf16[1,1,12,12,512]{4,3,2,1,0:T(8,128)(2,1)S(1)}, u32[]{:S(2)}, u32[]{:S(2)}) collective-permute-start(bf16[1,1,12,12,512]{4,3,2,1,0:T(8,128)(2,1)S(1)} %get-tuple-element.10), channel_id=1, source_target_pairs={{1,0},{3,2},{5,4},{7,6},{9,8},{11,10},{13,12},{15,14},{17,16},{19,... | collective-permute-start | bytes 442376 | tf_op jit(solution)/shard_map/ppermute | solution.py:22
  6.2 0.0 copy-done.5
  6.2 0.0 copy-done.4
  6.2 0.0 collective-permute-done
  6.2 2.0 %collective-permute-done.1 = bf16[1,1,12,12,512]{4,3,2,1,0:T(8,128)(2,1)S(1)} collective-permute-done((bf16[1,1,12,12,512]{4,3,2,1,0:T(8,128)(2,1)S(1)}, bf16[1,1,12,12,512]{4,3,2,1,0:T(8,128)(2,1)S(1)}, u32[]{:S(2)}, u32[]{:S(2)}) %collective-permute-start.1) | collective-permute-done | bytes 147488 | tf_op jit(solution)/shard_map/ppermute | solution.py:22
  8.2 0.2 maximum_bitcast_fusion
  8.5 0.6 pad_convert_fusion.e_ref
  9.1 4.8 %shard_map.91 = bf16[6,12,16,512]{3,2,1,0:T(8,128)(2,1)S(1)} custom-call(f32[8,14,16,512]{3,2,1,0:T(8,128)S(1)} %pad_convert_fusion.e_ref, f32[27,512]{1,0:T(8,128)S(1)} %convert_element_type.51.t_ref), custom_call_target="tpu_custom_call" | custom-call | tf_op jit(solution)/shard_map/pallas_call | solution.py:91
  13.9 0.5 multiply_reduce_fusion
  14.4 0.5 slice.22
  14.9 0.2 reshape.71.stream_ref
  15.1 0.0 copy-start.1
  15.1 0.1 rsqrt.12
  15.2 0.0 copy-start.6
  15.2 2.6 %convolution_convert_fusion.kv_ref = bf16[864,1024]{1,0:T(8,128)(2,1)S(1)} fusion(bf16[512,1536]{1,0:T(8,128)(2,1)} %param.13, bf16[864,512]{1,0:T(8,128)(2,1)S(1)} %reshape.71.stream_ref, f32[512]{0:T(512)S(1)} %convert_element_type.54, f32[864]{0:T(1024)S(1)} %rsqrt.12), kind=kOutput, calls=%fused_computation.4 | convolution fusion | flops 908623872 | bytes 3708288 | tf_op jit(solution)/shard_map/dot_general | solution.py:308
  17.8 0.0 copy-start.2
  17.8 0.2 collective-permute-start.2
  18.0 0.0 copy-done.6
  18.0 0.8 reshape.75
  18.8 0.0 copy-done.1
  18.8 2.7 %convolution_convert_fusion.2.q_ref = bf16[864,512]{1,0:T(8,128)(2,1)} fusion(bf16[512,1536]{1,0:T(8,128)(2,1)} %param.13, bf16[864,512]{1,0:T(8,128)(2,1)S(1)} %reshape.71.stream_ref, f32[512]{0:T(512)S(1)} %convert_element_type.54, f32[864]{0:T(1024)S(1)} %rsqrt.12), kind=kOutput, calls=%fused_computation.7 | convolution fusion | flops 455196672 | bytes 2299264 | tf_op jit(solution)/shard_map/dot_general | solution.py:313
  21.5 0.0 copy-done.2
  21.5 0.1 collective-permute-done.2.other_ref
  21.6 0.0 copy-start.3
  21.6 1.2 copy-done.3
  22.8 0.0 copy-start.7
  22.8 100.5 %shard_map.92 = (bf16[864,512]{1,0:T(8,128)(2,1)}, bf16[864,512]{1,0:T(8,128)(2,1)}) custom-call(bf16[864,512]{1,0:T(8,128)(2,1)} %convolution_convert_fusion.2.q_ref, bf16[864,1024]{1,0:T(8,128)(2,1)} %copy-done.2, bf16[864,1024]{1,0:T(8,128)(2,1)} %copy-done.3, bf16[864,512]{1,0:T(8,128)(2,1)} %copy-done.1, bf16[512,512]{1,0:T(8,128)(2,1)} %wo_ref.1, ...), custom_call_target="tpu_custom_call" | custom-call | tf_op jit(solution)/shard_map/pallas_call | solution.py:266
  123.3 0.0 copy-done.7
  123.3 2.1 %add_convert_fusion = bf16[864,512]{1,0:T(8,128)(2,1)S(1)} fusion(bf16[864,512]{1,0:T(8,128)(2,1)} %get-tuple-element.7, bf16[864,512]{1,0:T(8,128)(2,1)} %get-tuple-element.8, bf16[512,512]{1,0:T(8,128)(2,1)S(1)} %copy-done.7), kind=kOutput, calls=%fused_computation.2 | convolution fusion | flops 454311936 | bytes 3178496 | tf_op jit(solution)/shard_map/dot_general | solution.py:319
  125.3 1.2 reshape.74
  (4 shorter events, 0.1 us)
Async XLA Ops:
  0.0 1.3 %copy-start = (bf16[1,6,12,12,512]{4,3,2,1,0:T(8,128)(2,1)S(1)}, bf16[1,6,12,12,512]{4,3,2,1,0:T(8,128)(2,1)}, u32[]{:S(2)}) copy-start(bf16[1,6,12,12,512]{4,3,2,1,0:T(8,128)(2,1)} %param.9) | copy-start | bytes 2654212
  0.0 6.2 %copy-start.5 = (bf16[512]{0:T(512)(128)(2,1)S(1)}, bf16[512]{0:T(512)(128)(2,1)}, u32[]{:S(2)}) copy-start(bf16[512]{0:T(512)(128)(2,1)} %param.12) | copy-start | bytes 3076
  0.0 6.2 %copy-start.4 = (bf16[27,512]{1,0:T(8,128)(2,1)S(1)}, bf16[27,512]{1,0:T(8,128)(2,1)}, u32[]{:S(2)}) copy-start(bf16[27,512]{1,0:T(8,128)(2,1)} %param.11) | copy-start | bytes 82948
  3.1 3.1 %collective-permute-start = (bf16[1,1,12,12,512]{4,3,2,1,0:T(8,128)(2,1)S(1)}, bf16[1,1,12,12,512]{4,3,2,1,0:T(8,128)(2,1)S(1)}, u32[]{:S(2)}, u32[]{:S(2)}) collective-permute-start(bf16[1,1,12,12,512]{4,3,2,1,0:T(8,128)(2,1)S(1)} %get-tuple-element.9), channel_id=1, source_target_pairs={{0,1},{2,3},{4,5},{6,7},{8,9},{10,11},{12,13},{14,15},{16,17},{18,... | collective-permute-start | bytes 442376 | tf_op jit(solution)/shard_map/ppermute | solution.py:19
  4.9 3.3 %collective-permute-start.1 = (bf16[1,1,12,12,512]{4,3,2,1,0:T(8,128)(2,1)S(1)}, bf16[1,1,12,12,512]{4,3,2,1,0:T(8,128)(2,1)S(1)}, u32[]{:S(2)}, u32[]{:S(2)}) collective-permute-start(bf16[1,1,12,12,512]{4,3,2,1,0:T(8,128)(2,1)S(1)} %get-tuple-element.10), channel_id=1, source_target_pairs={{1,0},{3,2},{5,4},{7,6},{9,8},{11,10},{13,12},{15,14},{17,16},{19,... | collective-permute-start | bytes 442376 | tf_op jit(solution)/shard_map/ppermute | solution.py:22
  15.1 3.8 %copy-start.1 = (bf16[864,512]{1,0:T(8,128)(2,1)}, bf16[864,512]{1,0:T(8,128)(2,1)S(1)}, u32[]{:S(2)}) copy-start(bf16[864,512]{1,0:T(8,128)(2,1)S(1)} %reshape.71.stream_ref) | copy-start | bytes 2654212
  15.2 2.8 %copy-start.6 = (bf16[512]{0:T(512)(128)(2,1)S(1)}, bf16[512]{0:T(512)(128)(2,1)}, u32[]{:S(2)}) copy-start(bf16[512]{0:T(512)(128)(2,1)} %param.15) | copy-start | bytes 3076
  17.8 3.7 %copy-start.2 = (bf16[864,1024]{1,0:T(8,128)(2,1)}, bf16[864,1024]{1,0:T(8,128)(2,1)S(1)}, u32[]{:S(2)}) copy-start(bf16[864,1024]{1,0:T(8,128)(2,1)S(1)} %convolution_convert_fusion.kv_ref) | copy-start | bytes 5308420
  17.8 3.8 %collective-permute-start.2 = (bf16[864,1024]{1,0:T(8,128)(2,1)S(1)}, bf16[864,1024]{1,0:T(8,128)(2,1)S(1)}, u32[]{:S(2)}, u32[]{:S(2)}) collective-permute-start(bf16[864,1024]{1,0:T(8,128)(2,1)S(1)} %convolution_convert_fusion.kv_ref), channel_id=1, source_target_pairs={{0,1},{1,0},{2,3},{3,2},{4,5},{5,4},{6,7},{7,6},{8,9},{9,8},{10,11... | collective-permute-start | bytes 5308424 | tf_op jit(solution)/shard_map/ppermute | solution.py:312
  21.6 1.2 copy-start.3
  22.8 100.5 %copy-start.7 = (bf16[512,512]{1,0:T(8,128)(2,1)S(1)}, bf16[512,512]{1,0:T(8,128)(2,1)}, u32[]{:S(2)}) copy-start(bf16[512,512]{1,0:T(8,128)(2,1)} %param.17) | copy-start | bytes 1572868

commit v6 on v5

--- a/solution.py
+++ b/solution.py
@@ -99,7 +99,7 @@
 
 
 def block_kernel(
-    chunks, q_ref, kv_ref, other_ref, stream_ref, wo_ref, gain_ref, wt_ref,
+    chunks, ws_ref, gain_s_ref, kv_ref, other_ref, stream_ref, wo_ref, gain_ref, wt_ref,
     out_ref, stream2_ref, own, query2, hist, mixed, total, sum_ref, send_sem, recv_sem,
 ):
     me = lax.axis_index("tm")
@@ -181,9 +181,15 @@
     def space_step(piece, carry):
         span = span_of(piece)
         pieces = []
+        current = stream_ref[span, :].astype(jnp.float32)
+        mean_cur = jnp.mean(current * current, axis=-1, keepdims=True)
+        normed = (current * lax.rsqrt(mean_cur + 1e-06) * gain_s_ref[...]).astype(jnp.bfloat16)
+        query_s = jnp.dot(normed, ws_ref[...], preferred_element_type=jnp.float32).astype(
+            jnp.bfloat16
+        )
         for pair in range(width // lanes):
             cols = slice(pair * lanes, (pair + 1) * lanes)
-            q = q_ref[span, cols]
+            q = query_s[:, cols]
             key_cols = slice(width + pair * lanes, width + (pair + 1) * lanes)
             sources = (
                 (kv_ref[:, cols], kv_ref[:, key_cols]),
@@ -258,15 +264,16 @@
     out_ref[...] = (mixed[...] / total[...]).astype(out_ref.dtype)
 
 
-def block_tail(query, keys_values, other, stream, out_space, gain_time, qkv_time, chunks=6):
+def block_tail(q_weight, gain_space, keys_values, other, stream, out_space, gain_time, qkv_time, chunks=6):
     rows, width = stream.shape
     gain = gain_time.astype(jnp.float32).reshape(1, width)
+    gain_s = gain_space.astype(jnp.float32).reshape(1, width)
     vmem = pl.BlockSpec(memory_space=pltpu.VMEM)
     plane = jax.ShapeDtypeStruct((rows, width), jnp.bfloat16)
     return pl.pallas_call(
         functools.partial(block_kernel, chunks),
         out_shape=(plane, plane),
-        in_specs=[vmem] * 7,
+        in_specs=[vmem] * 8,
         out_specs=(vmem, vmem),
         scratch_shapes=[
             pltpu.VMEM((rows, width), jnp.bfloat16),
@@ -281,7 +288,7 @@
         compiler_params=pltpu.CompilerParams(
             collective_id=0, has_side_effects=True, vmem_limit_bytes=56 * 1024 * 1024
         ),
-    )(query, keys_values, other, stream, out_space, gain, qkv_time)
+    )(q_weight, gain_s, keys_values, other, stream, out_space, gain, qkv_time)
 
 
 def local(
@@ -298,10 +305,15 @@
     frames, zdev, grid, _, patch = patches.shape
     width = patch_weight.shape[1]
     tokens = zdev * grid * grid
+    ends = extended(patches, (("tok", 1),), 1)
     embed = jnp.dot(patches, patch_weight, preferred_element_type=jnp.float32).astype(
         jnp.bfloat16
     )
-    padded = extended(embed, (("tok", 1),), 1)
+    low = jnp.dot(ends[:, :1], patch_weight, preferred_element_type=jnp.float32)
+    high = jnp.dot(ends[:, -1:], patch_weight, preferred_element_type=jnp.float32)
+    padded = jnp.concatenate(
+        [low.astype(jnp.bfloat16), embed, high.astype(jnp.bfloat16)], axis=1
+    )
     stream = depthwise(padded[0], conv_taps).reshape(frames, tokens, width)
     normed = rms_scale(stream.astype(jnp.float32), gain_space).astype(jnp.bfloat16)
     flat = normed.reshape(-1, width)
@@ -310,11 +322,9 @@
     )
     count = lax.axis_size("tok")
     other_kv = lax.ppermute(own_kv, "tok", [(i, (i + 1) % count) for i in range(count)])
-    query = jnp.dot(flat, qkv_space[:, :width], preferred_element_type=jnp.float32).astype(
-        jnp.bfloat16
-    )
     temporal, stream2 = block_tail(
-        query, own_kv, other_kv, stream.reshape(-1, width), out_space, gain_time, qkv_time
+        qkv_space[:, :width], gain_space, own_kv, other_kv, stream.reshape(-1, width),
+        out_space, gain_time, qkv_time,
     )
     time_proj = jnp.dot(
         temporal.reshape(-1, width), out_time, preferred_element_type=jnp.float32

time: 127 us -> 129 us (1.016)
  Pallas kernels: 105 us -> 107 us
  matrix products: 9.09 us -> 7.17 us
  local copies, waits for them, and re-layouts: 4.53 us -> 6.23 us
    dot_general x1 -> x2, matrix products: 2.66 us -> 0.53 us  [the longest x1 0.26 us: local(): low = jnp.dot(ends[:, :1], patch_weight, preferred_element_type=jnp.float32)]
    ppermute x1, waiting for transfers between devices: 1.98 us -> 0.01 us  [extended(): lax.ppermute(lax.slice_in_dim(block, 0, width, axis=dim), axis, backward)]
    slice x0 -> x1, local copies, waits for them, and re-layouts: none -> 1.91 us  [local(): qkv_space[:, :width]]
    pallas_call x1, Pallas kernels: 100 us -> 102 us  [block_tail(): pl.pallas_call(functools.partial(block_kernel, chunks), out_shape=(plane,...]
  transfers between devices with their start and end apart: 3 -> 3, of which waited for: 2 -> 1; matrix products, arithmetic and copies ran while one was open for 3% -> 5% of each run, Pallas kernels for 0% -> 0%
where the time goes in v6:
time: 129 us
  Pallas kernels  107 us (83%)
  matrix products  7.17 us (6%)
  local copies, waits for them, and re-layouts  6.23 us (5%)
  starting transfers between devices  4.26 us (3%)
  other arithmetic  3.35 us (3%)
    pallas_call x1, Pallas kernels, block_tail(): pl.pallas_call(functools.partial(block_kernel, chunks), out_shape=(plane,...  102 us
    pallas_call x1, Pallas kernels, depthwise(): pl.pallas_call(conv_kernel, out_shape=jax.ShapeDtypeStruct((planes, grid,...  4.84 us
  transfers between devices with their start and end apart: 3, of which 1 were waited for; matrix products, arithmetic and copies ran while one was open for 5% of the time, Pallas kernels for 0%

profile of v6, /device:TPU:24, one launch (start us, length us, event | category | flops | bytes accessed | tf_op | source)
XLA Modules:
  0.0 128.9 jit_solution(13679866698248286411)
XLA Ops:
  0.0 0.0 copy-start
  0.0 1.1 fusion.12
  1.1 1.8 %collective-permute-start = (bf16[1,1,12,12,512]{4,3,2,1,0:T(8,128)(2,1)S(1)}, bf16[1,1,12,12,512]{4,3,2,1,0:T(8,128)(2,1)S(1)}, u32[]{:S(2)}, u32[]{:S(2)}) collective-permute-start(bf16[1,1,12,12,512]{4,3,2,1,0:T(8,128)(2,1)S(1)} %get-tuple-element.9), channel_id=1, source_target_pairs={{0,1},{2,3},{4,5},{6,7},{8,9},{10,11},{12,13},{14,15},{16,17},{18,... | collective-permute-start | bytes 442376 | tf_op jit(solution)/shard_map/ppermute | solution.py:19
  2.9 1.3 %collective-permute-start.1 = (bf16[1,1,12,12,512]{4,3,2,1,0:T(8,128)(2,1)S(1)}, bf16[1,1,12,12,512]{4,3,2,1,0:T(8,128)(2,1)S(1)}, u32[]{:S(2)}, u32[]{:S(2)}) collective-permute-start(bf16[1,1,12,12,512]{4,3,2,1,0:T(8,128)(2,1)S(1)} %get-tuple-element.10), channel_id=1, source_target_pairs={{1,0},{3,2},{5,4},{7,6},{9,8},{11,10},{13,12},{15,14},{17,16},{19,... | collective-permute-start | bytes 442376 | tf_op jit(solution)/shard_map/ppermute | solution.py:22
  4.2 0.7 convert_element_type.58
  4.9 0.0 copy-start.4
  4.9 0.8 convert_element_type.66.t_ref
  5.6 0.0 copy-done
  5.6 2.0 %fusion = bf16[1,6,12,12,512]{4,3,2,1,0:T(8,128)(2,1)S(1)} fusion(bf16[1,6,12,12,512]{4,3,2,1,0:T(8,128)(2,1)} %param.9, bf16[512,512]{1,0:T(8,128)(2,1)S(1)} %copy-done), kind=kOutput, calls=%fused_computation.7 | convolution fusion | flops 453427200 | bytes 2293760 | tf_op jit(solution)/shard_map/dot_general | solution.py:309
  7.7 0.0 collective-permute-done
  7.7 0.3 fusion.2
  8.0 0.0 collective-permute-done.1
  8.0 0.3 fusion.3
  8.2 0.2 maximum_bitcast_fusion
  8.5 0.6 pad_convert_fusion.e_ref
  9.1 4.8 %shard_map.91 = bf16[6,12,16,512]{3,2,1,0:T(8,128)(2,1)S(1)} custom-call(f32[8,14,16,512]{3,2,1,0:T(8,128)S(1)} %pad_convert_fusion.e_ref, f32[27,512]{1,0:T(8,128)S(1)} %convert_element_type.66.t_ref), custom_call_target="tpu_custom_call" | custom-call | tf_op jit(solution)/shard_map/pallas_call | solution.py:91
  13.9 0.5 multiply_reduce_fusion
  14.4 0.5 slice.20
  14.9 0.2 reshape.87.stream_ref
  15.1 0.0 copy-start.1
  15.1 0.1 rsqrt.12
  15.2 0.0 copy-done.4
  15.2 0.0 copy-start.5
  15.3 2.5 %convolution_convert_fusion.kv_ref = bf16[864,1024]{1,0:T(8,128)(2,1)S(1)} fusion(bf16[512,1536]{1,0:T(8,128)(2,1)} %param.13, bf16[864,512]{1,0:T(8,128)(2,1)S(1)} %reshape.87.stream_ref, f32[512]{0:T(512)S(1)} %convert_element_type.58, f32[864]{0:T(1024)S(1)} %rsqrt.12), kind=kOutput, calls=%fused_computation.4 | convolution fusion | flops 908623872 | bytes 3708288 | tf_op jit(solution)/shard_map/dot_general | solution.py:320
  17.8 0.0 copy-done.1
  17.8 0.0 copy-start.2
  17.8 1.2 collective-permute-start.2
  19.0 1.9 %slice.15.ws_ref = bf16[512,512]{1,0:T(8,128)(2,1)} slice(bf16[512,1536]{1,0:T(8,128)(2,1)} %param.13), slice={[0:512], [0:512]} | slice | bytes 1048576 | tf_op jit(solution)/shard_map/slice | solution.py:326
  21.0 0.0 copy-done.5
  21.0 0.6 reshape.91
  21.6 0.8 collective-permute-done.2.other_ref
  22.4 0.0 copy-start.3
  22.4 0.0 copy-done.2
  22.4 1.2 copy-done.3
  23.6 0.0 copy-start.6
  23.6 102.0 %shard_map.92 = (bf16[864,512]{1,0:T(8,128)(2,1)}, bf16[864,512]{1,0:T(8,128)(2,1)}) custom-call(bf16[512,512]{1,0:T(8,128)(2,1)} %slice.15.ws_ref, f32[1,512]{1,0:T(1,128)} %bitcast.31, bf16[864,1024]{1,0:T(8,128)(2,1)} %copy-done.2, bf16[864,1024]{1,0:T(8,128)(2,1)} %copy-done.3, bf16[864,512]{1,0:T(8,128)(2,1)} %copy-done.1, bf16[512,512]{1,0:T(8,128)(2,1)} %wo_ref.1, ...), custom_call_target="tpu_custom_call" | custom-call | tf_op jit(solution)/shard_map/pallas_call | solution.py:273
  125.6 0.0 copy-done.6
  125.6 2.1 %add_convert_fusion = bf16[864,512]{1,0:T(8,128)(2,1)S(1)} fusion(bf16[864,512]{1,0:T(8,128)(2,1)} %get-tuple-element.7, bf16[864,512]{1,0:T(8,128)(2,1)} %get-tuple-element.8, bf16[512,512]{1,0:T(8,128)(2,1)S(1)} %copy-done.6), kind=kOutput, calls=%fused_computation.2 | convolution fusion | flops 454311936 | bytes 3178496 | tf_op jit(solution)/shard_map/dot_general | solution.py:329
  127.7 1.2 reshape.90
  (1 shorter events, 0.0 us)
Async XLA Ops:
  0.0 5.6 %copy-start = (bf16[512,512]{1,0:T(8,128)(2,1)S(1)}, bf16[512,512]{1,0:T(8,128)(2,1)}, u32[]{:S(2)}) copy-start(bf16[512,512]{1,0:T(8,128)(2,1)} %param.10) | copy-start | bytes 1572868
  1.1 6.6 %collective-permute-start = (bf16[1,1,12,12,512]{4,3,2,1,0:T(8,128)(2,1)S(1)}, bf16[1,1,12,12,512]{4,3,2,1,0:T(8,128)(2,1)S(1)}, u32[]{:S(2)}, u32[]{:S(2)}) collective-permute-start(bf16[1,1,12,12,512]{4,3,2,1,0:T(8,128)(2,1)S(1)} %get-tuple-element.9), channel_id=1, source_target_pairs={{0,1},{2,3},{4,5},{6,7},{8,9},{10,11},{12,13},{14,15},{16,17},{18,... | collective-permute-start | bytes 442376 | tf_op jit(solution)/shard_map/ppermute | solution.py:19
  2.9 5.1 %collective-permute-start.1 = (bf16[1,1,12,12,512]{4,3,2,1,0:T(8,128)(2,1)S(1)}, bf16[1,1,12,12,512]{4,3,2,1,0:T(8,128)(2,1)S(1)}, u32[]{:S(2)}, u32[]{:S(2)}) collective-permute-start(bf16[1,1,12,12,512]{4,3,2,1,0:T(8,128)(2,1)S(1)} %get-tuple-element.10), channel_id=1, source_target_pairs={{1,0},{3,2},{5,4},{7,6},{9,8},{11,10},{13,12},{15,14},{17,16},{19,... | collective-permute-start | bytes 442376 | tf_op jit(solution)/shard_map/ppermute | solution.py:22
  4.9 10.4 %copy-start.4 = (f32[512]{0:T(512)}, f32[512]{0:T(512)S(1)}, u32[]{:S(2)}) copy-start(f32[512]{0:T(512)S(1)} %convert_element_type.58) | copy-start | bytes 6148
  15.1 2.7 %copy-start.1 = (bf16[864,512]{1,0:T(8,128)(2,1)}, bf16[864,512]{1,0:T(8,128)(2,1)S(1)}, u32[]{:S(2)}) copy-start(bf16[864,512]{1,0:T(8,128)(2,1)S(1)} %reshape.87.stream_ref) | copy-start | bytes 2654212
  15.2 5.7 %copy-start.5 = (bf16[512]{0:T(512)(128)(2,1)S(1)}, bf16[512]{0:T(512)(128)(2,1)}, u32[]{:S(2)}) copy-start(bf16[512]{0:T(512)(128)(2,1)} %param.15) | copy-start | bytes 3076
  17.8 4.6 %copy-start.2 = (bf16[864,1024]{1,0:T(8,128)(2,1)}, bf16[864,1024]{1,0:T(8,128)(2,1)S(1)}, u32[]{:S(2)}) copy-start(bf16[864,1024]{1,0:T(8,128)(2,1)S(1)} %convolution_convert_fusion.kv_ref) | copy-start | bytes 5308420
  17.8 4.5 %collective-permute-start.2 = (bf16[864,1024]{1,0:T(8,128)(2,1)S(1)}, bf16[864,1024]{1,0:T(8,128)(2,1)S(1)}, u32[]{:S(2)}, u32[]{:S(2)}) collective-permute-start(bf16[864,1024]{1,0:T(8,128)(2,1)S(1)} %convolution_convert_fusion.kv_ref), channel_id=1, source_target_pairs={{0,1},{1,0},{2,3},{3,2},{4,5},{5,4},{6,7},{7,6},{8,9},{9,8},{10,11... | collective-permute-start | bytes 5308424 | tf_op jit(solution)/shard_map/ppermute | solution.py:324
  22.4 1.2 copy-start.3
  23.6 102.0 %copy-start.6 = (bf16[512,512]{1,0:T(8,128)(2,1)S(1)}, bf16[512,512]{1,0:T(8,128)(2,1)}, u32[]{:S(2)}) copy-start(bf16[512,512]{1,0:T(8,128)(2,1)} %param.17) | copy-start | bytes 1572868

commit v7 on v5

--- a/solution.py
+++ b/solution.py
@@ -304,7 +304,7 @@
     padded = extended(embed, (("tok", 1),), 1)
     stream = depthwise(padded[0], conv_taps).reshape(frames, tokens, width)
     normed = rms_scale(stream.astype(jnp.float32), gain_space).astype(jnp.bfloat16)
-    flat = normed.reshape(-1, width)
+    flat = lax.optimization_barrier(normed.reshape(-1, width))
     own_kv = jnp.dot(flat, qkv_space[:, width:], preferred_element_type=jnp.float32).astype(
         jnp.bfloat16
     )

time: 127 us -> 127 us (level)
  matrix products: 9.09 us -> 6.49 us
  local copies, waits for them, and re-layouts: 4.53 us -> 5.83 us
    dot_general x1, matrix products: 2.57 us -> 1.08 us  [local(): jnp.dot(flat, qkv_space[:, width:], preferred_element_type=jnp.float32)]
    unnamed x16 -> x18, local copies, waits for them, and re-layouts: 2.5 us -> 3.81 us
  transfers between devices with their start and end apart: 3 -> 3, of which waited for: 2 -> 2; matrix products, arithmetic and copies ran while one was open for 3% -> 2% of each run, Pallas kernels for 0% -> 0%
where the time goes in v7:
time: 127 us
  Pallas kernels  105 us (83%)
  matrix products  6.49 us (5%)
  local copies, waits for them, and re-layouts  5.83 us (5%)
  starting transfers between devices  3.27 us (3%)
  waiting for transfers between devices  3.19 us (3%)
  other arithmetic  2.39 us (2%)
    pallas_call x1, Pallas kernels, block_tail(): pl.pallas_call(functools.partial(block_kernel, chunks), out_shape=(plane,...  100 us
    pallas_call x1, Pallas kernels, depthwise(): pl.pallas_call(conv_kernel, out_shape=jax.ShapeDtypeStruct((planes, grid,...  4.84 us
    unnamed x18, local copies, waits for them, and re-layouts  3.81 us
  transfers between devices with their start and end apart: 3, of which 2 were waited for; matrix products, arithmetic and copies ran while one was open for 2% of the time, Pallas kernels for 0%

profile of v7, /device:TPU:24, one launch (start us, length us, event | category | flops | bytes accessed | tf_op | source)
XLA Modules:
  0.0 126.7 jit_solution(11888625225073921193)
XLA Ops:
  0.0 0.0 copy-start
  0.0 0.0 copy-start.5
  0.0 0.0 copy-start.4
  0.0 1.3 copy-done
  1.3 1.8 %fusion = bf16[1,6,12,12,512]{4,3,2,1,0:T(8,128)(2,1)S(1)} fusion(bf16[1,6,12,12,512]{4,3,2,1,0:T(8,128)(2,1)S(1)} %copy-done, bf16[512,512]{1,0:T(8,128)(2,1)} %param.10), kind=kOutput, calls=%fused_computation.8 | convolution fusion | flops 453427200 | bytes 2293760 | tf_op jit(solution)/shard_map/dot_general | solution.py:301
  3.1 1.8 %collective-permute-start = (bf16[1,1,12,12,512]{4,3,2,1,0:T(8,128)(2,1)S(1)}, bf16[1,1,12,12,512]{4,3,2,1,0:T(8,128)(2,1)S(1)}, u32[]{:S(2)}, u32[]{:S(2)}) collective-permute-start(bf16[1,1,12,12,512]{4,3,2,1,0:T(8,128)(2,1)S(1)} %get-tuple-element.9), channel_id=1, source_target_pairs={{0,1},{2,3},{4,5},{6,7},{8,9},{10,11},{12,13},{14,15},{16,17},{18,... | collective-permute-start | bytes 442376 | tf_op jit(solution)/shard_map/ppermute | solution.py:19
  4.9 1.3 %collective-permute-start.1 = (bf16[1,1,12,12,512]{4,3,2,1,0:T(8,128)(2,1)S(1)}, bf16[1,1,12,12,512]{4,3,2,1,0:T(8,128)(2,1)S(1)}, u32[]{:S(2)}, u32[]{:S(2)}) collective-permute-start(bf16[1,1,12,12,512]{4,3,2,1,0:T(8,128)(2,1)S(1)} %get-tuple-element.10), channel_id=1, source_target_pairs={{1,0},{3,2},{5,4},{7,6},{9,8},{11,10},{13,12},{15,14},{17,16},{19,... | collective-permute-start | bytes 442376 | tf_op jit(solution)/shard_map/ppermute | solution.py:22
  6.2 0.0 copy-done.5
  6.2 0.0 copy-done.4
  6.2 0.0 collective-permute-done
  6.2 2.0 %collective-permute-done.1 = bf16[1,1,12,12,512]{4,3,2,1,0:T(8,128)(2,1)S(1)} collective-permute-done((bf16[1,1,12,12,512]{4,3,2,1,0:T(8,128)(2,1)S(1)}, bf16[1,1,12,12,512]{4,3,2,1,0:T(8,128)(2,1)S(1)}, u32[]{:S(2)}, u32[]{:S(2)}) %collective-permute-start.1) | collective-permute-done | bytes 147488 | tf_op jit(solution)/shard_map/ppermute | solution.py:22
  8.2 0.2 maximum_bitcast_fusion
  8.5 0.6 pad_convert_fusion.e_ref
  9.1 4.8 %shard_map.91 = bf16[6,12,16,512]{3,2,1,0:T(8,128)(2,1)S(1)} custom-call(f32[8,14,16,512]{3,2,1,0:T(8,128)S(1)} %pad_convert_fusion.e_ref, f32[27,512]{1,0:T(8,128)S(1)} %convert_element_type.51.t_ref), custom_call_target="tpu_custom_call" | custom-call | tf_op jit(solution)/shard_map/pallas_call | solution.py:91
  13.9 0.5 multiply_reduce_fusion
  14.4 0.5 slice.22
  14.9 0.2 reshape.71.stream_ref
  15.1 0.0 copy-start.1
  15.1 0.1 rsqrt.12
  15.2 0.0 copy-start.7
  15.2 0.3 multiply_convert_fusion
  15.5 1.3 %copy-done.7 = bf16[512,1536]{1,0:T(8,128)(2,1)S(1)} copy-done((bf16[512,1536]{1,0:T(8,128)(2,1)S(1)}, bf16[512,1536]{1,0:T(8,128)(2,1)}, u32[]{:S(2)}) %copy-start.7) | copy-done | bytes 1572888
  16.8 0.0 copy-start.6
  16.8 1.1 convolution_convert_fusion.kv_ref
  17.9 0.0 copy-done.1
  17.9 0.0 copy-start.2
  17.9 0.2 collective-permute-start.2
  18.2 0.0 copy-done.6
  18.2 0.8 reshape.75
  19.0 1.5 %convolution_convert_fusion.2.q_ref = bf16[864,512]{1,0:T(8,128)(2,1)} fusion(bf16[864,512]{1,0:T(8,128)(2,1)S(1)} %multiply_convert_fusion, bf16[512,1536]{1,0:T(8,128)(2,1)S(1)} %copy-done.7), kind=kOutput, calls=%fused_computation.7 | convolution fusion | flops 453427200 | bytes 2293760 | tf_op jit(solution)/shard_map/dot_general | solution.py:313
  20.5 1.2 collective-permute-done.2.other_ref
  21.7 0.0 copy-start.3
  21.7 0.0 copy-done.2
  21.7 1.2 copy-done.3
  22.9 0.0 copy-start.8
  22.9 100.5 %shard_map.92 = (bf16[864,512]{1,0:T(8,128)(2,1)}, bf16[864,512]{1,0:T(8,128)(2,1)}) custom-call(bf16[864,512]{1,0:T(8,128)(2,1)} %convolution_convert_fusion.2.q_ref, bf16[864,1024]{1,0:T(8,128)(2,1)} %copy-done.2, bf16[864,1024]{1,0:T(8,128)(2,1)} %copy-done.3, bf16[864,512]{1,0:T(8,128)(2,1)} %copy-done.1, bf16[512,512]{1,0:T(8,128)(2,1)} %wo_ref.1, ...), custom_call_target="tpu_custom_call" | custom-call | tf_op jit(solution)/shard_map/pallas_call | solution.py:266
  123.4 0.0 copy-done.8
  123.4 2.1 %add_convert_fusion = bf16[864,512]{1,0:T(8,128)(2,1)S(1)} fusion(bf16[864,512]{1,0:T(8,128)(2,1)} %get-tuple-element.7, bf16[864,512]{1,0:T(8,128)(2,1)} %get-tuple-element.8, bf16[512,512]{1,0:T(8,128)(2,1)S(1)} %copy-done.8), kind=kOutput, calls=%fused_computation.2 | convolution fusion | flops 454311936 | bytes 3178496 | tf_op jit(solution)/shard_map/dot_general | solution.py:319
  125.5 1.2 reshape.74
  (4 shorter events, 0.1 us)
Async XLA Ops:
  0.0 1.3 %copy-start = (bf16[1,6,12,12,512]{4,3,2,1,0:T(8,128)(2,1)S(1)}, bf16[1,6,12,12,512]{4,3,2,1,0:T(8,128)(2,1)}, u32[]{:S(2)}) copy-start(bf16[1,6,12,12,512]{4,3,2,1,0:T(8,128)(2,1)} %param.9) | copy-start | bytes 2654212
  0.0 6.2 %copy-start.5 = (bf16[512]{0:T(512)(128)(2,1)S(1)}, bf16[512]{0:T(512)(128)(2,1)}, u32[]{:S(2)}) copy-start(bf16[512]{0:T(512)(128)(2,1)} %param.12) | copy-start | bytes 3076
  0.0 6.2 %copy-start.4 = (bf16[27,512]{1,0:T(8,128)(2,1)S(1)}, bf16[27,512]{1,0:T(8,128)(2,1)}, u32[]{:S(2)}) copy-start(bf16[27,512]{1,0:T(8,128)(2,1)} %param.11) | copy-start | bytes 82948
  3.1 3.1 %collective-permute-start = (bf16[1,1,12,12,512]{4,3,2,1,0:T(8,128)(2,1)S(1)}, bf16[1,1,12,12,512]{4,3,2,1,0:T(8,128)(2,1)S(1)}, u32[]{:S(2)}, u32[]{:S(2)}) collective-permute-start(bf16[1,1,12,12,512]{4,3,2,1,0:T(8,128)(2,1)S(1)} %get-tuple-element.9), channel_id=1, source_target_pairs={{0,1},{2,3},{4,5},{6,7},{8,9},{10,11},{12,13},{14,15},{16,17},{18,... | collective-permute-start | bytes 442376 | tf_op jit(solution)/shard_map/ppermute | solution.py:19
  4.9 3.3 %collective-permute-start.1 = (bf16[1,1,12,12,512]{4,3,2,1,0:T(8,128)(2,1)S(1)}, bf16[1,1,12,12,512]{4,3,2,1,0:T(8,128)(2,1)S(1)}, u32[]{:S(2)}, u32[]{:S(2)}) collective-permute-start(bf16[1,1,12,12,512]{4,3,2,1,0:T(8,128)(2,1)S(1)} %get-tuple-element.10), channel_id=1, source_target_pairs={{1,0},{3,2},{5,4},{7,6},{9,8},{11,10},{13,12},{15,14},{17,16},{19,... | collective-permute-start | bytes 442376 | tf_op jit(solution)/shard_map/ppermute | solution.py:22
  15.1 2.8 %copy-start.1 = (bf16[864,512]{1,0:T(8,128)(2,1)}, bf16[864,512]{1,0:T(8,128)(2,1)S(1)}, u32[]{:S(2)}) copy-start(bf16[864,512]{1,0:T(8,128)(2,1)S(1)} %reshape.71.stream_ref) | copy-start | bytes 2654212
  15.2 1.6 %copy-start.7 = (bf16[512,1536]{1,0:T(8,128)(2,1)S(1)}, bf16[512,1536]{1,0:T(8,128)(2,1)}, u32[]{:S(2)}) copy-start(bf16[512,1536]{1,0:T(8,128)(2,1)} %param.13) | copy-start | bytes 4718596
  16.8 1.3 %copy-start.6 = (bf16[512]{0:T(512)(128)(2,1)S(1)}, bf16[512]{0:T(512)(128)(2,1)}, u32[]{:S(2)}) copy-start(bf16[512]{0:T(512)(128)(2,1)} %param.15) | copy-start | bytes 3076
  17.9 3.8 %copy-start.2 = (bf16[864,1024]{1,0:T(8,128)(2,1)}, bf16[864,1024]{1,0:T(8,128)(2,1)S(1)}, u32[]{:S(2)}) copy-start(bf16[864,1024]{1,0:T(8,128)(2,1)S(1)} %convolution_convert_fusion.kv_ref) | copy-start | bytes 5308420
  17.9 3.8 %collective-permute-start.2 = (bf16[864,1024]{1,0:T(8,128)(2,1)S(1)}, bf16[864,1024]{1,0:T(8,128)(2,1)S(1)}, u32[]{:S(2)}, u32[]{:S(2)}) collective-permute-start(bf16[864,1024]{1,0:T(8,128)(2,1)S(1)} %convolution_convert_fusion.kv_ref), channel_id=1, source_target_pairs={{0,1},{1,0},{2,3},{3,2},{4,5},{5,4},{6,7},{7,6},{8,9},{9,8},{10,11... | collective-permute-start | bytes 5308424 | tf_op jit(solution)/shard_map/ppermute | solution.py:312
  21.7 1.2 copy-start.3
  22.9 100.5 %copy-start.8 = (bf16[512,512]{1,0:T(8,128)(2,1)S(1)}, bf16[512,512]{1,0:T(8,128)(2,1)}, u32[]{:S(2)}) copy-start(bf16[512,512]{1,0:T(8,128)(2,1)} %param.17) | copy-start | bytes 1572868

commit v8 on v5

--- a/solution.py
+++ b/solution.py
@@ -301,7 +301,16 @@
     embed = jnp.dot(patches, patch_weight, preferred_element_type=jnp.float32).astype(
         jnp.bfloat16
     )
-    padded = extended(embed, (("tok", 1),), 1)
+    if lax.axis_size("tok") == 2:
+        side = lax.axis_index("tok")
+        edge = lax.dynamic_slice_in_dim(embed, jnp.where(side == 0, zdev - 1, 0), 1, axis=1)
+        halo = lax.ppermute(edge, "tok", [(0, 1), (1, 0)])
+        empty = jnp.zeros_like(halo)
+        low = jnp.where(side == 1, halo, empty)
+        high = jnp.where(side == 0, halo, empty)
+        padded = jnp.concatenate([low, embed, high], axis=1)
+    else:
+        padded = extended(embed, (("tok", 1),), 1)
     stream = depthwise(padded[0], conv_taps).reshape(frames, tokens, width)
     normed = rms_scale(stream.astype(jnp.float32), gain_space).astype(jnp.bfloat16)
     flat = normed.reshape(-1, width)

time: 127 us -> 123 us (0.969)
  starting transfers between devices: 3.27 us -> 0.32 us
    ppermute x2 -> x1, starting transfers between devices: 3.04 us -> 0.09 us  [local(): halo = lax.ppermute(edge, 'tok', [(0, 1), (1, 0)])]
  transfers between devices with their start and end apart: 3 -> 2, of which waited for: 2 -> 2; matrix products, arithmetic and copies ran while one was open for 3% -> 3% of each run, Pallas kernels for 0% -> 0%
where the time goes in v8:
time: 123 us
  Pallas kernels  105 us (85%)
  matrix products  9.11 us (7%)
  local copies, waits for them, and re-layouts  4.52 us (4%)
  other arithmetic  2.16 us (2%)
  waiting for transfers between devices  1.46 us (1%)
    pallas_call x1, Pallas kernels, block_tail(): pl.pallas_call(functools.partial(block_kernel, chunks), out_shape=(plane,...  101 us
    pallas_call x1, Pallas kernels, depthwise(): pl.pallas_call(conv_kernel, out_shape=jax.ShapeDtypeStruct((planes, grid,...  4.84 us
    dot_general x1, matrix products, local(): jnp.dot(flat, qkv_space[:, :width], preferred_element_type=jnp.float32)  2.66 us
    dot_general x1, matrix products, local(): jnp.dot(flat, qkv_space[:, width:], preferred_element_type=jnp.float32)  2.57 us
    unnamed x16, local copies, waits for them, and re-layouts  2.49 us
  transfers between devices with their start and end apart: 2, of which 2 were waited for; matrix products, arithmetic and copies ran while one was open for 3% of the time, Pallas kernels for 0%

profile of v8, /device:TPU:24, one launch (start us, length us, event | category | flops | bytes accessed | tf_op | source)
XLA Modules:
  0.0 123.1 jit_solution(15542085808837789764)
XLA Ops:
  0.0 0.0 copy-start
  0.0 1.3 %copy-done = bf16[1,6,12,12,512]{4,3,2,1,0:T(8,128)(2,1)S(1)} copy-done((bf16[1,6,12,12,512]{4,3,2,1,0:T(8,128)(2,1)S(1)}, bf16[1,6,12,12,512]{4,3,2,1,0:T(8,128)(2,1)}, u32[]{:S(2)}) %copy-start) | copy-done | bytes 884760
  1.3 0.0 copy-start.5
  1.3 0.0 copy-start.4
  1.3 1.8 %convolution_convert_fusion.1 = bf16[6,12,12,512]{3,2,1,0:T(8,128)(2,1)S(1)} fusion(bf16[1,6,12,12,512]{4,3,2,1,0:T(8,128)(2,1)S(1)} %copy-done, bf16[512,512]{1,0:T(8,128)(2,1)} %param.10), kind=kOutput, calls=%fused_computation.6 | convolution fusion | flops 453427200 | bytes 2293760 | tf_op jit(solution)/shard_map/dot_general | solution.py:301
  3.1 0.1 collective-permute-start
  3.2 0.0 copy-done.5
  3.3 0.0 copy-done.4
  3.3 1.4 %collective-permute-done = bf16[1,1,12,12,512]{4,3,2,1,0:T(8,128)(2,1)S(1)} collective-permute-done((bf16[1,1,12,12,512]{4,3,2,1,0:T(8,128)(2,1)S(1)}, bf16[1,1,12,12,512]{4,3,2,1,0:T(8,128)(2,1)S(1)}, u32[]{:S(2)}, u32[]{:S(2)}) %collective-permute-start) | collective-permute-done | bytes 147488 | tf_op jit(solution)/shard_map/ppermute | solution.py:307
  4.7 0.2 maximum_bitcast_fusion
  4.9 0.6 pad_convert_fusion.e_ref
  5.5 4.8 %shard_map.91 = bf16[6,12,16,512]{3,2,1,0:T(8,128)(2,1)S(1)} custom-call(f32[8,14,16,512]{3,2,1,0:T(8,128)S(1)} %pad_convert_fusion.e_ref, f32[27,512]{1,0:T(8,128)S(1)} %convert_element_type.51.t_ref), custom_call_target="tpu_custom_call" | custom-call | tf_op jit(solution)/shard_map/pallas_call | solution.py:91
  10.4 0.5 multiply_reduce_fusion
  10.9 0.5 slice.12
  11.4 0.2 reshape.72.stream_ref
  11.6 0.0 copy-start.1
  11.6 0.1 rsqrt.12
  11.7 0.0 copy-start.6
  11.7 2.6 %convolution_convert_fusion.kv_ref = bf16[864,1024]{1,0:T(8,128)(2,1)S(1)} fusion(bf16[512,1536]{1,0:T(8,128)(2,1)} %param.13, bf16[864,512]{1,0:T(8,128)(2,1)S(1)} %reshape.72.stream_ref, f32[512]{0:T(512)S(1)} %convert_element_type.54, f32[864]{0:T(1024)S(1)} %rsqrt.12), kind=kOutput, calls=%fused_computation.4 | convolution fusion | flops 908623872 | bytes 3708288 | tf_op jit(solution)/shard_map/dot_general | solution.py:317
  14.3 0.0 copy-start.2
  14.3 0.2 collective-permute-start.1
  14.5 0.0 copy-done.6
  14.5 0.8 reshape.76
  15.3 0.0 copy-done.1
  15.3 2.7 %convolution_convert_fusion.2.q_ref = bf16[864,512]{1,0:T(8,128)(2,1)} fusion(bf16[512,1536]{1,0:T(8,128)(2,1)} %param.13, bf16[864,512]{1,0:T(8,128)(2,1)S(1)} %reshape.72.stream_ref, f32[512]{0:T(512)S(1)} %convert_element_type.54, f32[864]{0:T(1024)S(1)} %rsqrt.12), kind=kOutput, calls=%fused_computation.7 | convolution fusion | flops 455196672 | bytes 2299264 | tf_op jit(solution)/shard_map/dot_general | solution.py:322
  18.0 0.0 copy-done.2
  18.0 0.1 collective-permute-done.1.other_ref
  18.1 0.0 copy-start.3
  18.1 1.2 copy-done.3
  19.3 0.0 copy-start.7
  19.3 100.5 %shard_map.92 = (bf16[864,512]{1,0:T(8,128)(2,1)}, bf16[864,512]{1,0:T(8,128)(2,1)}) custom-call(bf16[864,512]{1,0:T(8,128)(2,1)} %convolution_convert_fusion.2.q_ref, bf16[864,1024]{1,0:T(8,128)(2,1)} %copy-done.2, bf16[864,1024]{1,0:T(8,128)(2,1)} %copy-done.3, bf16[864,512]{1,0:T(8,128)(2,1)} %copy-done.1, bf16[512,512]{1,0:T(8,128)(2,1)} %wo_ref.1, ...), custom_call_target="tpu_custom_call" | custom-call | tf_op jit(solution)/shard_map/pallas_call | solution.py:266
  119.8 0.0 copy-done.7
  119.8 2.1 %add_convert_fusion = bf16[864,512]{1,0:T(8,128)(2,1)S(1)} fusion(bf16[864,512]{1,0:T(8,128)(2,1)} %get-tuple-element.7, bf16[864,512]{1,0:T(8,128)(2,1)} %get-tuple-element.8, bf16[512,512]{1,0:T(8,128)(2,1)S(1)} %copy-done.7), kind=kOutput, calls=%fused_computation.2 | convolution fusion | flops 454311936 | bytes 3178496 | tf_op jit(solution)/shard_map/dot_general | solution.py:328
  121.9 1.2 reshape.75
  (5 shorter events, 0.1 us)
Async XLA Ops:
  0.0 1.3 %copy-start = (bf16[1,6,12,12,512]{4,3,2,1,0:T(8,128)(2,1)S(1)}, bf16[1,6,12,12,512]{4,3,2,1,0:T(8,128)(2,1)}, u32[]{:S(2)}) copy-start(bf16[1,6,12,12,512]{4,3,2,1,0:T(8,128)(2,1)} %param.9) | copy-start | bytes 2654212
  1.3 2.0 %copy-start.5 = (bf16[512]{0:T(512)(128)(2,1)S(1)}, bf16[512]{0:T(512)(128)(2,1)}, u32[]{:S(2)}) copy-start(bf16[512]{0:T(512)(128)(2,1)} %param.12) | copy-start | bytes 3076
  1.3 2.0 %copy-start.4 = (bf16[27,512]{1,0:T(8,128)(2,1)S(1)}, bf16[27,512]{1,0:T(8,128)(2,1)}, u32[]{:S(2)}) copy-start(bf16[27,512]{1,0:T(8,128)(2,1)} %param.11) | copy-start | bytes 82948
  3.1 1.5 %collective-permute-start = (bf16[1,1,12,12,512]{4,3,2,1,0:T(8,128)(2,1)S(1)}, bf16[1,1,12,12,512]{4,3,2,1,0:T(8,128)(2,1)S(1)}, u32[]{:S(2)}, u32[]{:S(2)}) collective-permute-start(bf16[1,1,12,12,512]{4,3,2,1,0:T(8,128)(2,1)S(1)} %dynamic-slice_bitcast_fusion), channel_id=1, source_target_pairs={{0,1},{1,0},{2,3},{3,2},{4,5},{5,4},{6,7},{7,6},{8,9},{9,8},{10,11... | collective-permute-start | bytes 442376 | tf_op jit(solution)/shard_map/ppermute | solution.py:307
  11.6 3.8 %copy-start.1 = (bf16[864,512]{1,0:T(8,128)(2,1)}, bf16[864,512]{1,0:T(8,128)(2,1)S(1)}, u32[]{:S(2)}) copy-start(bf16[864,512]{1,0:T(8,128)(2,1)S(1)} %reshape.72.stream_ref) | copy-start | bytes 2654212
  11.7 2.8 %copy-start.6 = (bf16[512]{0:T(512)(128)(2,1)S(1)}, bf16[512]{0:T(512)(128)(2,1)}, u32[]{:S(2)}) copy-start(bf16[512]{0:T(512)(128)(2,1)} %param.15) | copy-start | bytes 3076
  14.3 3.7 %copy-start.2 = (bf16[864,1024]{1,0:T(8,128)(2,1)}, bf16[864,1024]{1,0:T(8,128)(2,1)S(1)}, u32[]{:S(2)}) copy-start(bf16[864,1024]{1,0:T(8,128)(2,1)S(1)} %convolution_convert_fusion.kv_ref) | copy-start | bytes 5308420
  14.3 3.8 %collective-permute-start.1 = (bf16[864,1024]{1,0:T(8,128)(2,1)S(1)}, bf16[864,1024]{1,0:T(8,128)(2,1)S(1)}, u32[]{:S(2)}, u32[]{:S(2)}) collective-permute-start(bf16[864,1024]{1,0:T(8,128)(2,1)S(1)} %convolution_convert_fusion.kv_ref), channel_id=1, source_target_pairs={{0,1},{1,0},{2,3},{3,2},{4,5},{5,4},{6,7},{7,6},{8,9},{9,8},{10,11... | collective-permute-start | bytes 5308424 | tf_op jit(solution)/shard_map/ppermute | solution.py:321
  18.1 1.2 copy-start.3
  19.3 100.5 %copy-start.7 = (bf16[512,512]{1,0:T(8,128)(2,1)S(1)}, bf16[512,512]{1,0:T(8,128)(2,1)}, u32[]{:S(2)}) copy-start(bf16[512,512]{1,0:T(8,128)(2,1)} %param.17) | copy-start | bytes 1572868

commit v9 on v8

--- a/solution.py
+++ b/solution.py
@@ -99,7 +99,7 @@
 
 
 def block_kernel(
-    chunks, q_ref, kv_ref, other_ref, stream_ref, wo_ref, gain_ref, wt_ref,
+    chunks, q_ref, kv_ref, other_ref, stream_ref, wo_ref, gain_ref, wt_ref, wout_ref,
     out_ref, stream2_ref, own, query2, hist, mixed, total, sum_ref, send_sem, recv_sem,
 ):
     me = lax.axis_index("tm")
@@ -245,6 +245,12 @@
                     copy_of(hop + 1, piece).start()
 
             add_term(hist[hop, span, :], span, me - (hop + 1) >= 0, False)
+            if hop + 1 == WIN:
+                temporal = (mixed[span, :] / total[span, :]).astype(jnp.bfloat16)
+                out_ref[span, :] = (
+                    stream2_ref[span, :].astype(jnp.float32)
+                    + jnp.dot(temporal, wout_ref[...], preferred_element_type=jnp.float32)
+                ).astype(out_ref.dtype)
             return carry
 
         lax.fori_loop(0, chunks, hop_step, 0)
@@ -255,20 +261,21 @@
             for piece in range(chunks):
                 copy_of(hop, piece).wait_send()
 
-    out_ref[...] = (mixed[...] / total[...]).astype(out_ref.dtype)
-
-
-def block_tail(query, keys_values, other, stream, out_space, gain_time, qkv_time, chunks=6):
+
+def block_tail(
+    query, keys_values, other, stream, out_space, gain_time, qkv_time, out_time, chunks=6
+):
     rows, width = stream.shape
     gain = gain_time.astype(jnp.float32).reshape(1, width)
     vmem = pl.BlockSpec(memory_space=pltpu.VMEM)
     plane = jax.ShapeDtypeStruct((rows, width), jnp.bfloat16)
     return pl.pallas_call(
         functools.partial(block_kernel, chunks),
-        out_shape=(plane, plane),
-        in_specs=[vmem] * 7,
-        out_specs=(vmem, vmem),
+        out_shape=plane,
+        in_specs=[vmem] * 8,
+        out_specs=vmem,
         scratch_shapes=[
+            pltpu.VMEM((rows, width), jnp.bfloat16),
             pltpu.VMEM((rows, width), jnp.bfloat16),
             pltpu.VMEM((rows, width), jnp.bfloat16),
             pltpu.VMEM((WIN, rows, width), jnp.bfloat16),
@@ -281,7 +288,7 @@
         compiler_params=pltpu.CompilerParams(
             collective_id=0, has_side_effects=True, vmem_limit_bytes=56 * 1024 * 1024
         ),
-    )(query, keys_values, other, stream, out_space, gain, qkv_time)
+    )(query, keys_values, other, stream, out_space, gain, qkv_time, out_time)
 
 
 def local(
@@ -322,13 +329,10 @@
     query = jnp.dot(flat, qkv_space[:, :width], preferred_element_type=jnp.float32).astype(
         jnp.bfloat16
     )
-    temporal, stream2 = block_tail(
-        query, own_kv, other_kv, stream.reshape(-1, width), out_space, gain_time, qkv_time
-    )
-    time_proj = jnp.dot(
-        temporal.reshape(-1, width), out_time, preferred_element_type=jnp.float32
-    ).reshape(frames, tokens, width)
-    output = (stream2.astype(jnp.float32) + time_proj).astype(jnp.bfloat16)
+    output = block_tail(
+        query, own_kv, other_kv, stream.reshape(-1, width), out_space, gain_time, qkv_time,
+        out_time,
+    )
     return output.reshape(frames, zdev, grid, grid, width)
 
 

time: 123 us -> 122 us (level)
  matrix products: 9.11 us -> 7.05 us
    dot_general x1 -> x0, matrix products: 2.05 us -> none  [local(): jnp.dot(temporal.reshape(-1, width), out_time, preferred_element_type=jnp...]
    unnamed x16 -> x14, local copies, waits for them, and re-layouts: 2.49 us -> 2.5 us
where the time goes in v9:
time: 122 us
  Pallas kernels  105 us (86%)
  matrix products  7.05 us (6%)
  local copies, waits for them, and re-layouts  5.47 us (4%)
  other arithmetic  2.12 us (2%)
  waiting for transfers between devices  1.51 us (1%)
    pallas_call x1, Pallas kernels, block_tail(): pl.pallas_call(functools.partial(block_kernel, chunks), out_shape=plane,...  100 us
    pallas_call x1, Pallas kernels, depthwise(): pl.pallas_call(conv_kernel, out_shape=jax.ShapeDtypeStruct((planes, grid,...  4.84 us
    dot_general x1, matrix products, local(): jnp.dot(flat, qkv_space[:, :width], preferred_element_type=jnp.float32)  2.66 us
    dot_general x1, matrix products, local(): jnp.dot(flat, qkv_space[:, width:], preferred_element_type=jnp.float32)  2.57 us
    unnamed x14, local copies, waits for them, and re-layouts  2.5 us
  transfers between devices with their start and end apart: 2, of which 2 were waited for; matrix products, arithmetic and copies ran while one was open for 3% of the time, Pallas kernels for 0%

profile of v9, /device:TPU:24, one launch (start us, length us, event | category | flops | bytes accessed | tf_op | source)
XLA Modules:
  0.0 121.9 jit_solution(8734838130133821332)
XLA Ops:
  0.0 0.0 copy-start
  0.0 1.3 %copy-done = bf16[1,6,12,12,512]{4,3,2,1,0:T(8,128)(2,1)S(1)} copy-done((bf16[1,6,12,12,512]{4,3,2,1,0:T(8,128)(2,1)S(1)}, bf16[1,6,12,12,512]{4,3,2,1,0:T(8,128)(2,1)}, u32[]{:S(2)}) %copy-start) | copy-done | bytes 884760
  1.3 0.0 copy-start.5
  1.3 0.0 copy-start.4
  1.3 1.8 %convolution_convert_fusion.1 = bf16[6,12,12,512]{3,2,1,0:T(8,128)(2,1)S(1)} fusion(bf16[1,6,12,12,512]{4,3,2,1,0:T(8,128)(2,1)S(1)} %copy-done, bf16[512,512]{1,0:T(8,128)(2,1)} %param.10), kind=kOutput, calls=%fused_computation.5 | convolution fusion | flops 453427200 | bytes 2293760 | tf_op jit(solution)/shard_map/dot_general | solution.py:308
  3.1 0.1 collective-permute-start
  3.2 0.0 copy-done.5
  3.3 0.0 copy-done.4
  3.3 1.4 %collective-permute-done = bf16[1,1,12,12,512]{4,3,2,1,0:T(8,128)(2,1)S(1)} collective-permute-done((bf16[1,1,12,12,512]{4,3,2,1,0:T(8,128)(2,1)S(1)}, bf16[1,1,12,12,512]{4,3,2,1,0:T(8,128)(2,1)S(1)}, u32[]{:S(2)}, u32[]{:S(2)}) %collective-permute-start) | collective-permute-done | bytes 147488 | tf_op jit(solution)/shard_map/ppermute | solution.py:314
  4.7 0.2 maximum_bitcast_fusion
  4.9 0.6 pad_convert_fusion.e_ref
  5.5 4.8 %shard_map.91 = bf16[6,12,16,512]{3,2,1,0:T(8,128)(2,1)S(1)} custom-call(f32[8,14,16,512]{3,2,1,0:T(8,128)S(1)} %pad_convert_fusion.e_ref, f32[27,512]{1,0:T(8,128)S(1)} %convert_element_type.44.t_ref), custom_call_target="tpu_custom_call" | custom-call | tf_op jit(solution)/shard_map/pallas_call | solution.py:91
  10.4 0.5 multiply_reduce_fusion
  10.9 0.5 slice.12
  11.4 0.2 reshape.68.stream_ref
  11.6 0.0 copy-start.1
  11.6 0.1 rsqrt.12
  11.7 0.0 copy-start.6
  11.7 2.6 %convolution_convert_fusion.kv_ref = bf16[864,1024]{1,0:T(8,128)(2,1)S(1)} fusion(bf16[512,1536]{1,0:T(8,128)(2,1)} %param.13, bf16[864,512]{1,0:T(8,128)(2,1)S(1)} %reshape.68.stream_ref, f32[512]{0:T(512)S(1)} %convert_element_type.47, f32[864]{0:T(1024)S(1)} %rsqrt.12), kind=kOutput, calls=%fused_computation.3 | convolution fusion | flops 908623872 | bytes 3708288 | tf_op jit(solution)/shard_map/dot_general | solution.py:324
  14.3 0.0 copy-start.2
  14.3 0.2 collective-permute-start.1
  14.5 0.0 copy-done.6
  14.5 0.8 reshape.72
  15.3 0.0 copy-done.1
  15.3 2.7 %convolution_convert_fusion.2.q_ref = bf16[864,512]{1,0:T(8,128)(2,1)} fusion(bf16[512,1536]{1,0:T(8,128)(2,1)} %param.13, bf16[864,512]{1,0:T(8,128)(2,1)S(1)} %reshape.68.stream_ref, f32[512]{0:T(512)S(1)} %convert_element_type.47, f32[864]{0:T(1024)S(1)} %rsqrt.12), kind=kOutput, calls=%fused_computation.6 | convolution fusion | flops 455196672 | bytes 2299264 | tf_op jit(solution)/shard_map/dot_general | solution.py:329
  18.0 0.0 copy-done.2
  18.0 0.1 collective-permute-done.1.other_ref
  18.1 0.0 copy-start.3
  18.1 1.2 copy-done.3
  19.3 100.5 %shard_map.92 = bf16[864,512]{1,0:T(8,128)(2,1)} custom-call(bf16[864,512]{1,0:T(8,128)(2,1)} %convolution_convert_fusion.2.q_ref, bf16[864,1024]{1,0:T(8,128)(2,1)} %copy-done.2, bf16[864,1024]{1,0:T(8,128)(2,1)} %copy-done.3, bf16[864,512]{1,0:T(8,128)(2,1)} %copy-done.1, bf16[512,512]{1,0:T(8,128)(2,1)} %wo_ref.1, f32[1,512]{1,0:T(1,128)} %bitcast.15, ...), custom_call_target="tpu_custom_call" | custom-call | tf_op jit(solution)/shard_map/pallas_call | solution.py:272
  119.8 2.2 %reshape.71 = bf16[1,6,12,12,512]{4,3,2,1,0:T(8,128)(2,1)} reshape(bf16[864,512]{1,0:T(8,128)(2,1)} %shard_map.92) | data formatting | bytes 1769472 | tf_op jit(solution)/shard_map/reshape | solution.py:336
  (5 shorter events, 0.1 us)
Async XLA Ops:
  0.0 1.3 %copy-start = (bf16[1,6,12,12,512]{4,3,2,1,0:T(8,128)(2,1)S(1)}, bf16[1,6,12,12,512]{4,3,2,1,0:T(8,128)(2,1)}, u32[]{:S(2)}) copy-start(bf16[1,6,12,12,512]{4,3,2,1,0:T(8,128)(2,1)} %param.9) | copy-start | bytes 2654212
  1.3 2.0 %copy-start.5 = (bf16[512]{0:T(512)(128)(2,1)S(1)}, bf16[512]{0:T(512)(128)(2,1)}, u32[]{:S(2)}) copy-start(bf16[512]{0:T(512)(128)(2,1)} %param.12) | copy-start | bytes 3076
  1.3 2.0 %copy-start.4 = (bf16[27,512]{1,0:T(8,128)(2,1)S(1)}, bf16[27,512]{1,0:T(8,128)(2,1)}, u32[]{:S(2)}) copy-start(bf16[27,512]{1,0:T(8,128)(2,1)} %param.11) | copy-start | bytes 82948
  3.1 1.5 %collective-permute-start = (bf16[1,1,12,12,512]{4,3,2,1,0:T(8,128)(2,1)S(1)}, bf16[1,1,12,12,512]{4,3,2,1,0:T(8,128)(2,1)S(1)}, u32[]{:S(2)}, u32[]{:S(2)}) collective-permute-start(bf16[1,1,12,12,512]{4,3,2,1,0:T(8,128)(2,1)S(1)} %dynamic-slice_bitcast_fusion), channel_id=1, source_target_pairs={{0,1},{1,0},{2,3},{3,2},{4,5},{5,4},{6,7},{7,6},{8,9},{9,8},{10,11... | collective-permute-start | bytes 442376 | tf_op jit(solution)/shard_map/ppermute | solution.py:314
  11.6 3.7 %copy-start.1 = (bf16[864,512]{1,0:T(8,128)(2,1)}, bf16[864,512]{1,0:T(8,128)(2,1)S(1)}, u32[]{:S(2)}) copy-start(bf16[864,512]{1,0:T(8,128)(2,1)S(1)} %reshape.68.stream_ref) | copy-start | bytes 2654212
  11.7 2.8 %copy-start.6 = (bf16[512]{0:T(512)(128)(2,1)S(1)}, bf16[512]{0:T(512)(128)(2,1)}, u32[]{:S(2)}) copy-start(bf16[512]{0:T(512)(128)(2,1)} %param.15) | copy-start | bytes 3076
  14.3 3.7 %copy-start.2 = (bf16[864,1024]{1,0:T(8,128)(2,1)}, bf16[864,1024]{1,0:T(8,128)(2,1)S(1)}, u32[]{:S(2)}) copy-start(bf16[864,1024]{1,0:T(8,128)(2,1)S(1)} %convolution_convert_fusion.kv_ref) | copy-start | bytes 5308420
  14.3 3.8 %collective-permute-start.1 = (bf16[864,1024]{1,0:T(8,128)(2,1)S(1)}, bf16[864,1024]{1,0:T(8,128)(2,1)S(1)}, u32[]{:S(2)}, u32[]{:S(2)}) collective-permute-start(bf16[864,1024]{1,0:T(8,128)(2,1)S(1)} %convolution_convert_fusion.kv_ref), channel_id=1, source_target_pairs={{0,1},{1,0},{2,3},{3,2},{4,5},{5,4},{6,7},{7,6},{8,9},{9,8},{10,11... | collective-permute-start | bytes 5308424 | tf_op jit(solution)/shard_map/ppermute | solution.py:328
  18.1 1.2 copy-start.3

commit v10 on v9

--- a/solution.py
+++ b/solution.py
@@ -99,7 +99,7 @@
 
 
 def block_kernel(
-    chunks, q_ref, kv_ref, other_ref, stream_ref, wo_ref, gain_ref, wt_ref, wout_ref,
+    chunks, ws_ref, gain_s_ref, kv_ref, other_ref, stream_ref, wo_ref, gain_ref, wt_ref, wout_ref,
     out_ref, stream2_ref, own, query2, hist, mixed, total, sum_ref, send_sem, recv_sem,
 ):
     me = lax.axis_index("tm")
@@ -181,9 +181,15 @@
     def space_step(piece, carry):
         span = span_of(piece)
         pieces = []
+        current = stream_ref[span, :].astype(jnp.float32)
+        mean_cur = jnp.mean(current * current, axis=-1, keepdims=True)
+        normed = (current * lax.rsqrt(mean_cur + 1e-06) * gain_s_ref[...]).astype(jnp.bfloat16)
+        query_s = jnp.dot(normed, ws_ref[:, :width], preferred_element_type=jnp.float32).astype(
+            jnp.bfloat16
+        )
         for pair in range(width // lanes):
             cols = slice(pair * lanes, (pair + 1) * lanes)
-            q = q_ref[span, cols]
+            q = query_s[:, cols]
             key_cols = slice(width + pair * lanes, width + (pair + 1) * lanes)
             sources = (
                 (kv_ref[:, cols], kv_ref[:, key_cols]),
@@ -263,16 +269,18 @@
 
 
 def block_tail(
-    query, keys_values, other, stream, out_space, gain_time, qkv_time, out_time, chunks=6
+    qkv_space, gain_space, keys_values, other, stream, out_space, gain_time, qkv_time, out_time,
+    chunks=6,
 ):
     rows, width = stream.shape
     gain = gain_time.astype(jnp.float32).reshape(1, width)
+    gain_s = gain_space.astype(jnp.float32).reshape(1, width)
     vmem = pl.BlockSpec(memory_space=pltpu.VMEM)
     plane = jax.ShapeDtypeStruct((rows, width), jnp.bfloat16)
     return pl.pallas_call(
         functools.partial(block_kernel, chunks),
         out_shape=plane,
-        in_specs=[vmem] * 8,
+        in_specs=[vmem] * 9,
         out_specs=vmem,
         scratch_shapes=[
             pltpu.VMEM((rows, width), jnp.bfloat16),
@@ -288,7 +296,7 @@
         compiler_params=pltpu.CompilerParams(
             collective_id=0, has_side_effects=True, vmem_limit_bytes=56 * 1024 * 1024
         ),
-    )(query, keys_values, other, stream, out_space, gain, qkv_time, out_time)
+    )(qkv_space, gain_s, keys_values, other, stream, out_space, gain, qkv_time, out_time)
 
 
 def local(
@@ -326,12 +334,9 @@
     )
     count = lax.axis_size("tok")
     other_kv = lax.ppermute(own_kv, "tok", [(i, (i + 1) % count) for i in range(count)])
-    query = jnp.dot(flat, qkv_space[:, :width], preferred_element_type=jnp.float32).astype(
-        jnp.bfloat16
-    )
     output = block_tail(
-        query, own_kv, other_kv, stream.reshape(-1, width), out_space, gain_time, qkv_time,
-        out_time,
+        qkv_space, gain_space, own_kv, other_kv, stream.reshape(-1, width), out_space,
+        gain_time, qkv_time, out_time,
     )
     return output.reshape(frames, zdev, grid, grid, width)
 

time: 122 us -> 124 us (1.016)
  matrix products: 7.05 us -> 4.37 us
  waiting for transfers between devices: 1.51 us -> 4.08 us
  Pallas kernels: 105 us -> 107 us
    dot_general x1 -> x0, matrix products: 2.66 us -> none  [local(): jnp.dot(flat, qkv_space[:, :width], preferred_element_type=jnp.float32)]
    ppermute x1, waiting for transfers between devices: 0.12 us -> 2.71 us  [local(): lax.ppermute(own_kv, 'tok', [(i, (i + 1) % count) for i in range(count)])]
    pallas_call x1, Pallas kernels: 100 us -> 102 us  [block_tail(): pl.pallas_call(functools.partial(block_kernel, chunks), out_shape=plane,...]
    unnamed x14 -> x16, local copies, waits for them, and re-layouts: 2.5 us -> 2.5 us
  transfers between devices with their start and end apart: 2 -> 2, of which waited for: 2 -> 2; matrix products, arithmetic and copies ran while one was open for 3% -> 1% of each run, Pallas kernels for 0% -> 0%
where the time goes in v10:
time: 124 us; the launch traced here: 123 us
  Pallas kernels  107 us (86%)
  local copies, waits for them, and re-layouts  5.46 us (4%)
  matrix products  4.37 us (4%)
  waiting for transfers between devices  4.08 us (3%)
  other arithmetic  2.2 us (2%)
    pallas_call x1, Pallas kernels, block_tail(): pl.pallas_call(functools.partial(block_kernel, chunks), out_shape=plane,...  102 us
    pallas_call x1, Pallas kernels, depthwise(): pl.pallas_call(conv_kernel, out_shape=jax.ShapeDtypeStruct((planes, grid,...  4.84 us
    ppermute x1, waiting for transfers between devices, local(): lax.ppermute(own_kv, 'tok', [(i, (i + 1) % count) for i in range(count)])  2.71 us
    dot_general x1, matrix products, local(): jnp.dot(flat, qkv_space[:, width:], preferred_element_type=jnp.float32)  2.54 us
    unnamed x16, local copies, waits for them, and re-layouts  2.5 us
  transfers between devices with their start and end apart: 2, of which 2 were waited for; matrix products, arithmetic and copies ran while one was open for 1% of the time, Pallas kernels for 0%

profile of v10, /device:TPU:24, one launch (start us, length us, event | category | flops | bytes accessed | tf_op | source)
XLA Modules:
  0.0 123.5 jit_solution(14700364449415807025)
XLA Ops:
  0.0 0.0 copy-start
  0.0 1.3 %copy-done = bf16[1,6,12,12,512]{4,3,2,1,0:T(8,128)(2,1)S(1)} copy-done((bf16[1,6,12,12,512]{4,3,2,1,0:T(8,128)(2,1)S(1)}, bf16[1,6,12,12,512]{4,3,2,1,0:T(8,128)(2,1)}, u32[]{:S(2)}) %copy-start) | copy-done | bytes 884760
  1.3 0.0 copy-start.6
  1.3 0.0 copy-start.4
  1.3 1.8 %convolution_convert_fusion.1 = bf16[6,12,12,512]{3,2,1,0:T(8,128)(2,1)S(1)} fusion(bf16[1,6,12,12,512]{4,3,2,1,0:T(8,128)(2,1)S(1)} %copy-done, bf16[512,512]{1,0:T(8,128)(2,1)} %param.10), kind=kOutput, calls=%fused_computation.5 | convolution fusion | flops 453427200 | bytes 2293760 | tf_op jit(solution)/shard_map/dot_general | solution.py:316
  3.1 0.1 collective-permute-start
  3.2 0.0 copy-done.6
  3.3 0.0 copy-done.4
  3.3 0.0 copy-start.5
  3.3 1.4 %collective-permute-done = bf16[1,1,12,12,512]{4,3,2,1,0:T(8,128)(2,1)S(1)} collective-permute-done((bf16[1,1,12,12,512]{4,3,2,1,0:T(8,128)(2,1)S(1)}, bf16[1,1,12,12,512]{4,3,2,1,0:T(8,128)(2,1)S(1)}, u32[]{:S(2)}, u32[]{:S(2)}) %collective-permute-start) | collective-permute-done | bytes 147488 | tf_op jit(solution)/shard_map/ppermute | solution.py:322
  4.7 0.2 maximum_bitcast_fusion
  5.0 0.6 pad_convert_fusion.e_ref
  5.5 4.8 %shard_map.91 = bf16[6,12,16,512]{3,2,1,0:T(8,128)(2,1)S(1)} custom-call(f32[8,14,16,512]{3,2,1,0:T(8,128)S(1)} %pad_convert_fusion.e_ref, f32[27,512]{1,0:T(8,128)S(1)} %convert_element_type.43.t_ref), custom_call_target="tpu_custom_call" | custom-call | tf_op jit(solution)/shard_map/pallas_call | solution.py:91
  10.4 0.5 multiply_reduce_fusion
  10.9 0.5 slice.8
  11.4 0.2 reshape.72.stream_ref
  11.6 0.0 copy-start.1
  11.6 0.1 rsqrt.12
  11.7 0.0 copy-done.5
  11.7 0.0 copy-start.7
  11.7 2.5 %convolution_convert_fusion.kv_ref = bf16[864,1024]{1,0:T(8,128)(2,1)S(1)} fusion(bf16[512,1536]{1,0:T(8,128)(2,1)} %ws_ref.1, bf16[864,512]{1,0:T(8,128)(2,1)S(1)} %reshape.72.stream_ref, f32[512]{0:T(512)S(1)} %convert_element_type.39, f32[864]{0:T(1024)S(1)} %rsqrt.12), kind=kOutput, calls=%fused_computation.3 | convolution fusion | flops 908623872 | bytes 3708288 | tf_op jit(solution)/shard_map/dot_general | solution.py:332
  14.3 0.0 copy-done.1
  14.3 0.0 copy-start.2
  14.3 0.2 collective-permute-start.1
  14.5 0.0 copy-done.7
  14.5 0.8 reshape.76
  15.4 2.7 %collective-permute-done.1.other_ref = bf16[864,1024]{1,0:T(8,128)(2,1)S(1)} collective-permute-done((bf16[864,1024]{1,0:T(8,128)(2,1)S(1)}, bf16[864,1024]{1,0:T(8,128)(2,1)S(1)}, u32[]{:S(2)}, u32[]{:S(2)}) %collective-permute-start.1) | collective-permute-done | bytes 1769504 | tf_op jit(solution)/shard_map/ppermute | solution.py:336
  18.1 0.0 copy-start.3
  18.1 0.0 copy-done.2
  18.1 1.2 copy-done.3
  19.3 102.0 %shard_map.92 = bf16[864,512]{1,0:T(8,128)(2,1)} custom-call(bf16[512,1536]{1,0:T(8,128)(2,1)} %ws_ref.1, f32[1,512]{1,0:T(1,128)} %bitcast.16, bf16[864,1024]{1,0:T(8,128)(2,1)} %copy-done.2, bf16[864,1024]{1,0:T(8,128)(2,1)} %copy-done.3, bf16[864,512]{1,0:T(8,128)(2,1)} %copy-done.1, bf16[512,512]{1,0:T(8,128)(2,1)} %wo_ref.1, f32[1,512]{1,0:T(1,128)} %bitcast.17, ...), custom_call_target="tpu_custom_call" | custom-call | tf_op jit(solution)/shard_map/pallas_call | solution.py:280
  121.3 2.2 %reshape.75 = bf16[1,6,12,12,512]{4,3,2,1,0:T(8,128)(2,1)} reshape(bf16[864,512]{1,0:T(8,128)(2,1)} %shard_map.92) | data formatting | bytes 1769472 | tf_op jit(solution)/shard_map/reshape | solution.py:341
  (5 shorter events, 0.1 us)
Async XLA Ops:
  0.0 1.3 %copy-start = (bf16[1,6,12,12,512]{4,3,2,1,0:T(8,128)(2,1)S(1)}, bf16[1,6,12,12,512]{4,3,2,1,0:T(8,128)(2,1)}, u32[]{:S(2)}) copy-start(bf16[1,6,12,12,512]{4,3,2,1,0:T(8,128)(2,1)} %param.9) | copy-start | bytes 2654212
  1.3 2.0 %copy-start.6 = (bf16[512]{0:T(512)(128)(2,1)S(1)}, bf16[512]{0:T(512)(128)(2,1)}, u32[]{:S(2)}) copy-start(bf16[512]{0:T(512)(128)(2,1)} %param.12) | copy-start | bytes 3076
  1.3 2.0 %copy-start.4 = (bf16[27,512]{1,0:T(8,128)(2,1)S(1)}, bf16[27,512]{1,0:T(8,128)(2,1)}, u32[]{:S(2)}) copy-start(bf16[27,512]{1,0:T(8,128)(2,1)} %param.11) | copy-start | bytes 82948
  3.1 1.5 %collective-permute-start = (bf16[1,1,12,12,512]{4,3,2,1,0:T(8,128)(2,1)S(1)}, bf16[1,1,12,12,512]{4,3,2,1,0:T(8,128)(2,1)S(1)}, u32[]{:S(2)}, u32[]{:S(2)}) collective-permute-start(bf16[1,1,12,12,512]{4,3,2,1,0:T(8,128)(2,1)S(1)} %dynamic-slice_bitcast_fusion), channel_id=1, source_target_pairs={{0,1},{1,0},{2,3},{3,2},{4,5},{5,4},{6,7},{7,6},{8,9},{9,8},{10,11... | collective-permute-start | bytes 442376 | tf_op jit(solution)/shard_map/ppermute | solution.py:322
  3.3 8.4 %copy-start.5 = (f32[512]{0:T(512)}, f32[512]{0:T(512)S(1)}, u32[]{:S(2)}) copy-start(f32[512]{0:T(512)S(1)} %convert_element_type.39) | copy-start | bytes 6148
  11.6 2.7 %copy-start.1 = (bf16[864,512]{1,0:T(8,128)(2,1)}, bf16[864,512]{1,0:T(8,128)(2,1)S(1)}, u32[]{:S(2)}) copy-start(bf16[864,512]{1,0:T(8,128)(2,1)S(1)} %reshape.72.stream_ref) | copy-start | bytes 2654212
  11.7 2.8 %copy-start.7 = (bf16[512]{0:T(512)(128)(2,1)S(1)}, bf16[512]{0:T(512)(128)(2,1)}, u32[]{:S(2)}) copy-start(bf16[512]{0:T(512)(128)(2,1)} %param.15) | copy-start | bytes 3076
  14.3 3.8 %copy-start.2 = (bf16[864,1024]{1,0:T(8,128)(2,1)}, bf16[864,1024]{1,0:T(8,128)(2,1)S(1)}, u32[]{:S(2)}) copy-start(bf16[864,1024]{1,0:T(8,128)(2,1)S(1)} %convolution_convert_fusion.kv_ref) | copy-start | bytes 5308420
  14.3 3.8 %collective-permute-start.1 = (bf16[864,1024]{1,0:T(8,128)(2,1)S(1)}, bf16[864,1024]{1,0:T(8,128)(2,1)S(1)}, u32[]{:S(2)}, u32[]{:S(2)}) collective-permute-start(bf16[864,1024]{1,0:T(8,128)(2,1)S(1)} %convolution_convert_fusion.kv_ref), channel_id=1, source_target_pairs={{0,1},{1,0},{2,3},{3,2},{4,5},{5,4},{6,7},{7,6},{8,9},{9,8},{10,11... | collective-permute-start | bytes 5308424 | tf_op jit(solution)/shard_map/ppermute | solution.py:336
  18.1 1.2 copy-start.3

commit v11 on v9

--- a/solution.py
+++ b/solution.py
@@ -263,7 +263,7 @@
 
 
 def block_tail(
-    query, keys_values, other, stream, out_space, gain_time, qkv_time, out_time, chunks=6
+    query, keys_values, other, stream, out_space, gain_time, qkv_time, out_time, chunks=3
 ):
     rows, width = stream.shape
     gain = gain_time.astype(jnp.float32).reshape(1, width)

time: 122 us -> 119 us (0.975)
  Pallas kernels: 105 us -> 103 us
    pallas_call x1, Pallas kernels: 100 us -> 97.7 us  [block_tail(): pl.pallas_call(functools.partial(block_kernel, chunks), out_shape=plane,...]
where the time goes in v11:
time: 119 us
  Pallas kernels  103 us (87%)
  matrix products  7.05 us (6%)
  local copies, waits for them, and re-layouts  5.47 us (5%)
  other arithmetic  2.12 us (2%)
  waiting for transfers between devices  1.51 us (1%)
    pallas_call x1, Pallas kernels, block_tail(): pl.pallas_call(functools.partial(block_kernel, chunks), out_shape=plane,...  97.7 us
    pallas_call x1, Pallas kernels, depthwise(): pl.pallas_call(conv_kernel, out_shape=jax.ShapeDtypeStruct((planes, grid,...  4.84 us
    dot_general x1, matrix products, local(): jnp.dot(flat, qkv_space[:, :width], preferred_element_type=jnp.float32)  2.66 us
    dot_general x1, matrix products, local(): jnp.dot(flat, qkv_space[:, width:], preferred_element_type=jnp.float32)  2.57 us
    unnamed x14, local copies, waits for them, and re-layouts  2.5 us
  transfers between devices with their start and end apart: 2, of which 2 were waited for; matrix products, arithmetic and copies ran while one was open for 3% of the time, Pallas kernels for 0%

profile of v11, /device:TPU:24, one launch (start us, length us, event | category | flops | bytes accessed | tf_op | source)
XLA Modules:
  0.0 119.2 jit_solution(15263987899514553058)
XLA Ops:
  0.0 0.0 copy-start
  0.0 1.3 %copy-done = bf16[1,6,12,12,512]{4,3,2,1,0:T(8,128)(2,1)S(1)} copy-done((bf16[1,6,12,12,512]{4,3,2,1,0:T(8,128)(2,1)S(1)}, bf16[1,6,12,12,512]{4,3,2,1,0:T(8,128)(2,1)}, u32[]{:S(2)}) %copy-start) | copy-done | bytes 884760
  1.3 0.0 copy-start.5
  1.3 0.0 copy-start.4
  1.3 1.8 %convolution_convert_fusion.1 = bf16[6,12,12,512]{3,2,1,0:T(8,128)(2,1)S(1)} fusion(bf16[1,6,12,12,512]{4,3,2,1,0:T(8,128)(2,1)S(1)} %copy-done, bf16[512,512]{1,0:T(8,128)(2,1)} %param.10), kind=kOutput, calls=%fused_computation.5 | convolution fusion | flops 453427200 | bytes 2293760 | tf_op jit(solution)/shard_map/dot_general | solution.py:308
  3.1 0.1 collective-permute-start
  3.2 0.0 copy-done.5
  3.3 0.0 copy-done.4
  3.3 1.4 %collective-permute-done = bf16[1,1,12,12,512]{4,3,2,1,0:T(8,128)(2,1)S(1)} collective-permute-done((bf16[1,1,12,12,512]{4,3,2,1,0:T(8,128)(2,1)S(1)}, bf16[1,1,12,12,512]{4,3,2,1,0:T(8,128)(2,1)S(1)}, u32[]{:S(2)}, u32[]{:S(2)}) %collective-permute-start) | collective-permute-done | bytes 147488 | tf_op jit(solution)/shard_map/ppermute | solution.py:314
  4.7 0.2 maximum_bitcast_fusion
  4.9 0.6 pad_convert_fusion.e_ref
  5.5 4.8 %shard_map.91 = bf16[6,12,16,512]{3,2,1,0:T(8,128)(2,1)S(1)} custom-call(f32[8,14,16,512]{3,2,1,0:T(8,128)S(1)} %pad_convert_fusion.e_ref, f32[27,512]{1,0:T(8,128)S(1)} %convert_element_type.44.t_ref), custom_call_target="tpu_custom_call" | custom-call | tf_op jit(solution)/shard_map/pallas_call | solution.py:91
  10.4 0.5 multiply_reduce_fusion
  10.9 0.5 slice.12
  11.4 0.2 reshape.68.stream_ref
  11.6 0.0 copy-start.1
  11.6 0.1 rsqrt.12
  11.7 0.0 copy-start.6
  11.7 2.6 %convolution_convert_fusion.kv_ref = bf16[864,1024]{1,0:T(8,128)(2,1)S(1)} fusion(bf16[512,1536]{1,0:T(8,128)(2,1)} %param.13, bf16[864,512]{1,0:T(8,128)(2,1)S(1)} %reshape.68.stream_ref, f32[512]{0:T(512)S(1)} %convert_element_type.47, f32[864]{0:T(1024)S(1)} %rsqrt.12), kind=kOutput, calls=%fused_computation.3 | convolution fusion | flops 908623872 | bytes 3708288 | tf_op jit(solution)/shard_map/dot_general | solution.py:324
  14.3 0.0 copy-start.2
  14.3 0.2 collective-permute-start.1
  14.5 0.0 copy-done.6
  14.5 0.8 reshape.72
  15.3 0.0 copy-done.1
  15.3 2.7 %convolution_convert_fusion.2.q_ref = bf16[864,512]{1,0:T(8,128)(2,1)} fusion(bf16[512,1536]{1,0:T(8,128)(2,1)} %param.13, bf16[864,512]{1,0:T(8,128)(2,1)S(1)} %reshape.68.stream_ref, f32[512]{0:T(512)S(1)} %convert_element_type.47, f32[864]{0:T(1024)S(1)} %rsqrt.12), kind=kOutput, calls=%fused_computation.6 | convolution fusion | flops 455196672 | bytes 2299264 | tf_op jit(solution)/shard_map/dot_general | solution.py:329
  18.0 0.0 copy-done.2
  18.0 0.1 collective-permute-done.1.other_ref
  18.1 0.0 copy-start.3
  18.1 1.2 %copy-done.3 = bf16[864,1024]{1,0:T(8,128)(2,1)} copy-done((bf16[864,1024]{1,0:T(8,128)(2,1)}, bf16[864,1024]{1,0:T(8,128)(2,1)S(1)}, u32[]{:S(2)}) %copy-start.3) | copy-done | bytes 1769496
  19.3 97.7 %shard_map.92 = bf16[864,512]{1,0:T(8,128)(2,1)} custom-call(bf16[864,512]{1,0:T(8,128)(2,1)} %convolution_convert_fusion.2.q_ref, bf16[864,1024]{1,0:T(8,128)(2,1)} %copy-done.2, bf16[864,1024]{1,0:T(8,128)(2,1)} %copy-done.3, bf16[864,512]{1,0:T(8,128)(2,1)} %copy-done.1, bf16[512,512]{1,0:T(8,128)(2,1)} %wo_ref.1, f32[1,512]{1,0:T(1,128)} %bitcast.15, ...), custom_call_target="tpu_custom_call" | custom-call | tf_op jit(solution)/shard_map/pallas_call | solution.py:272
  117.0 2.2 %reshape.71 = bf16[1,6,12,12,512]{4,3,2,1,0:T(8,128)(2,1)} reshape(bf16[864,512]{1,0:T(8,128)(2,1)} %shard_map.92) | data formatting | bytes 1769472 | tf_op jit(solution)/shard_map/reshape | solution.py:336
  (5 shorter events, 0.1 us)
Async XLA Ops:
  0.0 1.3 %copy-start = (bf16[1,6,12,12,512]{4,3,2,1,0:T(8,128)(2,1)S(1)}, bf16[1,6,12,12,512]{4,3,2,1,0:T(8,128)(2,1)}, u32[]{:S(2)}) copy-start(bf16[1,6,12,12,512]{4,3,2,1,0:T(8,128)(2,1)} %param.9) | copy-start | bytes 2654212
  1.3 2.0 %copy-start.5 = (bf16[512]{0:T(512)(128)(2,1)S(1)}, bf16[512]{0:T(512)(128)(2,1)}, u32[]{:S(2)}) copy-start(bf16[512]{0:T(512)(128)(2,1)} %param.12) | copy-start | bytes 3076
  1.3 2.0 %copy-start.4 = (bf16[27,512]{1,0:T(8,128)(2,1)S(1)}, bf16[27,512]{1,0:T(8,128)(2,1)}, u32[]{:S(2)}) copy-start(bf16[27,512]{1,0:T(8,128)(2,1)} %param.11) | copy-start | bytes 82948
  3.1 1.5 %collective-permute-start = (bf16[1,1,12,12,512]{4,3,2,1,0:T(8,128)(2,1)S(1)}, bf16[1,1,12,12,512]{4,3,2,1,0:T(8,128)(2,1)S(1)}, u32[]{:S(2)}, u32[]{:S(2)}) collective-permute-start(bf16[1,1,12,12,512]{4,3,2,1,0:T(8,128)(2,1)S(1)} %dynamic-slice_bitcast_fusion), channel_id=1, source_target_pairs={{0,1},{1,0},{2,3},{3,2},{4,5},{5,4},{6,7},{7,6},{8,9},{9,8},{10,11... | collective-permute-start | bytes 442376 | tf_op jit(solution)/shard_map/ppermute | solution.py:314
  11.6 3.7 %copy-start.1 = (bf16[864,512]{1,0:T(8,128)(2,1)}, bf16[864,512]{1,0:T(8,128)(2,1)S(1)}, u32[]{:S(2)}) copy-start(bf16[864,512]{1,0:T(8,128)(2,1)S(1)} %reshape.68.stream_ref) | copy-start | bytes 2654212
  11.7 2.8 %copy-start.6 = (bf16[512]{0:T(512)(128)(2,1)S(1)}, bf16[512]{0:T(512)(128)(2,1)}, u32[]{:S(2)}) copy-start(bf16[512]{0:T(512)(128)(2,1)} %param.15) | copy-start | bytes 3076
  14.3 3.7 %copy-start.2 = (bf16[864,1024]{1,0:T(8,128)(2,1)}, bf16[864,1024]{1,0:T(8,128)(2,1)S(1)}, u32[]{:S(2)}) copy-start(bf16[864,1024]{1,0:T(8,128)(2,1)S(1)} %convolution_convert_fusion.kv_ref) | copy-start | bytes 5308420
  14.3 3.8 %collective-permute-start.1 = (bf16[864,1024]{1,0:T(8,128)(2,1)S(1)}, bf16[864,1024]{1,0:T(8,128)(2,1)S(1)}, u32[]{:S(2)}, u32[]{:S(2)}) collective-permute-start(bf16[864,1024]{1,0:T(8,128)(2,1)S(1)} %convolution_convert_fusion.kv_ref), channel_id=1, source_target_pairs={{0,1},{1,0},{2,3},{3,2},{4,5},{5,4},{6,7},{7,6},{8,9},{9,8},{10,11... | collective-permute-start | bytes 5308424 | tf_op jit(solution)/shard_map/ppermute | solution.py:328
  18.1 1.2 %copy-start.3 = (bf16[864,1024]{1,0:T(8,128)(2,1)}, bf16[864,1024]{1,0:T(8,128)(2,1)S(1)}, u32[]{:S(2)}) copy-start(bf16[864,1024]{1,0:T(8,128)(2,1)S(1)} %collective-permute-done.1.other_ref) | copy-start | bytes 5308420

commit v12 on v11

--- a/solution.py
+++ b/solution.py
@@ -263,7 +263,7 @@
 
 
 def block_tail(
-    query, keys_values, other, stream, out_space, gain_time, qkv_time, out_time, chunks=3
+    query, keys_values, other, stream, out_space, gain_time, qkv_time, out_time, chunks=2
 ):
     rows, width = stream.shape
     gain = gain_time.astype(jnp.float32).reshape(1, width)

time: 119 us -> 125 us (1.050)
  Pallas kernels: 103 us -> 108 us
    pallas_call x1, Pallas kernels: 97.7 us -> 103 us  [block_tail(): pl.pallas_call(functools.partial(block_kernel, chunks), out_shape=plane,...]
where the time goes in v12:
time: 125 us; the launch traced here: 124 us
  Pallas kernels  108 us (86%)
  matrix products  7.05 us (6%)
  local copies, waits for them, and re-layouts  5.47 us (4%)
  other arithmetic  2.12 us (2%)
  waiting for transfers between devices  1.51 us (1%)
    pallas_call x1, Pallas kernels, block_tail(): pl.pallas_call(functools.partial(block_kernel, chunks), out_shape=plane,...  103 us
    pallas_call x1, Pallas kernels, depthwise(): pl.pallas_call(conv_kernel, out_shape=jax.ShapeDtypeStruct((planes, grid,...  4.84 us
    dot_general x1, matrix products, local(): jnp.dot(flat, qkv_space[:, :width], preferred_element_type=jnp.float32)  2.66 us
    dot_general x1, matrix products, local(): jnp.dot(flat, qkv_space[:, width:], preferred_element_type=jnp.float32)  2.57 us
    unnamed x14, local copies, waits for them, and re-layouts  2.5 us
  transfers between devices with their start and end apart: 2, of which 2 were waited for; matrix products, arithmetic and copies ran while one was open for 3% of the time, Pallas kernels for 0%

profile of v12, /device:TPU:24, one launch (start us, length us, event | category | flops | bytes accessed | tf_op | source)
XLA Modules:
  0.0 124.3 jit_solution(2825560196892843909)
XLA Ops:
  0.0 0.0 copy-start
  0.0 1.3 %copy-done = bf16[1,6,12,12,512]{4,3,2,1,0:T(8,128)(2,1)S(1)} copy-done((bf16[1,6,12,12,512]{4,3,2,1,0:T(8,128)(2,1)S(1)}, bf16[1,6,12,12,512]{4,3,2,1,0:T(8,128)(2,1)}, u32[]{:S(2)}) %copy-start) | copy-done | bytes 884760
  1.3 0.0 copy-start.5
  1.3 0.0 copy-start.4
  1.3 1.8 %convolution_convert_fusion.1 = bf16[6,12,12,512]{3,2,1,0:T(8,128)(2,1)S(1)} fusion(bf16[1,6,12,12,512]{4,3,2,1,0:T(8,128)(2,1)S(1)} %copy-done, bf16[512,512]{1,0:T(8,128)(2,1)} %param.10), kind=kOutput, calls=%fused_computation.5 | convolution fusion | flops 453427200 | bytes 2293760 | tf_op jit(solution)/shard_map/dot_general | solution.py:308
  3.1 0.1 collective-permute-start
  3.2 0.0 copy-done.5
  3.3 0.0 copy-done.4
  3.3 1.4 %collective-permute-done = bf16[1,1,12,12,512]{4,3,2,1,0:T(8,128)(2,1)S(1)} collective-permute-done((bf16[1,1,12,12,512]{4,3,2,1,0:T(8,128)(2,1)S(1)}, bf16[1,1,12,12,512]{4,3,2,1,0:T(8,128)(2,1)S(1)}, u32[]{:S(2)}, u32[]{:S(2)}) %collective-permute-start) | collective-permute-done | bytes 147488 | tf_op jit(solution)/shard_map/ppermute | solution.py:314
  4.7 0.2 maximum_bitcast_fusion
  4.9 0.6 pad_convert_fusion.e_ref
  5.5 4.8 %shard_map.91 = bf16[6,12,16,512]{3,2,1,0:T(8,128)(2,1)S(1)} custom-call(f32[8,14,16,512]{3,2,1,0:T(8,128)S(1)} %pad_convert_fusion.e_ref, f32[27,512]{1,0:T(8,128)S(1)} %convert_element_type.44.t_ref), custom_call_target="tpu_custom_call" | custom-call | tf_op jit(solution)/shard_map/pallas_call | solution.py:91
  10.4 0.5 multiply_reduce_fusion
  10.9 0.5 slice.12
  11.4 0.2 reshape.68.stream_ref
  11.6 0.0 copy-start.1
  11.6 0.1 rsqrt.12
  11.7 0.0 copy-start.6
  11.7 2.6 %convolution_convert_fusion.kv_ref = bf16[864,1024]{1,0:T(8,128)(2,1)S(1)} fusion(bf16[512,1536]{1,0:T(8,128)(2,1)} %param.13, bf16[864,512]{1,0:T(8,128)(2,1)S(1)} %reshape.68.stream_ref, f32[512]{0:T(512)S(1)} %convert_element_type.47, f32[864]{0:T(1024)S(1)} %rsqrt.12), kind=kOutput, calls=%fused_computation.3 | convolution fusion | flops 908623872 | bytes 3708288 | tf_op jit(solution)/shard_map/dot_general | solution.py:324
  14.3 0.0 copy-start.2
  14.3 0.2 collective-permute-start.1
  14.5 0.0 copy-done.6
  14.5 0.8 reshape.72
  15.3 0.0 copy-done.1
  15.3 2.7 %convolution_convert_fusion.2.q_ref = bf16[864,512]{1,0:T(8,128)(2,1)} fusion(bf16[512,1536]{1,0:T(8,128)(2,1)} %param.13, bf16[864,512]{1,0:T(8,128)(2,1)S(1)} %reshape.68.stream_ref, f32[512]{0:T(512)S(1)} %convert_element_type.47, f32[864]{0:T(1024)S(1)} %rsqrt.12), kind=kOutput, calls=%fused_computation.6 | convolution fusion | flops 455196672 | bytes 2299264 | tf_op jit(solution)/shard_map/dot_general | solution.py:329
  18.0 0.0 copy-done.2
  18.0 0.1 collective-permute-done.1.other_ref
  18.1 0.0 copy-start.3
  18.1 1.2 copy-done.3
  19.3 102.9 %shard_map.92 = bf16[864,512]{1,0:T(8,128)(2,1)} custom-call(bf16[864,512]{1,0:T(8,128)(2,1)} %convolution_convert_fusion.2.q_ref, bf16[864,1024]{1,0:T(8,128)(2,1)} %copy-done.2, bf16[864,1024]{1,0:T(8,128)(2,1)} %copy-done.3, bf16[864,512]{1,0:T(8,128)(2,1)} %copy-done.1, bf16[512,512]{1,0:T(8,128)(2,1)} %wo_ref.1, f32[1,512]{1,0:T(1,128)} %bitcast.15, ...), custom_call_target="tpu_custom_call" | custom-call | tf_op jit(solution)/shard_map/pallas_call | solution.py:272
  122.2 2.2 %reshape.71 = bf16[1,6,12,12,512]{4,3,2,1,0:T(8,128)(2,1)} reshape(bf16[864,512]{1,0:T(8,128)(2,1)} %shard_map.92) | data formatting | bytes 1769472 | tf_op jit(solution)/shard_map/reshape | solution.py:336
  (5 shorter events, 0.1 us)
Async XLA Ops:
  0.0 1.3 %copy-start = (bf16[1,6,12,12,512]{4,3,2,1,0:T(8,128)(2,1)S(1)}, bf16[1,6,12,12,512]{4,3,2,1,0:T(8,128)(2,1)}, u32[]{:S(2)}) copy-start(bf16[1,6,12,12,512]{4,3,2,1,0:T(8,128)(2,1)} %param.9) | copy-start | bytes 2654212
  1.3 2.0 %copy-start.5 = (bf16[512]{0:T(512)(128)(2,1)S(1)}, bf16[512]{0:T(512)(128)(2,1)}, u32[]{:S(2)}) copy-start(bf16[512]{0:T(512)(128)(2,1)} %param.12) | copy-start | bytes 3076
  1.3 2.0 %copy-start.4 = (bf16[27,512]{1,0:T(8,128)(2,1)S(1)}, bf16[27,512]{1,0:T(8,128)(2,1)}, u32[]{:S(2)}) copy-start(bf16[27,512]{1,0:T(8,128)(2,1)} %param.11) | copy-start | bytes 82948
  3.1 1.5 %collective-permute-start = (bf16[1,1,12,12,512]{4,3,2,1,0:T(8,128)(2,1)S(1)}, bf16[1,1,12,12,512]{4,3,2,1,0:T(8,128)(2,1)S(1)}, u32[]{:S(2)}, u32[]{:S(2)}) collective-permute-start(bf16[1,1,12,12,512]{4,3,2,1,0:T(8,128)(2,1)S(1)} %dynamic-slice_bitcast_fusion), channel_id=1, source_target_pairs={{0,1},{1,0},{2,3},{3,2},{4,5},{5,4},{6,7},{7,6},{8,9},{9,8},{10,11... | collective-permute-start | bytes 442376 | tf_op jit(solution)/shard_map/ppermute | solution.py:314
  11.6 3.7 %copy-start.1 = (bf16[864,512]{1,0:T(8,128)(2,1)}, bf16[864,512]{1,0:T(8,128)(2,1)S(1)}, u32[]{:S(2)}) copy-start(bf16[864,512]{1,0:T(8,128)(2,1)S(1)} %reshape.68.stream_ref) | copy-start | bytes 2654212
  11.7 2.8 %copy-start.6 = (bf16[512]{0:T(512)(128)(2,1)S(1)}, bf16[512]{0:T(512)(128)(2,1)}, u32[]{:S(2)}) copy-start(bf16[512]{0:T(512)(128)(2,1)} %param.15) | copy-start | bytes 3076
  14.3 3.7 %copy-start.2 = (bf16[864,1024]{1,0:T(8,128)(2,1)}, bf16[864,1024]{1,0:T(8,128)(2,1)S(1)}, u32[]{:S(2)}) copy-start(bf16[864,1024]{1,0:T(8,128)(2,1)S(1)} %convolution_convert_fusion.kv_ref) | copy-start | bytes 5308420
  14.3 3.8 %collective-permute-start.1 = (bf16[864,1024]{1,0:T(8,128)(2,1)S(1)}, bf16[864,1024]{1,0:T(8,128)(2,1)S(1)}, u32[]{:S(2)}, u32[]{:S(2)}) collective-permute-start(bf16[864,1024]{1,0:T(8,128)(2,1)S(1)} %convolution_convert_fusion.kv_ref), channel_id=1, source_target_pairs={{0,1},{1,0},{2,3},{3,2},{4,5},{5,4},{6,7},{7,6},{8,9},{9,8},{10,11... | collective-permute-start | bytes 5308424 | tf_op jit(solution)/shard_map/ppermute | solution.py:328
  18.1 1.2 copy-start.3

commit v13 on v11

--- a/solution.py
+++ b/solution.py
@@ -71,13 +71,13 @@
             for dz in range(3):
                 for dy in range(3):
                     tap = t_ref[pl.ds(9 * dz + 3 * dy + dx, 1), :]
-                    term = e_ref[z + dz, dy:dy + rows] * tap
+                    term = e_ref[z + dz, dy:dy + rows].astype(jnp.float32) * tap
                     acc = term if acc is None else acc + term
             parts.append(acc)
         conv = (
             pltpu.roll(parts[0], 1, 1) + parts[1] + pltpu.roll(parts[2], lanes_x - 1, 1)
         )
-        o_ref[z] = (e_ref[z + 1, 1:1 + rows] + conv).astype(o_ref.dtype)
+        o_ref[z] = (e_ref[z + 1, 1:1 + rows].astype(jnp.float32) + conv).astype(o_ref.dtype)
         return carry
 
     lax.fori_loop(0, planes, plane, 0)
@@ -86,7 +86,7 @@
 def depthwise(ext, taps):
     depth, grid, _, width = ext.shape
     planes = depth - 2
-    padded = jnp.pad(ext.astype(jnp.float32), ((0, 0), (1, 1), (1, 3), (0, 0)))
+    padded = jnp.pad(ext, ((0, 0), (1, 1), (1, 3), (0, 0)))
     vmem = pl.BlockSpec(memory_space=pltpu.VMEM)
     out = pl.pallas_call(
         conv_kernel,

time: 119 us -> 120 us (level)
  no operation moved by 1% of the time
where the time goes in v13:
time: 120 us
  Pallas kernels  103 us (86%)
  matrix products  7.05 us (6%)
  local copies, waits for them, and re-layouts  6.2 us (5%)
  other arithmetic  1.54 us (1%)
  waiting for transfers between devices  1.5 us (1%)
    pallas_call x1, Pallas kernels, block_tail(): pl.pallas_call(functools.partial(block_kernel, chunks), out_shape=plane,...  97.7 us
    pallas_call x1, Pallas kernels, depthwise(): pl.pallas_call(conv_kernel, out_shape=jax.ShapeDtypeStruct((planes, grid,...  5.43 us
    dot_general x1, matrix products, local(): jnp.dot(flat, qkv_space[:, :width], preferred_element_type=jnp.float32)  2.66 us
    dot_general x1, matrix products, local(): jnp.dot(flat, qkv_space[:, width:], preferred_element_type=jnp.float32)  2.57 us
    unnamed x14, local copies, waits for them, and re-layouts  2.5 us
  transfers between devices with their start and end apart: 2, of which 2 were waited for; matrix products, arithmetic and copies ran while one was open for 3% of the time, Pallas kernels for 0%

profile of v13, /device:TPU:24, one launch (start us, length us, event | category | flops | bytes accessed | tf_op | source)
XLA Modules:
  0.0 119.9 jit_solution(288485429674329050)
XLA Ops:
  0.0 0.0 copy-start
  0.0 1.3 %copy-done = bf16[1,6,12,12,512]{4,3,2,1,0:T(8,128)(2,1)S(1)} copy-done((bf16[1,6,12,12,512]{4,3,2,1,0:T(8,128)(2,1)S(1)}, bf16[1,6,12,12,512]{4,3,2,1,0:T(8,128)(2,1)}, u32[]{:S(2)}) %copy-start) | copy-done | bytes 884760
  1.3 0.0 copy-start.5
  1.3 0.0 copy-start.4
  1.3 1.8 %convolution_convert_fusion.1 = bf16[6,12,12,512]{3,2,1,0:T(8,128)(2,1)S(1)} fusion(bf16[1,6,12,12,512]{4,3,2,1,0:T(8,128)(2,1)S(1)} %copy-done, bf16[512,512]{1,0:T(8,128)(2,1)} %param.10), kind=kOutput, calls=%fused_computation.4 | convolution fusion | flops 453427200 | bytes 2293760 | tf_op jit(solution)/shard_map/dot_general | solution.py:308
  3.1 0.1 collective-permute-start
  3.2 0.0 copy-done.5
  3.3 0.0 copy-done.4
  3.3 1.4 %collective-permute-done = bf16[1,1,12,12,512]{4,3,2,1,0:T(8,128)(2,1)S(1)} collective-permute-done((bf16[1,1,12,12,512]{4,3,2,1,0:T(8,128)(2,1)S(1)}, bf16[1,1,12,12,512]{4,3,2,1,0:T(8,128)(2,1)S(1)}, u32[]{:S(2)}, u32[]{:S(2)}) %collective-permute-start) | collective-permute-done | bytes 147488 | tf_op jit(solution)/shard_map/ppermute | solution.py:314
  4.7 0.2 maximum_bitcast_fusion
  4.9 0.7 pad.4.e_ref
  5.7 5.4 %shard_map.91 = bf16[6,12,16,512]{3,2,1,0:T(8,128)(2,1)S(1)} custom-call(bf16[8,14,16,512]{3,2,1,0:T(8,128)(2,1)S(1)} %pad.4.e_ref, f32[27,512]{1,0:T(8,128)S(1)} %convert_element_type.39.t_ref), custom_call_target="tpu_custom_call" | custom-call | tf_op jit(solution)/shard_map/pallas_call | solution.py:91
  11.1 0.5 multiply_reduce_fusion
  11.6 0.5 slice.12
  12.1 0.2 reshape.66.stream_ref
  12.3 0.0 copy-start.1
  12.4 0.1 rsqrt.12
  12.5 0.0 copy-start.6
  12.5 2.6 %convolution_convert_fusion.kv_ref = bf16[864,1024]{1,0:T(8,128)(2,1)S(1)} fusion(bf16[512,1536]{1,0:T(8,128)(2,1)} %param.13, bf16[864,512]{1,0:T(8,128)(2,1)S(1)} %reshape.66.stream_ref, f32[512]{0:T(512)S(1)} %convert_element_type.42, f32[864]{0:T(1024)S(1)} %rsqrt.12), kind=kOutput, calls=%fused_computation.2 | convolution fusion | flops 908623872 | bytes 3708288 | tf_op jit(solution)/shard_map/dot_general | solution.py:324
  15.0 0.0 copy-start.2
  15.0 0.2 collective-permute-start.1
  15.3 0.0 copy-done.6
  15.3 0.8 reshape.70
  16.0 0.0 copy-done.1
  16.0 2.7 %convolution_convert_fusion.2.q_ref = bf16[864,512]{1,0:T(8,128)(2,1)} fusion(bf16[512,1536]{1,0:T(8,128)(2,1)} %param.13, bf16[864,512]{1,0:T(8,128)(2,1)S(1)} %reshape.66.stream_ref, f32[512]{0:T(512)S(1)} %convert_element_type.42, f32[864]{0:T(1024)S(1)} %rsqrt.12), kind=kOutput, calls=%fused_computation.5 | convolution fusion | flops 455196672 | bytes 2299264 | tf_op jit(solution)/shard_map/dot_general | solution.py:329
  18.7 0.0 copy-done.2
  18.7 0.1 collective-permute-done.1.other_ref
  18.8 0.0 copy-start.3
  18.8 1.2 %copy-done.3 = bf16[864,1024]{1,0:T(8,128)(2,1)} copy-done((bf16[864,1024]{1,0:T(8,128)(2,1)}, bf16[864,1024]{1,0:T(8,128)(2,1)S(1)}, u32[]{:S(2)}) %copy-start.3) | copy-done | bytes 1769496
  20.0 97.7 %shard_map.92 = bf16[864,512]{1,0:T(8,128)(2,1)} custom-call(bf16[864,512]{1,0:T(8,128)(2,1)} %convolution_convert_fusion.2.q_ref, bf16[864,1024]{1,0:T(8,128)(2,1)} %copy-done.2, bf16[864,1024]{1,0:T(8,128)(2,1)} %copy-done.3, bf16[864,512]{1,0:T(8,128)(2,1)} %copy-done.1, bf16[512,512]{1,0:T(8,128)(2,1)} %wo_ref.1, f32[1,512]{1,0:T(1,128)} %bitcast.15, ...), custom_call_target="tpu_custom_call" | custom-call | tf_op jit(solution)/shard_map/pallas_call | solution.py:272
  117.8 2.2 %reshape.69 = bf16[1,6,12,12,512]{4,3,2,1,0:T(8,128)(2,1)} reshape(bf16[864,512]{1,0:T(8,128)(2,1)} %shard_map.92) | data formatting | bytes 1769472 | tf_op jit(solution)/shard_map/reshape | solution.py:336
  (5 shorter events, 0.1 us)
Async XLA Ops:
  0.0 1.3 %copy-start = (bf16[1,6,12,12,512]{4,3,2,1,0:T(8,128)(2,1)S(1)}, bf16[1,6,12,12,512]{4,3,2,1,0:T(8,128)(2,1)}, u32[]{:S(2)}) copy-start(bf16[1,6,12,12,512]{4,3,2,1,0:T(8,128)(2,1)} %param.9) | copy-start | bytes 2654212
  1.3 2.0 %copy-start.5 = (bf16[512]{0:T(512)(128)(2,1)S(1)}, bf16[512]{0:T(512)(128)(2,1)}, u32[]{:S(2)}) copy-start(bf16[512]{0:T(512)(128)(2,1)} %param.12) | copy-start | bytes 3076
  1.3 2.0 %copy-start.4 = (bf16[27,512]{1,0:T(8,128)(2,1)S(1)}, bf16[27,512]{1,0:T(8,128)(2,1)}, u32[]{:S(2)}) copy-start(bf16[27,512]{1,0:T(8,128)(2,1)} %param.11) | copy-start | bytes 82948
  3.1 1.5 %collective-permute-start = (bf16[1,1,12,12,512]{4,3,2,1,0:T(8,128)(2,1)S(1)}, bf16[1,1,12,12,512]{4,3,2,1,0:T(8,128)(2,1)S(1)}, u32[]{:S(2)}, u32[]{:S(2)}) collective-permute-start(bf16[1,1,12,12,512]{4,3,2,1,0:T(8,128)(2,1)S(1)} %dynamic-slice_bitcast_fusion), channel_id=1, source_target_pairs={{0,1},{1,0},{2,3},{3,2},{4,5},{5,4},{6,7},{7,6},{8,9},{9,8},{10,11... | collective-permute-start | bytes 442376 | tf_op jit(solution)/shard_map/ppermute | solution.py:314
  12.3 3.7 %copy-start.1 = (bf16[864,512]{1,0:T(8,128)(2,1)}, bf16[864,512]{1,0:T(8,128)(2,1)S(1)}, u32[]{:S(2)}) copy-start(bf16[864,512]{1,0:T(8,128)(2,1)S(1)} %reshape.66.stream_ref) | copy-start | bytes 2654212
  12.5 2.8 %copy-start.6 = (bf16[512]{0:T(512)(128)(2,1)S(1)}, bf16[512]{0:T(512)(128)(2,1)}, u32[]{:S(2)}) copy-start(bf16[512]{0:T(512)(128)(2,1)} %param.15) | copy-start | bytes 3076
  15.0 3.7 %copy-start.2 = (bf16[864,1024]{1,0:T(8,128)(2,1)}, bf16[864,1024]{1,0:T(8,128)(2,1)S(1)}, u32[]{:S(2)}) copy-start(bf16[864,1024]{1,0:T(8,128)(2,1)S(1)} %convolution_convert_fusion.kv_ref) | copy-start | bytes 5308420
  15.0 3.8 %collective-permute-start.1 = (bf16[864,1024]{1,0:T(8,128)(2,1)S(1)}, bf16[864,1024]{1,0:T(8,128)(2,1)S(1)}, u32[]{:S(2)}, u32[]{:S(2)}) collective-permute-start(bf16[864,1024]{1,0:T(8,128)(2,1)S(1)} %convolution_convert_fusion.kv_ref), channel_id=1, source_target_pairs={{0,1},{1,0},{2,3},{3,2},{4,5},{5,4},{6,7},{7,6},{8,9},{9,8},{10,11... | collective-permute-start | bytes 5308424 | tf_op jit(solution)/shard_map/ppermute | solution.py:328
  18.8 1.2 %copy-start.3 = (bf16[864,1024]{1,0:T(8,128)(2,1)}, bf16[864,1024]{1,0:T(8,128)(2,1)S(1)}, u32[]{:S(2)}) copy-start(bf16[864,1024]{1,0:T(8,128)(2,1)S(1)} %collective-permute-done.1.other_ref) | copy-start | bytes 5308420

commit v14 on v11

--- a/solution.py
+++ b/solution.py
@@ -190,23 +190,26 @@
                 (other_ref[:, cols], other_ref[:, key_cols]),
             )
             outs = []
-            for mask in (first_half, jnp.logical_not(first_half)):
-                q_one = jnp.where(mask, q, jnp.zeros_like(q))
+            for half in range(2):
+                part_lanes = slice(half * head_size, (half + 1) * head_size)
+                q_one = q[:, part_lanes]
                 rowsum = None
                 mixed_one = None
                 for k, v in sources:
                     scores = lax.dot_general(
-                        q_one, k, (((1,), (1,)), ((), ())), preferred_element_type=jnp.float32
+                        q_one, k[:, part_lanes], (((1,), (1,)), ((), ())),
+                        preferred_element_type=jnp.float32,
                     ) * scale
                     expo = jnp.exp(scores)
                     part_sum = jnp.sum(expo, axis=-1, keepdims=True)
                     part = jnp.dot(
-                        expo.astype(jnp.bfloat16), v, preferred_element_type=jnp.float32
+                        expo.astype(jnp.bfloat16), v[:, part_lanes],
+                        preferred_element_type=jnp.float32,
                     )
                     rowsum = part_sum if rowsum is None else rowsum + part_sum
                     mixed_one = part if mixed_one is None else mixed_one + part
                 outs.append(mixed_one / rowsum)
-            pieces.append(jnp.where(first_half, outs[0], outs[1]).astype(jnp.bfloat16))
+            pieces.append(jnp.concatenate(outs, axis=1).astype(jnp.bfloat16))
         spatial = jnp.concatenate(pieces, axis=1)
         stream2 = (
             stream_ref[span, :].astype(jnp.float32)

time: 119 us -> 120 us (level)
  no operation moved by 1% of the time
where the time goes in v14:
time: 120 us
  Pallas kernels  103 us (86%)
  matrix products  7.05 us (6%)
  local copies, waits for them, and re-layouts  5.47 us (5%)
  other arithmetic  2.12 us (2%)
  waiting for transfers between devices  1.51 us (1%)
    pallas_call x1, Pallas kernels, block_tail(): pl.pallas_call(functools.partial(block_kernel, chunks), out_shape=plane,...  98.4 us
    pallas_call x1, Pallas kernels, depthwise(): pl.pallas_call(conv_kernel, out_shape=jax.ShapeDtypeStruct((planes, grid,...  4.84 us
    dot_general x1, matrix products, local(): jnp.dot(flat, qkv_space[:, :width], preferred_element_type=jnp.float32)  2.66 us
    dot_general x1, matrix products, local(): jnp.dot(flat, qkv_space[:, width:], preferred_element_type=jnp.float32)  2.57 us
    unnamed x14, local copies, waits for them, and re-layouts  2.5 us
  transfers between devices with their start and end apart: 2, of which 2 were waited for; matrix products, arithmetic and copies ran while one was open for 3% of the time, Pallas kernels for 0%

profile of v14, /device:TPU:24, one launch (start us, length us, event | category | flops | bytes accessed | tf_op | source)
XLA Modules:
  0.0 119.8 jit_solution(10740473711722712446)
XLA Ops:
  0.0 0.0 copy-start
  0.0 1.3 %copy-done = bf16[1,6,12,12,512]{4,3,2,1,0:T(8,128)(2,1)S(1)} copy-done((bf16[1,6,12,12,512]{4,3,2,1,0:T(8,128)(2,1)S(1)}, bf16[1,6,12,12,512]{4,3,2,1,0:T(8,128)(2,1)}, u32[]{:S(2)}) %copy-start) | copy-done | bytes 884760
  1.3 0.0 copy-start.5
  1.3 0.0 copy-start.4
  1.3 1.8 %convolution_convert_fusion.1 = bf16[6,12,12,512]{3,2,1,0:T(8,128)(2,1)S(1)} fusion(bf16[1,6,12,12,512]{4,3,2,1,0:T(8,128)(2,1)S(1)} %copy-done, bf16[512,512]{1,0:T(8,128)(2,1)} %param.10), kind=kOutput, calls=%fused_computation.5 | convolution fusion | flops 453427200 | bytes 2293760 | tf_op jit(solution)/shard_map/dot_general | solution.py:311
  3.1 0.1 collective-permute-start
  3.2 0.0 copy-done.5
  3.3 0.0 copy-done.4
  3.3 1.4 %collective-permute-done = bf16[1,1,12,12,512]{4,3,2,1,0:T(8,128)(2,1)S(1)} collective-permute-done((bf16[1,1,12,12,512]{4,3,2,1,0:T(8,128)(2,1)S(1)}, bf16[1,1,12,12,512]{4,3,2,1,0:T(8,128)(2,1)S(1)}, u32[]{:S(2)}, u32[]{:S(2)}) %collective-permute-start) | collective-permute-done | bytes 147488 | tf_op jit(solution)/shard_map/ppermute | solution.py:317
  4.7 0.2 maximum_bitcast_fusion
  4.9 0.6 pad_convert_fusion.e_ref
  5.5 4.8 %shard_map.91 = bf16[6,12,16,512]{3,2,1,0:T(8,128)(2,1)S(1)} custom-call(f32[8,14,16,512]{3,2,1,0:T(8,128)S(1)} %pad_convert_fusion.e_ref, f32[27,512]{1,0:T(8,128)S(1)} %convert_element_type.44.t_ref), custom_call_target="tpu_custom_call" | custom-call | tf_op jit(solution)/shard_map/pallas_call | solution.py:91
  10.4 0.5 multiply_reduce_fusion
  10.9 0.5 slice.12
  11.4 0.2 reshape.68.stream_ref
  11.6 0.0 copy-start.1
  11.6 0.1 rsqrt.12
  11.7 0.0 copy-start.6
  11.7 2.6 %convolution_convert_fusion.kv_ref = bf16[864,1024]{1,0:T(8,128)(2,1)S(1)} fusion(bf16[512,1536]{1,0:T(8,128)(2,1)} %param.13, bf16[864,512]{1,0:T(8,128)(2,1)S(1)} %reshape.68.stream_ref, f32[512]{0:T(512)S(1)} %convert_element_type.47, f32[864]{0:T(1024)S(1)} %rsqrt.12), kind=kOutput, calls=%fused_computation.3 | convolution fusion | flops 908623872 | bytes 3708288 | tf_op jit(solution)/shard_map/dot_general | solution.py:327
  14.3 0.0 copy-start.2
  14.3 0.2 collective-permute-start.1
  14.5 0.0 copy-done.6
  14.5 0.8 reshape.72
  15.3 0.0 copy-done.1
  15.3 2.7 %convolution_convert_fusion.2.q_ref = bf16[864,512]{1,0:T(8,128)(2,1)} fusion(bf16[512,1536]{1,0:T(8,128)(2,1)} %param.13, bf16[864,512]{1,0:T(8,128)(2,1)S(1)} %reshape.68.stream_ref, f32[512]{0:T(512)S(1)} %convert_element_type.47, f32[864]{0:T(1024)S(1)} %rsqrt.12), kind=kOutput, calls=%fused_computation.6 | convolution fusion | flops 455196672 | bytes 2299264 | tf_op jit(solution)/shard_map/dot_general | solution.py:332
  18.0 0.0 copy-done.2
  18.0 0.1 collective-permute-done.1.other_ref
  18.1 0.0 copy-start.3
  18.1 1.2 %copy-done.3 = bf16[864,1024]{1,0:T(8,128)(2,1)} copy-done((bf16[864,1024]{1,0:T(8,128)(2,1)}, bf16[864,1024]{1,0:T(8,128)(2,1)S(1)}, u32[]{:S(2)}) %copy-start.3) | copy-done | bytes 1769496
  19.3 98.4 %shard_map.92 = bf16[864,512]{1,0:T(8,128)(2,1)} custom-call(bf16[864,512]{1,0:T(8,128)(2,1)} %convolution_convert_fusion.2.q_ref, bf16[864,1024]{1,0:T(8,128)(2,1)} %copy-done.2, bf16[864,1024]{1,0:T(8,128)(2,1)} %copy-done.3, bf16[864,512]{1,0:T(8,128)(2,1)} %copy-done.1, bf16[512,512]{1,0:T(8,128)(2,1)} %wo_ref.1, f32[1,512]{1,0:T(1,128)} %bitcast.15, ...), custom_call_target="tpu_custom_call" | custom-call | tf_op jit(solution)/shard_map/pallas_call | solution.py:275
  117.7 2.2 %reshape.71 = bf16[1,6,12,12,512]{4,3,2,1,0:T(8,128)(2,1)} reshape(bf16[864,512]{1,0:T(8,128)(2,1)} %shard_map.92) | data formatting | bytes 1769472 | tf_op jit(solution)/shard_map/reshape | solution.py:339
  (5 shorter events, 0.1 us)
Async XLA Ops:
  0.0 1.3 %copy-start = (bf16[1,6,12,12,512]{4,3,2,1,0:T(8,128)(2,1)S(1)}, bf16[1,6,12,12,512]{4,3,2,1,0:T(8,128)(2,1)}, u32[]{:S(2)}) copy-start(bf16[1,6,12,12,512]{4,3,2,1,0:T(8,128)(2,1)} %param.9) | copy-start | bytes 2654212
  1.3 2.0 %copy-start.5 = (bf16[512]{0:T(512)(128)(2,1)S(1)}, bf16[512]{0:T(512)(128)(2,1)}, u32[]{:S(2)}) copy-start(bf16[512]{0:T(512)(128)(2,1)} %param.12) | copy-start | bytes 3076
  1.3 2.0 %copy-start.4 = (bf16[27,512]{1,0:T(8,128)(2,1)S(1)}, bf16[27,512]{1,0:T(8,128)(2,1)}, u32[]{:S(2)}) copy-start(bf16[27,512]{1,0:T(8,128)(2,1)} %param.11) | copy-start | bytes 82948
  3.1 1.5 %collective-permute-start = (bf16[1,1,12,12,512]{4,3,2,1,0:T(8,128)(2,1)S(1)}, bf16[1,1,12,12,512]{4,3,2,1,0:T(8,128)(2,1)S(1)}, u32[]{:S(2)}, u32[]{:S(2)}) collective-permute-start(bf16[1,1,12,12,512]{4,3,2,1,0:T(8,128)(2,1)S(1)} %dynamic-slice_bitcast_fusion), channel_id=1, source_target_pairs={{0,1},{1,0},{2,3},{3,2},{4,5},{5,4},{6,7},{7,6},{8,9},{9,8},{10,11... | collective-permute-start | bytes 442376 | tf_op jit(solution)/shard_map/ppermute | solution.py:317
  11.6 3.7 %copy-start.1 = (bf16[864,512]{1,0:T(8,128)(2,1)}, bf16[864,512]{1,0:T(8,128)(2,1)S(1)}, u32[]{:S(2)}) copy-start(bf16[864,512]{1,0:T(8,128)(2,1)S(1)} %reshape.68.stream_ref) | copy-start | bytes 2654212
  11.7 2.8 %copy-start.6 = (bf16[512]{0:T(512)(128)(2,1)S(1)}, bf16[512]{0:T(512)(128)(2,1)}, u32[]{:S(2)}) copy-start(bf16[512]{0:T(512)(128)(2,1)} %param.15) | copy-start | bytes 3076
  14.3 3.7 %copy-start.2 = (bf16[864,1024]{1,0:T(8,128)(2,1)}, bf16[864,1024]{1,0:T(8,128)(2,1)S(1)}, u32[]{:S(2)}) copy-start(bf16[864,1024]{1,0:T(8,128)(2,1)S(1)} %convolution_convert_fusion.kv_ref) | copy-start | bytes 5308420
  14.3 3.8 %collective-permute-start.1 = (bf16[864,1024]{1,0:T(8,128)(2,1)S(1)}, bf16[864,1024]{1,0:T(8,128)(2,1)S(1)}, u32[]{:S(2)}, u32[]{:S(2)}) collective-permute-start(bf16[864,1024]{1,0:T(8,128)(2,1)S(1)} %convolution_convert_fusion.kv_ref), channel_id=1, source_target_pairs={{0,1},{1,0},{2,3},{3,2},{4,5},{5,4},{6,7},{7,6},{8,9},{9,8},{10,11... | collective-permute-start | bytes 5308424 | tf_op jit(solution)/shard_map/ppermute | solution.py:331
  18.1 1.2 %copy-start.3 = (bf16[864,1024]{1,0:T(8,128)(2,1)}, bf16[864,1024]{1,0:T(8,128)(2,1)S(1)}, u32[]{:S(2)}) copy-start(bf16[864,1024]{1,0:T(8,128)(2,1)S(1)} %collective-permute-done.1.other_ref) | copy-start | bytes 5308420

commit v15 on v11

--- a/solution.py
+++ b/solution.py
@@ -320,7 +320,7 @@
         padded = extended(embed, (("tok", 1),), 1)
     stream = depthwise(padded[0], conv_taps).reshape(frames, tokens, width)
     normed = rms_scale(stream.astype(jnp.float32), gain_space).astype(jnp.bfloat16)
-    flat = normed.reshape(-1, width)
+    flat = lax.optimization_barrier(normed.reshape(-1, width))
     own_kv = jnp.dot(flat, qkv_space[:, width:], preferred_element_type=jnp.float32).astype(
         jnp.bfloat16
     )

time: 119 us -> 119 us (level)
  matrix products: 7.05 us -> 4.45 us
  local copies, waits for them, and re-layouts: 5.47 us -> 6.77 us
    dot_general x1, matrix products: 2.57 us -> 1.08 us  [local(): jnp.dot(flat, qkv_space[:, width:], preferred_element_type=jnp.float32)]
    unnamed x14 -> x16, local copies, waits for them, and re-layouts: 2.5 us -> 3.81 us
  transfers between devices with their start and end apart: 2 -> 2, of which waited for: 2 -> 2; matrix products, arithmetic and copies ran while one was open for 3% -> 2% of each run, Pallas kernels for 0% -> 0%
where the time goes in v15:
time: 119 us
  Pallas kernels  103 us (87%)
  local copies, waits for them, and re-layouts  6.77 us (6%)
  matrix products  4.45 us (4%)
  waiting for transfers between devices  2.63 us (2%)
  other arithmetic  2.38 us (2%)
    pallas_call x1, Pallas kernels, block_tail(): pl.pallas_call(functools.partial(block_kernel, chunks), out_shape=plane,...  97.7 us
    pallas_call x1, Pallas kernels, depthwise(): pl.pallas_call(conv_kernel, out_shape=jax.ShapeDtypeStruct((planes, grid,...  4.84 us
    unnamed x16, local copies, waits for them, and re-layouts  3.81 us
  transfers between devices with their start and end apart: 2, of which 2 were waited for; matrix products, arithmetic and copies ran while one was open for 2% of the time, Pallas kernels for 0%

profile of v15, /device:TPU:24, one launch (start us, length us, event | category | flops | bytes accessed | tf_op | source)
XLA Modules:
  0.0 119.2 jit_solution(10965583111820817890)
XLA Ops:
  0.0 0.0 copy-start
  0.0 1.3 %copy-done = bf16[1,6,12,12,512]{4,3,2,1,0:T(8,128)(2,1)S(1)} copy-done((bf16[1,6,12,12,512]{4,3,2,1,0:T(8,128)(2,1)S(1)}, bf16[1,6,12,12,512]{4,3,2,1,0:T(8,128)(2,1)}, u32[]{:S(2)}) %copy-start) | copy-done | bytes 884760
  1.3 0.0 copy-start.5
  1.3 0.0 copy-start.4
  1.3 1.8 %convolution_convert_fusion.1 = bf16[6,12,12,512]{3,2,1,0:T(8,128)(2,1)S(1)} fusion(bf16[1,6,12,12,512]{4,3,2,1,0:T(8,128)(2,1)S(1)} %copy-done, bf16[512,512]{1,0:T(8,128)(2,1)} %param.10), kind=kOutput, calls=%fused_computation.5 | convolution fusion | flops 453427200 | bytes 2293760 | tf_op jit(solution)/shard_map/dot_general | solution.py:308
  3.1 0.1 collective-permute-start
  3.2 0.0 copy-done.5
  3.3 0.0 copy-done.4
  3.3 1.4 %collective-permute-done = bf16[1,1,12,12,512]{4,3,2,1,0:T(8,128)(2,1)S(1)} collective-permute-done((bf16[1,1,12,12,512]{4,3,2,1,0:T(8,128)(2,1)S(1)}, bf16[1,1,12,12,512]{4,3,2,1,0:T(8,128)(2,1)S(1)}, u32[]{:S(2)}, u32[]{:S(2)}) %collective-permute-start) | collective-permute-done | bytes 147488 | tf_op jit(solution)/shard_map/ppermute | solution.py:314
  4.7 0.2 maximum_bitcast_fusion
  4.9 0.6 pad_convert_fusion.e_ref
  5.5 4.8 %shard_map.91 = bf16[6,12,16,512]{3,2,1,0:T(8,128)(2,1)S(1)} custom-call(f32[8,14,16,512]{3,2,1,0:T(8,128)S(1)} %pad_convert_fusion.e_ref, f32[27,512]{1,0:T(8,128)S(1)} %convert_element_type.44.t_ref), custom_call_target="tpu_custom_call" | custom-call | tf_op jit(solution)/shard_map/pallas_call | solution.py:91
  10.4 0.5 multiply_reduce_fusion
  10.9 0.5 slice.12
  11.4 0.2 reshape.68.stream_ref
  11.6 0.0 copy-start.1
  11.6 0.1 rsqrt.12
  11.7 0.0 copy-start.7
  11.7 0.3 multiply_convert_fusion
  12.0 1.3 %copy-done.7 = bf16[512,1536]{1,0:T(8,128)(2,1)S(1)} copy-done((bf16[512,1536]{1,0:T(8,128)(2,1)S(1)}, bf16[512,1536]{1,0:T(8,128)(2,1)}, u32[]{:S(2)}) %copy-start.7) | copy-done | bytes 1572888
  13.3 0.0 copy-start.6
  13.3 1.1 convolution_convert_fusion.kv_ref
  14.4 0.0 copy-done.1
  14.4 0.0 copy-start.2
  14.4 0.2 collective-permute-start.1
  14.6 0.0 copy-done.6
  14.6 0.8 reshape.72
  15.4 1.5 %convolution_convert_fusion.2.q_ref = bf16[864,512]{1,0:T(8,128)(2,1)} fusion(bf16[864,512]{1,0:T(8,128)(2,1)S(1)} %multiply_convert_fusion, bf16[512,1536]{1,0:T(8,128)(2,1)S(1)} %copy-done.7), kind=kOutput, calls=%fused_computation.6 | convolution fusion | flops 453427200 | bytes 2293760 | tf_op jit(solution)/shard_map/dot_general | solution.py:329
  16.9 1.3 %collective-permute-done.1.other_ref = bf16[864,1024]{1,0:T(8,128)(2,1)S(1)} collective-permute-done((bf16[864,1024]{1,0:T(8,128)(2,1)S(1)}, bf16[864,1024]{1,0:T(8,128)(2,1)S(1)}, u32[]{:S(2)}, u32[]{:S(2)}) %collective-permute-start.1) | collective-permute-done | bytes 1769504 | tf_op jit(solution)/shard_map/ppermute | solution.py:328
  18.2 0.0 copy-start.3
  18.2 0.0 copy-done.2
  18.2 1.2 %copy-done.3 = bf16[864,1024]{1,0:T(8,128)(2,1)} copy-done((bf16[864,1024]{1,0:T(8,128)(2,1)}, bf16[864,1024]{1,0:T(8,128)(2,1)S(1)}, u32[]{:S(2)}) %copy-start.3) | copy-done | bytes 1769496
  19.4 97.7 %shard_map.92 = bf16[864,512]{1,0:T(8,128)(2,1)} custom-call(bf16[864,512]{1,0:T(8,128)(2,1)} %convolution_convert_fusion.2.q_ref, bf16[864,1024]{1,0:T(8,128)(2,1)} %copy-done.2, bf16[864,1024]{1,0:T(8,128)(2,1)} %copy-done.3, bf16[864,512]{1,0:T(8,128)(2,1)} %copy-done.1, bf16[512,512]{1,0:T(8,128)(2,1)} %wo_ref.1, f32[1,512]{1,0:T(1,128)} %bitcast.17, ...), custom_call_target="tpu_custom_call" | custom-call | tf_op jit(solution)/shard_map/pallas_call | solution.py:272
  117.1 2.2 %reshape.71 = bf16[1,6,12,12,512]{4,3,2,1,0:T(8,128)(2,1)} reshape(bf16[864,512]{1,0:T(8,128)(2,1)} %shard_map.92) | data formatting | bytes 1769472 | tf_op jit(solution)/shard_map/reshape | solution.py:336
  (5 shorter events, 0.1 us)
Async XLA Ops:
  0.0 1.3 %copy-start = (bf16[1,6,12,12,512]{4,3,2,1,0:T(8,128)(2,1)S(1)}, bf16[1,6,12,12,512]{4,3,2,1,0:T(8,128)(2,1)}, u32[]{:S(2)}) copy-start(bf16[1,6,12,12,512]{4,3,2,1,0:T(8,128)(2,1)} %param.9) | copy-start | bytes 2654212
  1.3 2.0 %copy-start.5 = (bf16[512]{0:T(512)(128)(2,1)S(1)}, bf16[512]{0:T(512)(128)(2,1)}, u32[]{:S(2)}) copy-start(bf16[512]{0:T(512)(128)(2,1)} %param.12) | copy-start | bytes 3076
  1.3 2.0 %copy-start.4 = (bf16[27,512]{1,0:T(8,128)(2,1)S(1)}, bf16[27,512]{1,0:T(8,128)(2,1)}, u32[]{:S(2)}) copy-start(bf16[27,512]{1,0:T(8,128)(2,1)} %param.11) | copy-start | bytes 82948
  3.1 1.5 %collective-permute-start = (bf16[1,1,12,12,512]{4,3,2,1,0:T(8,128)(2,1)S(1)}, bf16[1,1,12,12,512]{4,3,2,1,0:T(8,128)(2,1)S(1)}, u32[]{:S(2)}, u32[]{:S(2)}) collective-permute-start(bf16[1,1,12,12,512]{4,3,2,1,0:T(8,128)(2,1)S(1)} %dynamic-slice_bitcast_fusion), channel_id=1, source_target_pairs={{0,1},{1,0},{2,3},{3,2},{4,5},{5,4},{6,7},{7,6},{8,9},{9,8},{10,11... | collective-permute-start | bytes 442376 | tf_op jit(solution)/shard_map/ppermute | solution.py:314
  11.6 2.8 %copy-start.1 = (bf16[864,512]{1,0:T(8,128)(2,1)}, bf16[864,512]{1,0:T(8,128)(2,1)S(1)}, u32[]{:S(2)}) copy-start(bf16[864,512]{1,0:T(8,128)(2,1)S(1)} %reshape.68.stream_ref) | copy-start | bytes 2654212
  11.7 1.6 %copy-start.7 = (bf16[512,1536]{1,0:T(8,128)(2,1)S(1)}, bf16[512,1536]{1,0:T(8,128)(2,1)}, u32[]{:S(2)}) copy-start(bf16[512,1536]{1,0:T(8,128)(2,1)} %param.13) | copy-start | bytes 4718596
  13.3 1.3 %copy-start.6 = (bf16[512]{0:T(512)(128)(2,1)S(1)}, bf16[512]{0:T(512)(128)(2,1)}, u32[]{:S(2)}) copy-start(bf16[512]{0:T(512)(128)(2,1)} %param.15) | copy-start | bytes 3076
  14.4 3.8 %copy-start.2 = (bf16[864,1024]{1,0:T(8,128)(2,1)}, bf16[864,1024]{1,0:T(8,128)(2,1)S(1)}, u32[]{:S(2)}) copy-start(bf16[864,1024]{1,0:T(8,128)(2,1)S(1)} %convolution_convert_fusion.kv_ref) | copy-start | bytes 5308420
  14.4 3.8 %collective-permute-start.1 = (bf16[864,1024]{1,0:T(8,128)(2,1)S(1)}, bf16[864,1024]{1,0:T(8,128)(2,1)S(1)}, u32[]{:S(2)}, u32[]{:S(2)}) collective-permute-start(bf16[864,1024]{1,0:T(8,128)(2,1)S(1)} %convolution_convert_fusion.kv_ref), channel_id=1, source_target_pairs={{0,1},{1,0},{2,3},{3,2},{4,5},{5,4},{6,7},{7,6},{8,9},{9,8},{10,11... | collective-permute-start | bytes 5308424 | tf_op jit(solution)/shard_map/ppermute | solution.py:328
  18.2 1.2 %copy-start.3 = (bf16[864,1024]{1,0:T(8,128)(2,1)}, bf16[864,1024]{1,0:T(8,128)(2,1)S(1)}, u32[]{:S(2)}) copy-start(bf16[864,1024]{1,0:T(8,128)(2,1)S(1)} %collective-permute-done.1.other_ref) | copy-start | bytes 5308420
